TPU v7x, 32 devices: a whole 2x2x4 slice. The times are simulated.
32 devices in a mesh: ctx: 8 (over z, x), wt: 4 (over y, core).
Axes of the slice: x: 2, y: 2, z: 4, core: 2. Of those that a mesh axis runs over, the one named last changes fastest.
Arguments:
- tokens: bfloat16 [2048, 2048], P('ctx'), may hold values from -6 to 6
- cotangent: bfloat16 [2048, 2048], P('ctx'), may hold values from -6 to 6
- doc_lengths: int32 [8], replicated, may hold values from 1 to 1280, as said below
- owners: int32 [64, 1], replicated, may hold values from 0 to 7; in each aligned block of 64 rows (0 to 63, 64 to 127, ...) at most 12 rows name the same one
- master: float32 [96, 128, 8192], P('ctx', None, 'wt'), may hold values from -0.125 to 0.125
- moment_one: float32 [96, 128, 8192], P('ctx', None, 'wt'), may hold values from -180 to 180
- moment_two: float32 [96, 128, 8192], P('ctx', None, 'wt'), may hold values from 100 to 10000
Outputs:
- output: bfloat16 [2048, 2048], P('ctx')
- input_grad: float32 [2048, 2048], P('ctx')
- new_master: float32 [96, 128, 8192], P('ctx', None, 'wt')
- new_one: float32 [96, 128, 8192], P('ctx', None, 'wt')
- new_two: float32 [96, 128, 8192], P('ctx', None, 'wt')
- new_copy: bfloat16 [96, 128, 8192], P('ctx', None, 'wt')
Inputs may be any that keep to these rules, and one draw needn't show every extreme that they name: `doc_lengths`: the lengths sum to 2048; the first document is the longest, exactly 1280 tokens. `owners`: every ctx index owns 1 to 12 tiles, and one owns exactly 12.
All inputs are finite; a program needn't handle non-finite values.
Results may differ from a plain program's by a relative error of at most 0.014.
Values may be sent and summed in bfloat16 or wider, within the bound.
No kernel may reach another device: no remote copies, remote signals or barrier semaphores. Data moves between devices by JAX's collectives and lax.ppermute only.
A program may use at most 320 MiB of HBM per device.

v0:
```python
from functools import partial
import math

import jax
import jax.numpy as jnp
from jax import lax
from jax.experimental import pallas as pl
from jax.experimental.pallas import tpu as pltpu
from jax.sharding import PartitionSpec as P

HEAD_DIM = 128
STEP = 3


adam_beta = 0.5
learn_rate = 0.01
decay_rate = 0.1
adam_eps = 1e-08
norm_eps = 1e-05
neg_fill = -1e30
rope_base = 10000.0


def from_behind(x, axis, by):
    count = lax.axis_size(axis)
    pairs = [(i, i + by) for i in range(count) if 0 <= i + by < count]
    return lax.ppermute(x, axis, pairs)


def from_behind_2(value, axis, steps):
    count = lax.axis_size(axis)
    pairs = [(source, (source + steps) % count) for source in range(count)]
    return lax.ppermute(value, axis, pairs)


def layer_norm(values):
    center = values - jnp.mean(values, axis=-1, keepdims=True)
    spread = jnp.mean(center * center, axis=-1, keepdims=True)
    return center * lax.rsqrt(spread + norm_eps)


def rotary(values, positions):
    half_dim = values.shape[-1] // 2
    frequencies = rope_base ** (-jnp.arange(half_dim, dtype=jnp.float32) * (2.0 / values.shape[-1]))
    angles = positions.astype(jnp.float32)[:, None] * frequencies[None, :]
    cosine = jnp.cos(angles)[:, None, :]
    sine_vals = jnp.sin(angles)[:, None, :]
    first_half = values[..., :half_dim]
    second_half = values[..., half_dim:]
    return jnp.concatenate(
        [
            first_half * cosine - second_half * sine_vals,
            second_half * cosine + first_half * sine_vals,
        ],
        axis=-1,
    )


def doc_index(positions, doc_starts):
    return jnp.sum((positions[:, None] >= doc_starts[None, :]).astype(jnp.int32), axis=1) - 1


def heads_dot(spec, left, right):
    return jnp.einsum(spec, left, right, preferred_element_type=jnp.float32)


def general_shards(tokens, cotangent, doc_lengths, owners, master, moment_one, moment_two):
    n_ctx = lax.axis_size("ctx")
    n_wt = lax.axis_size("wt")
    ctx_index = lax.axis_index("ctx")
    tok_rows, width = tokens.shape
    cap_slots, tile_rows, tile_width = master.shape
    n_tiles = owners.shape[0]
    head_dim = HEAD_DIM
    owner_col = owners[:, 0]
    tile_ids = jnp.arange(n_tiles, dtype=jnp.int32)
    earlier = (owner_col[None, :] == owner_col[:, None]) & (tile_ids[None, :] < tile_ids[:, None])
    slot_ids = owner_col * cap_slots + jnp.sum(earlier.astype(jnp.int32), axis=1)
    every_slot = lax.all_gather(master.astype(jnp.bfloat16), "ctx", axis=0, tiled=True)
    flat_w = every_slot[slot_ids].reshape(-1)
    local_width = width // n_wt
    heads_local = local_width // head_dim
    part_q = width * local_width
    ff_local = (flat_w.shape[0] - 4 * part_q) // (3 * width)
    part_f = width * ff_local
    w_qkv = flat_w[: 3 * part_q].reshape(3, width, local_width)
    w_out = flat_w[3 * part_q : 4 * part_q].reshape(local_width, width)
    w_gateup = flat_w[4 * part_q : 4 * part_q + 2 * part_f].reshape(2, width, ff_local)
    w_down = flat_w[4 * part_q + 2 * part_f :].reshape(ff_local, width)
    positions = ctx_index * tok_rows + jnp.arange(tok_rows, dtype=jnp.int32)
    doc_starts = jnp.cumsum(doc_lengths) - doc_lengths
    q_docs = doc_index(positions, doc_starts)
    score_scale = 1.0 / math.sqrt(head_dim)
    inputs = tokens.astype(jnp.float32)
    normed, norm_back = jax.vjp(layer_norm, inputs)
    normed_low = normed.astype(jnp.bfloat16)
    qkv_vals = heads_dot("td,jde->jte", normed_low, w_qkv)
    shaped = qkv_vals.reshape(3, tok_rows, heads_local, head_dim)
    rope_here = partial(rotary, positions=positions)
    qk_rot, rope_back = jax.vjp(rope_here, jnp.concatenate([shaped[0], shaped[1]], axis=1))
    q_low = qk_rot[:, :heads_local].astype(jnp.bfloat16)
    k_low = qk_rot[:, heads_local:].astype(jnp.bfloat16)
    v_low = shaped[2].astype(jnp.bfloat16)

    def masked_scores(key_block, key_pos, key_docs):
        raw_scores = heads_dot("qhd,khd->hqk", q_low, key_block)
        visible_mask = (key_pos[None, :] <= positions[:, None]) & (
            key_docs[None, :] == q_docs[:, None]
        )
        return (jnp.where(visible_mask[None], raw_scores * score_scale, neg_fill), visible_mask)

    def over_blocks(kv_piece, first_row, update_fn, running):
        key_count = kv_piece[0].shape[0]
        block_len = math.gcd(key_count, 512)
        n_blocks = key_count // block_len
        split_kv = tuple(
            (member.reshape((n_blocks, block_len) + member.shape[1:]) for member in kv_piece)
        )

        def step_fn(block_state, inputs_here):
            block_idx, block_vals = inputs_here
            block_row = first_row + block_idx * block_len
            key_pos = block_row + jnp.arange(block_len, dtype=jnp.int32)
            key_docs = doc_index(key_pos, doc_starts)
            block_state = update_fn(block_state, block_vals, key_pos, key_docs, block_row)
            return (block_state, None)

        running, _ = lax.scan(step_fn, running, (jnp.arange(n_blocks, dtype=jnp.int32), split_kv))
        return running

    def norm_update(block_state, block_vals, key_pos, key_docs, block_row):
        row_top, row_total = block_state
        scores, visible_mask = masked_scores(block_vals[0], key_pos, key_docs)
        new_top = jnp.maximum(row_top, jnp.max(scores, axis=-1))
        weights_exp = jnp.where(visible_mask[None], jnp.exp(scores - new_top[:, :, None]), 0.0)
        return (new_top, row_total * jnp.exp(row_top - new_top) + jnp.sum(weights_exp, axis=-1))

    start_top = jnp.full((heads_local, tok_rows), neg_fill, jnp.float32)
    start_total = jnp.zeros((heads_local, tok_rows), jnp.float32)
    row_top, row_total = over_blocks(
        (lax.all_gather(k_low, "ctx", axis=0, tiled=True),),
        jnp.int32(0),
        norm_update,
        (start_top, start_total),
    )
    log_sum = row_top + jnp.log(row_total)

    def block_probs(key_block, key_pos, key_docs):
        scores, visible_mask = masked_scores(key_block, key_pos, key_docs)
        return jnp.where(visible_mask[None], jnp.exp(scores - log_sum[:, :, None]), 0.0)

    def value_update(block_state, block_vals, key_pos, key_docs, block_row):
        prob_vals = block_probs(block_vals[0], key_pos, key_docs)
        return block_state + heads_dot(
            "hqk,khd->qhd", prob_vals.astype(jnp.bfloat16), block_vals[1]
        )

    zero_heads = jnp.zeros((tok_rows, heads_local, head_dim), jnp.float32)
    attended = over_blocks(
        (
            lax.all_gather(k_low, "ctx", axis=0, tiled=True),
            lax.all_gather(v_low, "ctx", axis=0, tiled=True),
        ),
        jnp.int32(0),
        value_update,
        zero_heads,
    )
    att_low = attended.reshape(tok_rows, local_width).astype(jnp.bfloat16)
    attn_part = jnp.dot(att_low, w_out, preferred_element_type=jnp.float32)
    residual = inputs + lax.psum(attn_part.astype(jnp.bfloat16), "wt").astype(jnp.float32)
    normed_two, norm_two_back = jax.vjp(layer_norm, residual)
    normed_two_low = normed_two.astype(jnp.bfloat16)
    gateup_vals = heads_dot("td,jde->jte", normed_two_low, w_gateup)
    gate_vals = gateup_vals[0]
    up_vals = gateup_vals[1]
    gate_sig = jax.nn.sigmoid(gate_vals)
    silu_vals = gate_vals * gate_sig
    hidden_low = (silu_vals * up_vals).astype(jnp.bfloat16)
    mlp_part = jnp.dot(hidden_low, w_down, preferred_element_type=jnp.float32)
    output = (residual + lax.psum(mlp_part.astype(jnp.bfloat16), "wt").astype(jnp.float32)).astype(
        jnp.bfloat16
    )
    out_grad = cotangent.astype(jnp.float32)
    grad_down = heads_dot("tf,td->fd", hidden_low, cotangent)
    grad_hidden = heads_dot("td,fd->tf", cotangent, w_down)
    grad_gate = grad_hidden * up_vals * gate_sig * (1.0 + gate_vals * (1.0 - gate_sig))
    grad_up = grad_hidden * silu_vals
    grad_gu_low = jnp.stack([grad_gate, grad_up]).astype(jnp.bfloat16)
    grad_gateup = heads_dot("td,jte->jde", normed_two_low, grad_gu_low)
    norm_two_part = heads_dot("jte,jde->td", grad_gu_low, w_gateup)
    norm_two_grad = lax.psum(norm_two_part.astype(jnp.bfloat16), "wt").astype(jnp.float32)
    resid_grad = out_grad + norm_two_back(norm_two_grad)[0]
    resid_low = resid_grad.astype(jnp.bfloat16)
    grad_out = heads_dot("tc,td->cd", att_low, resid_low)
    att_grad = heads_dot("td,cd->tc", resid_low, w_out)
    att_grad_low = att_grad.astype(jnp.bfloat16).reshape(tok_rows, heads_local, head_dim)
    row_delta = jnp.sum(att_grad_low * attended, axis=-1).T

    def grad_block(block_vals, key_pos, key_docs):
        prob_vals = block_probs(block_vals[0], key_pos, key_docs)
        value_grad = heads_dot("hqk,qhd->khd", prob_vals.astype(jnp.bfloat16), att_grad_low)
        prob_grad = heads_dot("qhd,khd->hqk", att_grad_low, block_vals[1])
        raw_grad = (prob_vals * (prob_grad - row_delta[:, :, None]) * score_scale).astype(
            jnp.bfloat16
        )
        query_grad = heads_dot("hqk,khd->qhd", raw_grad, block_vals[0])
        key_grad = heads_dot("hqk,qhd->khd", raw_grad, q_low)
        return (query_grad, key_grad, value_grad)

    def add_rows(target, addend):
        return target + addend

    def cycle_step(turn_idx, cycle_state):
        query_acc, key_cur, value_cur, key_acc, value_acc = cycle_state
        anchor = (ctx_index - turn_idx) % n_ctx

        def cycle_update(block_state, block_vals, key_pos, key_docs, block_row):
            q_acc, k_acc, v_acc = block_state
            query_grad, key_grad, value_grad = grad_block(block_vals, key_pos, key_docs)
            return (q_acc + query_grad, add_rows(k_acc, key_grad), add_rows(v_acc, value_grad))

        query_acc, key_acc, value_acc = over_blocks(
            (key_cur, value_cur), anchor * tok_rows, cycle_update, (query_acc, key_acc, value_acc)
        )
        key_cur, value_cur = from_behind((key_cur, value_cur), "ctx", 1)
        key_acc, value_acc = (
            from_behind_2(key_acc.astype(jnp.bfloat16), "ctx", 1).astype(key_acc.dtype),
            from_behind_2(value_acc.astype(jnp.bfloat16), "ctx", 1).astype(value_acc.dtype),
        )
        return (query_acc, key_cur, value_cur, key_acc, value_acc)

    cycle_start = (zero_heads, k_low, v_low, zero_heads, zero_heads)
    query_acc, _, _, key_acc, value_acc = lax.fori_loop(0, n_ctx, cycle_step, cycle_start)
    qk_pre_grad = rope_back(jnp.concatenate([query_acc, key_acc], axis=1))[0]
    qkv_grad_low = jnp.stack(
        [
            qk_pre_grad[:, :heads_local].reshape(tok_rows, local_width),
            qk_pre_grad[:, heads_local:].reshape(tok_rows, local_width),
            value_acc.reshape(tok_rows, local_width),
        ]
    ).astype(jnp.bfloat16)
    grad_qkv = heads_dot("td,jte->jde", normed_low, qkv_grad_low)
    norm_one_part = heads_dot("jte,jde->td", qkv_grad_low, w_qkv)
    norm_one_grad = lax.psum(norm_one_part.astype(jnp.bfloat16), "wt").astype(jnp.float32)
    input_grad = resid_grad + norm_back(norm_one_grad)[0]
    grad_tiles = jnp.concatenate(
        [grad_qkv.reshape(-1), grad_out.reshape(-1), grad_gateup.reshape(-1), grad_down.reshape(-1)]
    ).reshape(n_tiles, tile_rows, tile_width)
    slot_range = jnp.arange(n_ctx * cap_slots, dtype=jnp.int32)
    matches = slot_ids[None, :] == slot_range[:, None]
    tile_of_slot = jnp.sum(jnp.where(matches, tile_ids[None, :], 0), axis=1)
    slot_used = jnp.any(matches, axis=1)
    slot_grads = lax.psum_scatter(
        jnp.where(slot_used[:, None, None], grad_tiles[tile_of_slot], 0.0).astype(jnp.bfloat16),
        "ctx",
        scatter_dimension=0,
        tiled=True,
    ).astype(jnp.float32)
    new_one = adam_beta * moment_one + (1.0 - adam_beta) * slot_grads
    new_two = adam_beta * moment_two + (1.0 - adam_beta) * slot_grads * slot_grads
    bias_one = 1.0 - adam_beta**STEP
    bias_two = 1.0 - adam_beta**STEP
    step_ratio = new_one / bias_one / (jnp.sqrt(new_two / bias_two) + adam_eps)
    new_master = master - learn_rate * (step_ratio + decay_rate * master)
    return (output, input_grad, new_master, new_one, new_two, new_master.astype(jnp.bfloat16))


AXES = ("ctx", "wt")
LOW = jnp.bfloat16
F32 = jnp.float32


def swap(value, ctx_bits, wt_bits):
    n_ctx, n_wt = lax.axis_size("ctx"), lax.axis_size("wt")
    pairs = [
        (c * n_wt + w, (c ^ ctx_bits) * n_wt + (w ^ wt_bits))
        for c in range(n_ctx)
        for w in range(n_wt)
    ]
    return lax.ppermute(value, AXES, pairs)


def shift_z(value, step, starts):
    n_wt = lax.axis_size("wt")
    pairs = [
        ((2 * z + x) * n_wt + w, (2 * (z + step) + x) * n_wt + w)
        for z in starts
        for x in range(2)
        for w in range(n_wt)
    ]
    return lax.ppermute(value, AXES, pairs)


def dot(left, right):
    return jnp.dot(left, right, preferred_element_type=F32)


def dot_tn(left, right):
    return lax.dot_general(left, right, (((0,), (0,)), ((), ())), preferred_element_type=F32)


def dot_nt(left, right):
    return lax.dot_general(left, right, (((1,), (1,)), ((), ())), preferred_element_type=F32)


def lane_split(value, lane_starts):
    count, rows, width = value.shape
    homes = lane_starts.shape[0] // 2

    def body(starts, src, *outs):
        for home in range(homes):
            for half in range(2):
                start = pl.multiple_of(starts[2 * home + half], 128)
                outs[home][0, :, half * 128 : half * 128 + 128] = src[
                    0, :, pl.ds(start, 128)
                ].astype(LOW)

    return pl.pallas_call(
        body,
        grid_spec=pltpu.PrefetchScalarGridSpec(
            num_scalar_prefetch=1,
            grid=(count,),
            in_specs=[pl.BlockSpec((1, rows, width), lambda i, s: (i, 0, 0))],
            out_specs=[pl.BlockSpec((1, rows, 256), lambda i, s: (i, 0, 0))] * homes,
        ),
        out_shape=[jax.ShapeDtypeStruct((count, rows, 256), LOW)] * homes,
        name="lane_split",
    )(lane_starts, value)


def lane_join(own, other, lane_starts):
    homes, count, rows, _ = own.shape
    width = homes * 512

    def body(starts, own_ref, other_ref, out):
        for home in range(homes):
            for side, ref in ((0, own_ref), (1, other_ref)):
                for half in range(2):
                    start = pl.multiple_of(starts[4 * home + 2 * side + half], 128)
                    out[0, :, pl.ds(start, 128)] = ref[home, 0, :, half * 128 : half * 128 + 128]

    return pl.pallas_call(
        body,
        grid_spec=pltpu.PrefetchScalarGridSpec(
            num_scalar_prefetch=1,
            grid=(count,),
            in_specs=[
                pl.BlockSpec((homes, 1, rows, 256), lambda i, s: (0, i, 0, 0)),
                pl.BlockSpec(
                    (homes, 1, rows, 256), lambda i, s: (0, (i + count // 2) % count, 0, 0)
                ),
            ],
            out_specs=pl.BlockSpec((1, rows, width), lambda i, s: (i, 0, 0)),
        ),
        out_shape=jax.ShapeDtypeStruct((count, rows, width), LOW),
        name="lane_join",
    )(lane_starts, own, other)


def lane_halves(value, lane_starts):
    count, rows, width = value.shape
    homes = width // 512

    def body(starts, src, own_ref, other_ref):
        for home in range(homes):
            for side, ref in ((0, own_ref), (1, other_ref)):
                for half in range(2):
                    start = pl.multiple_of(starts[4 * home + 2 * side + half], 128)
                    ref[home, 0, :, half * 128 : half * 128 + 128] = src[
                        0, :, pl.ds(start, 128)
                    ].astype(ref.dtype)

    return pl.pallas_call(
        body,
        grid_spec=pltpu.PrefetchScalarGridSpec(
            num_scalar_prefetch=1,
            grid=(count,),
            in_specs=[pl.BlockSpec((1, rows, width), lambda i, s: (i, 0, 0))],
            out_specs=[
                pl.BlockSpec((homes, 1, rows, 256), lambda i, s: (0, i, 0, 0)),
                pl.BlockSpec(
                    (homes, 1, rows, 256), lambda i, s: (0, (i + count // 2) % count, 0, 0)
                ),
            ],
        ),
        out_shape=[
            jax.ShapeDtypeStruct((homes, count, rows, 256), dtype) for dtype in (F32, LOW)
        ],
        name="lane_halves",
    )(lane_starts, value)


def return_halves(grad, lane_starts):
    own, other = lane_halves(grad, lane_starts)
    back = swap(other, 1, 0)
    sums = [(own[m] + back[m].astype(F32)).astype(LOW) for m in range(4)]
    return [sums[0]] + [swap(sums[m], 2 * m, 0) for m in (1, 2, 3)]


VMEM_SPEC = pl.BlockSpec(memory_space=pltpu.VMEM)
SMEM_SPEC = pl.BlockSpec(memory_space=pltpu.SMEM)
ANY_SPEC = pl.BlockSpec(memory_space=pl.ANY)


def pick_qkv(came, picked, rows):
    n_src = len(came)

    def body(which, where, *refs):
        srcs, out = refs[:n_src], refs[n_src]

        def copy(tile, carry):
            for n in range(n_src):

                @pl.when(which[tile] == n)
                def _(n=n):
                    for half in range(2):
                        row = pl.multiple_of(half * 512 + (tile % 4) * 128, 128)
                        lane = pl.multiple_of((tile // 4) * 128, 128)
                        out[pl.ds(row, 128), pl.ds(lane, 128)] = srcs[n][
                            where[tile], :, half * 128 : half * 128 + 128
                        ]

            return carry

        lax.fori_loop(0, 12, copy, 0)

    return pl.pallas_call(
        body,
        in_specs=[SMEM_SPEC, SMEM_SPEC] + [VMEM_SPEC] * n_src,
        out_specs=VMEM_SPEC,
        out_shape=jax.ShapeDtypeStruct((1024, 384), LOW),
        name="pick_qkv",
    )(picked, rows, *came)


def row_gather(sources, picked, rows, sizes):
    total = sum(sizes)
    n_src = len(sources)

    def body(which, where, *refs):
        srcs, outs, sem = refs[:n_src], refs[n_src:-1], refs[-1]
        first = 0
        for out, size in zip(outs, sizes):

            def start(j, carry, out=out, first=first):
                t = first + j
                for n in range(n_src):

                    @pl.when(which[t] == n)
                    def _(n=n):
                        pltpu.make_async_copy(srcs[n].at[where[t]], out.at[j], sem.at[t]).start()

                return carry

            lax.fori_loop(0, size, start, 0)
            first += size
        first = 0
        for out, size in zip(outs, sizes):

            def finish(j, carry, out=out, first=first):
                pltpu.make_async_copy(srcs[0].at[0], out.at[j], sem.at[first + j]).wait()
                return carry

            lax.fori_loop(0, size, finish, 0)
            first += size

    tail = sources[0].shape[1:]
    return pl.pallas_call(
        body,
        in_specs=[SMEM_SPEC, SMEM_SPEC] + [VMEM_SPEC] * n_src,
        out_specs=[ANY_SPEC] * len(sizes),
        out_shape=[jax.ShapeDtypeStruct((size,) + tail, LOW) for size in sizes],
        scratch_shapes=[pltpu.SemaphoreType.DMA((total,))],
        name="row_gather",
    )(picked, rows, *sources)


def send_tile(src, tile, to, row, outs, sem):
    for n, out in enumerate(outs):

        @pl.when(to[tile] == n)
        def _(out=out):
            pltpu.make_async_copy(src, out.at[row[tile]], sem.at[tile]).start()


def place_mlp(gate_up, downs, to, row, place, count, size):
    def body(to_ref, row_ref, z_ref, gu_ref, *refs):
        down_refs, outs, sem = refs[:4], refs[4:-1], refs[-1]
        down_tile = lambda m, k: 48 + 4 * ((k + 2 * z_ref[1]) % 4) + (z_ref[0] ^ m)

        def start(j, carry):
            at = pl.ds(pl.multiple_of(128 * j, 128), 128)
            for half in range(2):
                src = gu_ref.at[at, pl.ds(256 * half, 256)]
                send_tile(src, 16 + 16 * half + j, to_ref, row_ref, outs, sem)
            return carry

        lax.fori_loop(0, 16, start, 0)
        for m in range(4):

            def start_down(k, carry, m=m):
                send_tile(down_refs[m].at[k], down_tile(m, k), to_ref, row_ref, outs, sem)
                return carry

            lax.fori_loop(0, 4, start_down, 0)

        def finish(tile, carry):
            pltpu.make_async_copy(down_refs[0].at[0], outs[0].at[0], sem.at[tile]).wait()
            return carry

        lax.fori_loop(16, 64, finish, 0)

    return pl.pallas_call(
        body,
        in_specs=[SMEM_SPEC] * 3 + [VMEM_SPEC] * 5,
        out_specs=[ANY_SPEC] * count,
        out_shape=[jax.ShapeDtypeStruct((size, 128, 256), LOW)] * count,
        scratch_shapes=[pltpu.SemaphoreType.DMA((64,))],
        name="place_mlp",
    )(to, row, place, gate_up, *downs)


def place_attention(buffers, qkv, outs_from, to, row, place):
    count = len(buffers)

    def body(to_ref, row_ref, z_ref, qkv_ref, *refs):
        out_refs, outs = refs[:4], refs[4 + count : 4 + 2 * count]
        tiles, sem = refs[-2:]

        def start(tile, carry):
            lane = pl.multiple_of((tile // 4) * 128, 128)
            for half in range(2):
                at = pl.ds(pl.multiple_of(half * 512 + (tile % 4) * 128, 128), 128)
                tiles[tile, :, half * 128 : half * 128 + 128] = qkv_ref[at, pl.ds(lane, 128)]
            return carry

        lax.fori_loop(0, 12, start, 0)

        def start_copy(tile, carry):
            send_tile(tiles.at[tile], tile, to_ref, row_ref, outs, sem)
            return carry

        for m in range(4):
            send_tile(out_refs[m].at[0], 12 + (z_ref[0] ^ m), to_ref, row_ref, outs, sem)
        lax.fori_loop(0, 12, start_copy, 0)

        def finish(tile, carry):
            pltpu.make_async_copy(tiles.at[0], outs[0].at[0], sem.at[tile]).wait()
            return carry

        lax.fori_loop(0, 16, finish, 0)

    return pl.pallas_call(
        body,
        in_specs=[SMEM_SPEC] * 3 + [VMEM_SPEC] * 5 + [ANY_SPEC] * count,
        out_specs=[ANY_SPEC] * count,
        out_shape=[jax.ShapeDtypeStruct(buf.shape, buf.dtype) for buf in buffers],
        scratch_shapes=[pltpu.VMEM((12, 128, 256), LOW), pltpu.SemaphoreType.DMA((16,))],
        input_output_aliases={8 + n: n for n in range(count)},
        name="place_attention",
    )(to, row, place, qkv, *outs_from, *buffers)


def after(value, *earlier):
    return lax.optimization_barrier((value,) + earlier)[0]


def key_scores(q, here, there, masks):
    qp, qd, kp, kd = masks
    raw = jnp.concatenate([dot_nt(q, here[:, :128]), dot_nt(q, there[:, :128])], axis=1)
    seen = (kp[...] <= qp[...]) & (kd[...] == qd[...])
    return jnp.where(seen, raw * (1.0 / math.sqrt(HEAD_DIM)), neg_fill)


def attend(query, here, there, masks, n_blocks):
    rows = query.shape[0]
    block = rows // n_blocks

    def body(q, kv, kv_there, qp, qd, kp, kd, out, lse):
        scores = key_scores(q[...], kv[...], kv_there[...], (qp, qd, kp, kd))
        top = jnp.max(scores, axis=1, keepdims=True)
        weights = jnp.exp(scores - top)
        total = jnp.sum(weights, axis=1, keepdims=True)
        probs = (weights * (1.0 / total)).astype(LOW)
        mixed = dot(probs[:, :rows], kv[:, 128:]) + dot(probs[:, rows:], kv_there[:, 128:])
        out[...] = mixed.astype(LOW)
        lse[...] = top + jnp.log(total)

    whole = lambda arr: pl.BlockSpec(arr.shape, lambda i: (0, 0))
    part = lambda arr: pl.BlockSpec((block, arr.shape[1]), lambda i: (i, 0))
    q_pos, q_doc, k_pos, k_doc = masks
    return pl.pallas_call(
        body,
        grid=(n_blocks,),
        in_specs=[
            part(query), whole(here), whole(there), part(q_pos), part(q_doc), whole(k_pos), whole(k_doc),
        ],
        out_specs=[
            pl.BlockSpec((block, HEAD_DIM), lambda i: (i, 0)),
            pl.BlockSpec((block, 1), lambda i: (i, 0)),
        ],
        out_shape=[
            jax.ShapeDtypeStruct((rows, HEAD_DIM), LOW),
            jax.ShapeDtypeStruct((rows, 1), F32),
        ],
        name="attend",
    )(query, here, there, *masks)


def attend_back(query, here, there, out_grad, lse, masks, n_blocks):
    rows = query.shape[0]
    block = rows // n_blocks

    def body(q, kv, kv_there, do, ls, qp, qd, kp, kd, dq, d_here, d_there, acc):
        step = pl.program_id(0)

        @pl.when(step == 0)
        def _():
            d_here[...] = jnp.zeros_like(d_here)
            acc[...] = jnp.zeros_like(acc)

        scores = key_scores(q[...], kv[...], kv_there[...], (qp, qd, kp, kd))
        probs = jnp.exp(scores - ls[...])
        prob_grad = jnp.concatenate(
            [dot_nt(do[...], kv[:, 128:]), dot_nt(do[...], kv_there[:, 128:])], axis=1
        )
        delta = jnp.sum(probs * prob_grad, axis=1, keepdims=True)
        score_grad = (probs * (prob_grad - delta) * (1.0 / math.sqrt(HEAD_DIM))).astype(LOW)
        probs_low = probs.astype(LOW)
        dq[...] = dot(score_grad[:, :rows], kv[:, :128]) + dot(
            score_grad[:, rows:], kv_there[:, :128]
        )
        for first, out in ((0, d_here), (rows, acc)):
            out[:, :128] += dot_tn(score_grad[:, first : first + rows], q[...])
            out[:, 128:] += dot_tn(probs_low[:, first : first + rows], do[...])

        @pl.when(step == n_blocks - 1)
        def _():
            d_there[...] = acc[...].astype(LOW)

    whole = lambda arr: pl.BlockSpec(arr.shape, lambda i: (0, 0))
    part = lambda arr: pl.BlockSpec((block, arr.shape[1]), lambda i: (i, 0))
    kept = pl.BlockSpec((rows, 2 * HEAD_DIM), lambda i: (0, 0))
    q_pos, q_doc, k_pos, k_doc = masks
    return pl.pallas_call(
        body,
        grid=(n_blocks,),
        in_specs=[
            part(query), whole(here), whole(there), part(out_grad), part(lse),
            part(q_pos), part(q_doc), whole(k_pos), whole(k_doc),
        ],
        out_specs=[pl.BlockSpec((block, HEAD_DIM), lambda i: (i, 0)), kept, kept],
        out_shape=[
            jax.ShapeDtypeStruct((rows, HEAD_DIM), F32),
            jax.ShapeDtypeStruct((rows, 2 * HEAD_DIM), F32),
            jax.ShapeDtypeStruct((rows, 2 * HEAD_DIM), LOW),
        ],
        scratch_shapes=[pltpu.VMEM((rows, 2 * HEAD_DIM), F32)],
        name="attend_back",
    )(query, here, there, out_grad, lse, *masks)


def update(state, pieces, lane_starts, used, first, done):
    rows, width = state[0].shape[1:]
    count, homes = pieces[0].shape[0], len(pieces)
    bias = 1.0 - adam_beta**STEP

    def body(starts, live, mas, one, two, *refs):
        grads, (new_mas, new_one, new_two, copy) = refs[:homes], refs[-4:]
        alive = live[pl.program_id(0) + first] > 0
        for home in range(homes):
            for half in range(2):
                at = (0, slice(None), pl.ds(pl.multiple_of(starts[2 * home + half], 128), 128))
                grad = grads[home][0, :, half * 128 : half * 128 + 128].astype(F32)
                grad = jnp.where(alive, grad, 0.0)
                mean = adam_beta * one[at] + (1.0 - adam_beta) * grad
                square = adam_beta * two[at] + (1.0 - adam_beta) * grad * grad
                ratio = (mean * (1.0 / bias)) / (jnp.sqrt(square * (1.0 / bias)) + adam_eps)
                old = mas[at]
                new = old - learn_rate * (ratio + decay_rate * old)
                new_mas[at] = new
                new_one[at] = mean
                new_two[at] = square
                copy[at] = new.astype(LOW)

    slot = pl.BlockSpec((1, rows, width), lambda i, s, u: (i + first, 0, 0))
    piece = pl.BlockSpec((1, rows, 256), lambda i, s, u: (i, 0, 0))
    shape = state[0].shape
    return pl.pallas_call(
        body,
        grid_spec=pltpu.PrefetchScalarGridSpec(
            num_scalar_prefetch=2,
            grid=(count,),
            in_specs=[slot] * 3 + [piece] * homes + [ANY_SPEC] * len(done),
            out_specs=[slot] * 4,
        ),
        out_shape=[jax.ShapeDtypeStruct(shape, F32)] * 3 + [jax.ShapeDtypeStruct(shape, LOW)],
        input_output_aliases={5 + homes + n: n for n in range(len(done))},
        name="update",
    )(lane_starts, used, *state, *pieces, *done)


def z_hops(piece, z_at):
    ups, downs = [piece], [piece]
    for step in (1, 2, 3):
        ups.append(shift_z(ups[-1], 1, range(step - 1, 3)))
        downs.append(shift_z(downs[-1], -1, range(1, 5 - step)))
    return [
        piece,
        jnp.where(z_at % 2 == 0, downs[1], ups[1]),
        jnp.where(z_at < 2, downs[2], ups[2]),
        jnp.where(
            z_at < 2,
            jnp.where(z_at == 0, downs[3], downs[1]),
            jnp.where(z_at == 2, ups[1], ups[3]),
        ),
    ]


def z_sums(kept, z_at):
    def own(target):
        bits = z_at ^ target
        return jnp.where(bits == 1, kept[1], jnp.where(bits == 2, kept[2], kept[3]))

    up = down = 0.0
    for far in (3, 2, 1):
        up = shift_z((own(z_at + far) + up).astype(LOW), 1, range(0, 4 - far)).astype(F32)
        down = shift_z((own(z_at - far) + down).astype(LOW), -1, range(far, 4)).astype(F32)
    return kept[0] + up + down


def gather_rows(piece, z_at=None):
    if z_at is None:
        near = [piece] + [swap(piece, 2 * k, 0) for k in (1, 2, 3)]
    else:
        near = z_hops(piece, z_at)
    blocks = []
    for part in near:
        pair = jnp.concatenate([part, swap(part, 0, 2)])
        blocks += [pair, swap(pair, 0, 1)]
    return jnp.concatenate(blocks)


def scatter_sum(partial_sum, z_at=None):
    quarter = partial_sum.shape[0] // 4
    half, rows = quarter // 2, quarter // 4
    kept = [None] * 4
    for k in (3, 2, 1, 0):
        chunk = partial_sum[quarter * k : quarter * (k + 1)]
        other = swap(chunk[half:].astype(LOW), 0, 1)
        pair = chunk[:half].astype(F32) + other.astype(F32)
        other = swap(pair[rows:].astype(LOW), 0, 2)
        kept[k] = pair[:rows] + other.astype(F32)
    if z_at is not None:
        return z_sums(kept, z_at), kept[0]
    total = kept[0]
    for k in (1, 2, 3):
        total = total + swap(kept[k].astype(LOW), 2 * k, 0).astype(F32)
    return total, kept[0]


def share_rows(piece, wt_index):
    rows = piece.shape[0]
    out = jnp.zeros((4 * rows,) + piece.shape[1:], piece.dtype)
    over_y = swap(piece, 0, 2)
    for bits, part in ((0, piece), (2, over_y), (1, swap(piece, 0, 1)), (3, swap(over_y, 0, 1))):
        out = lax.dynamic_update_slice(out, part, ((wt_index ^ bits) * rows, 0))
    return out


def rotate(values, cosine, sine):
    half = values.shape[-1] // 2
    first, second = values[:, :half], values[:, half:]
    return jnp.concatenate([first * cosine - second * sine, second * cosine + first * sine], axis=1)


def fast_shards(tokens, cotangent, doc_lengths, owners, master, moment_one, moment_two):
    ctx, wt = lax.axis_index("ctx"), lax.axis_index("wt")
    z_at, x_at = ctx // 2, ctx % 2
    tok_rows, width = tokens.shape
    cap, tile_rows, _ = master.shape
    n_tiles = owners.shape[0]
    rows = tok_rows // 4
    bits = jnp.arange(4, dtype=jnp.int32)
    homes = jnp.arange(8, dtype=jnp.int32) ^ ctx
    lane_starts = (
        ((2 * (homes % 2))[:, None] + jnp.arange(2, dtype=jnp.int32)) * 4 + (homes // 2)[:, None]
    ).reshape(-1) * 128

    owner_col = owners[:, 0]
    tile_ids = jnp.arange(n_tiles, dtype=jnp.int32)
    earlier = (owner_col[None, :] == owner_col[:, None]) & (tile_ids[None, :] < tile_ids[:, None])
    slot_in_owner = jnp.sum(earlier.astype(jnp.int32), axis=1)
    owner_bits = owner_col ^ ctx

    def to_cut_order(values):
        cut_vals = values.reshape(-1, width // 4, 4).transpose(0, 2, 1).reshape(-1, width)
        flipped = jnp.concatenate([cut_vals[:, width // 2 :], cut_vals[:, : width // 2]], axis=1)
        return jnp.where(x_at == 0, cut_vals, flipped)

    def from_cut_order(values):
        flipped = jnp.concatenate([values[:, width // 2 :], values[:, : width // 2]], axis=1)
        cut_vals = jnp.where(x_at == 0, values, flipped)
        return cut_vals.reshape(-1, 4, width // 4).transpose(0, 2, 1).reshape(-1, width)

    cut = lane_split(master, lane_starts)
    came = [cut[0]] + [swap(cut[k], k, 0) for k in range(1, 8)]
    tokens_later, grads_later = after(tokens, cut[0]), after(cotangent, cut[0])
    inputs = lax.dynamic_slice(tokens_later, (wt * rows, 0), (rows, width)).astype(F32)
    out_grad_low = lax.dynamic_slice(grads_later, (wt * rows, 0), (rows, width))
    normed, norm_back = jax.vjp(layer_norm, inputs)
    normed_cut = to_cut_order(normed.astype(LOW))
    normed_all = gather_rows(normed_cut, z_at)
    grad_all = gather_rows(out_grad_low, z_at)
    came[7], normed_all, grad_all = lax.optimization_barrier((came[7], normed_all, grad_all))
    w_qkv = pick_qkv(came, owner_bits[:12], slot_in_owner[:12])
    w_qkv_pair = swap(w_qkv, 1, 0)
    wanted = jnp.concatenate(
        [
            jnp.arange(16, 48, dtype=jnp.int32),
            12 + (z_at ^ bits),
            (48 + 4 * ((bits + 2 * x_at) % 4)[None, :] + (z_at ^ bits)[:, None]).reshape(-1),
        ]
    )
    wanted = after(wanted, w_qkv)
    home_gu, *sends = row_gather(
        came, owner_bits[wanted], slot_in_owner[wanted], [32] + [1] * 4 + [4] * 4
    )
    out_came = [sends[0]] + [swap(sends[m], 2 * m, 0) for m in (1, 2, 3)]
    down_here = [sends[4]] + [swap(sends[4 + m], 2 * m, 0) for m in (1, 2, 3)]
    down_here = jnp.stack(down_here)

    block_z = z_at ^ bits
    block_w = wt ^ jnp.array([0, 2, 1, 3], jnp.int32)

    def group_positions(x_index):
        starts = (2 * block_z + x_index)[:, None] * tok_rows + block_w[None, :] * rows
        return (starts.reshape(-1)[:, None] + jnp.arange(rows, dtype=jnp.int32)).reshape(-1)

    q_pos = group_positions(x_at)
    k_pos = jnp.concatenate([q_pos, group_positions(1 - x_at)])
    doc_starts = jnp.cumsum(doc_lengths) - doc_lengths
    q_doc, k_doc = doc_index(q_pos, doc_starts), doc_index(k_pos, doc_starts)
    masks = (q_pos[:, None], q_doc[:, None], k_pos[None, :], k_doc[None, :])
    freqs = rope_base ** (-jnp.arange(HEAD_DIM // 2, dtype=F32) * (2.0 / HEAD_DIM))
    angles = q_pos.astype(F32)[:, None] * freqs[None, :]
    cosine, sine = jnp.cos(angles), jnp.sin(angles)

    half = width // 2
    qkv = dot(normed_all[:, :half], w_qkv) + dot(normed_all[:, half:], w_qkv_pair)
    query = rotate(qkv[:, :128], cosine, sine).astype(LOW)
    kv_here = jnp.concatenate(
        [rotate(qkv[:, 128:256], cosine, sine).astype(LOW), qkv[:, 256:].astype(LOW)], axis=1
    )
    kv_there = swap(kv_here, 1, 0)
    out_here = after(jnp.stack(out_came), kv_here)
    out_there = swap(out_here, 1, 0)
    att_low, lse = attend(query, kv_here, kv_there, masks, 4)
    w_out = lane_join(out_here, out_there, lane_starts).reshape(tile_rows, width)

    pair_gu = swap(after(home_gu, kv_there), 1, 0)
    w_down = lane_join(down_here, swap(after(down_here, kv_there), 1, 0), lane_starts)
    w_down = w_down.reshape(512, width)
    w_gu = jnp.concatenate(
        [part.reshape(width, 256) for half_gu in (home_gu, pair_gu) for part in (half_gu[:16], half_gu[16:])],
        axis=1,
    )
    att_out, _ = scatter_sum(dot(att_low, w_out).astype(LOW))
    residual = inputs + att_out

    normed_two, norm_two_back = jax.vjp(layer_norm, residual)
    two_all = gather_rows(normed_two.astype(LOW))
    gu = dot(two_all, w_gu)
    gate = jnp.concatenate([gu[:, :256], gu[:, 512:768]], axis=1)
    up = jnp.concatenate([gu[:, 256:512], gu[:, 768:]], axis=1)
    gate_sig = jax.nn.sigmoid(gate)
    silu = gate * gate_sig
    hidden = (silu * up).astype(LOW)

    hidden_grad = dot_nt(grad_all, w_down)
    grad_gate = (hidden_grad * up * gate_sig * (1.0 + gate * (1.0 - gate_sig))).astype(LOW)
    grad_up = (hidden_grad * silu).astype(LOW)
    grad_gu = jnp.concatenate(
        [grad_gate[:, :256], grad_up[:, :256], grad_gate[:, 256:], grad_up[:, 256:]], axis=1
    )
    two_grad, begun = scatter_sum(dot_nt(grad_gu, w_gu).astype(LOW))
    hidden_later, grad_gu_later = lax.optimization_barrier((hidden, grad_gu, begun))[:2]
    grad_w_gu = dot_tn(two_all, grad_gu_later)
    gu_back = swap(grad_w_gu[:, 512:].astype(LOW), 1, 0)
    grad_w_down = dot_tn(hidden_later, grad_all)

    resid_grad = out_grad_low.astype(F32) + norm_two_back(two_grad)[0]
    resid_all = gather_rows(resid_grad.astype(LOW))
    gu_sum = (grad_w_gu[:, :512] + gu_back.astype(F32)).astype(LOW)
    down_came = return_halves(grad_w_down.reshape(4, tile_rows, width), lane_starts)

    part_slots = cap // 2
    send_to = owner_bits + 8 * (slot_in_owner // part_slots)
    send_row = slot_in_owner % part_slots
    place = jnp.stack([z_at, x_at])
    sends = place_mlp(gu_sum, down_came, send_to, send_row, place, 16, part_slots)

    att_grad = dot_nt(resid_all, w_out).astype(LOW)
    out_grad_came = return_halves(
        dot_tn(att_low, resid_all).reshape(1, tile_rows, width), lane_starts
    )
    query_grad, kv_grad, kv_grad_there = attend_back(
        query, kv_here, kv_there, att_grad, lse, masks, 4
    )
    kv_grad_back = swap(kv_grad_there, 1, 0)
    kv_grad = kv_grad + kv_grad_back.astype(F32)
    qkv_grad = jnp.concatenate(
        [
            rotate(query_grad, cosine, -sine),
            rotate(kv_grad[:, :128], cosine, -sine),
            kv_grad[:, 128:],
        ],
        axis=1,
    ).astype(LOW)
    qkv_back = swap(dot_tn(normed_all[:, half:], qkv_grad).astype(LOW), 1, 0)
    qkv_sum = (dot_tn(normed_all[:, :half], qkv_grad) + qkv_back.astype(F32)).astype(LOW)
    sends = place_attention(sends, qkv_sum, out_grad_came, send_to, send_row, place)

    qkv_grad_later, hidden_last = lax.optimization_barrier((qkv_grad, hidden, sends[0]))[:2]
    one_part = jnp.concatenate(
        [dot_nt(qkv_grad_later, w_qkv), dot_nt(qkv_grad_later, w_qkv_pair)], axis=1
    )
    down_part = dot(hidden_last, w_down)
    one_grad = from_cut_order(scatter_sum(one_part.astype(LOW), z_at)[0])
    input_grad = resid_grad + norm_back(one_grad)[0]
    input_grad = share_rows(input_grad.astype(LOW), wt).astype(F32)
    down, _ = scatter_sum(down_part.astype(LOW), z_at)
    output = share_rows((residual + down).astype(LOW), wt)

    slot_range = jnp.arange(cap, dtype=jnp.int32) + ctx * cap
    used = jnp.any(
        (owner_col * cap + slot_in_owner)[None, :] == slot_range[:, None], axis=1
    ).astype(jnp.int32)
    state, done = (master, moment_one, moment_two), ()
    for part in range(2):
        mine = sends[8 * part : 8 * part + 8]
        pieces = [mine[0]] + [swap(mine[k], k, 0) for k in range(1, 8)]
        done = tuple(update(state, pieces, lane_starts, used, part * part_slots, done))
    return (output, input_grad) + done


def choose_shards(*args):
    sizes = (lax.axis_size("ctx"), lax.axis_size("wt"), args[0].shape, args[4].shape[1:])
    if sizes == (8, 4, (256, 2048), (128, 2048)) and args[3].shape[0] == 64:
        return fast_shards(*args)
    return general_shards(*args)


def solution(mesh):
    placed = (
        P("ctx", None),
        P("ctx", None),
        P(),
        P(),
        P("ctx", None, "wt"),
        P("ctx", None, "wt"),
        P("ctx", None, "wt"),
    )
    return jax.shard_map(
        choose_shards,
        mesh=mesh,
        in_specs=placed,
        out_specs=(
            P("ctx", None),
            P("ctx", None),
            P("ctx", None, "wt"),
            P("ctx", None, "wt"),
            P("ctx", None, "wt"),
            P("ctx", None, "wt"),
        ),
        check_vma=False,
    )
```

profile of v0, /device:TPU:9, one launch (start us, length us, event | category | flops | bytes accessed | tf_op | source)
XLA Modules:
  0.0 914.9 jit_solution(9759945498424224818)
XLA Ops:
  1.4 12.4 %lane_split.1 = (bf16[12,128,256]{2,1,0:T(8,128)(2,1)}, bf16[12,128,256]{2,1,0:T(8,128)(2,1)}, bf16[12,128,256]{2,1,0:T(8,128)(2,1)}, bf16[12,128,256]{2,1,0:T(8...) custom-call(s32[16]{0:T(128)} %mul.264.starts, ...), custom_call_target="tpu_custom_call" | custom-call | tf_op jit(solution)/shard_map/lane_split/pallas_call | solution.py:318
  67.6 15.2 %collective-permute-done.8 = bf16[64,2048]{1,0:T(8,128)(2,1)S(1)} collective-permute-done((bf16[64,2048]{1,0:T(8,128)(2,1)}, bf16[64,2048]{1,0:T(8,128)(2,1)S(1)}, u32[]{:S(2)}, u32[]{:S(2)}) %collective-permute-start.8) | collective-permute-done | bytes 262176 | tf_op jit(solution)/shard_map/ppermute | solution.py:291
  122.0 6.1 collective-permute-start.14
  143.5 24.6 %collective-permute-done.31.refs_3_ = bf16[12,128,256]{2,1,0:T(8,128)(2,1)S(1)} collective-permute-done((bf16[12,128,256]{2,1,0:T(8,128)(2,1)}, bf16[12,128,256]{2,1,0:T(8,128)(2,1)S(1)}, u32[]{:S(2)}, u32[]{:S(2)}) %collective-permute-start.31) | collective-permute-done | bytes 786464 | tf_op jit(solution)/shard_map/ppermute | solution.py:280
  168.1 35.7 %collective-permute-done.32.refs_4_ = bf16[12,128,256]{2,1,0:T(8,128)(2,1)S(1)} collective-permute-done((bf16[12,128,256]{2,1,0:T(8,128)(2,1)}, bf16[12,128,256]{2,1,0:T(8,128)(2,1)S(1)}, u32[]{:S(2)}, u32[]{:S(2)}) %collective-permute-start.32) | collective-permute-done | bytes 786464 | tf_op jit(solution)/shard_map/ppermute | solution.py:280
  203.8 16.9 %collective-permute-done.33.refs_5_ = bf16[12,128,256]{2,1,0:T(8,128)(2,1)S(1)} collective-permute-done((bf16[12,128,256]{2,1,0:T(8,128)(2,1)}, bf16[12,128,256]{2,1,0:T(8,128)(2,1)S(1)}, u32[]{:S(2)}, u32[]{:S(2)}) %collective-permute-start.33) | collective-permute-done | bytes 786464 | tf_op jit(solution)/shard_map/ppermute | solution.py:280
  220.6 17.6 %collective-permute-done.34.refs_6_ = bf16[12,128,256]{2,1,0:T(8,128)(2,1)S(1)} collective-permute-done((bf16[12,128,256]{2,1,0:T(8,128)(2,1)}, bf16[12,128,256]{2,1,0:T(8,128)(2,1)S(1)}, u32[]{:S(2)}, u32[]{:S(2)}) %collective-permute-start.34) | collective-permute-done | bytes 786464 | tf_op jit(solution)/shard_map/ppermute | solution.py:280
  250.6 5.5 row_gather.1
  273.1 14.2 %collective-permute-done.40.other_ref = bf16[4,1,128,256]{3,2,1,0:T(8,128)(2,1)S(1)} collective-permute-done((bf16[4,1,128,256]{3,2,1,0:T(8,128)(2,1)S(1)}, bf16[4,1,128,256]{3,2,1,0:T(8,128)(2,1)S(1)}, u32[]{:S(2)}, u32[]{:S(2)}) %collective-permute-start.40) | collective-permute-done | bytes 262176 | tf_op jit(solution)/shard_map/ppermute | solution.py:280
  291.5 7.9 attend.1
  338.0 13.2 %collective-permute-done.48 = bf16[64,2048]{1,0:T(8,128)(2,1)S(1)} collective-permute-done((bf16[64,2048]{1,0:T(8,128)(2,1)S(1)}, bf16[64,2048]{1,0:T(8,128)(2,1)S(1)}, u32[]{:S(2)}, u32[]{:S(2)}) %collective-permute-start.48) | collective-permute-done | bytes 262176 | tf_op jit(solution)/shard_map/ppermute | solution.py:280
  351.1 6.5 collective-permute-done.51
  373.7 12.1 %collective-permute-start.57 = (bf16[128,2048]{1,0:T(8,128)(2,1)S(1)}, bf16[128,2048]{1,0:T(8,128)(2,1)S(1)}, u32[]{:S(2)}, u32[]{:S(2)}) collective-permute-start(bf16[128,2048]{1,0:T(8,128)(2,1)S(1)} %pad_maximum_fusion.17), channel_id=1, source_target_pairs={{0,1},{1,0},{2,3},{3,2},{4,5},{5,4},{6,7},{7,6},{8,9},{9,8},{10,11... | collective-permute-start | bytes 1572872 | tf_op jit(solution)/shard_map/ppermute | solution.py:280
  467.5 7.1 collective-permute-done.75
  474.6 6.5 collective-permute-done.78
  496.9 6.4 fusion.116
  509.7 6.0 collective-permute-start.80
  534.5 11.9 %attend_back.1 = (f32[1024,128]{1,0:T(8,128)}, f32[1024,256]{1,0:T(8,128)}, bf16[1024,256]{1,0:T(8,128)(2,1)}) custom-call(bf16[1024,128]{1,0:T(8,128)(2,1)} %pad_maximum_fusion.25.q, bf16[1024,256]{1,0:T(8,128)(2,1)} %copy-done.7, bf16[1024,256]{1,0:T(8,128)(2,1)} %copy-done.24, bf16[1024,128]{1,0:T(8,128)(2,1)} %convolution_convert_fusion.5.do, ...), custom_call_target="tpu_custom_call" | custom-call | tf_op jit(solution)/shard_map/attend_back/pallas_call | solution.py:645
  559.4 11.8 %collective-permute-done.90 = bf16[1024,256]{1,0:T(8,128)(2,1)} collective-permute-done((bf16[1024,256]{1,0:T(8,128)(2,1)}, bf16[1024,256]{1,0:T(8,128)(2,1)}, u32[]{:S(2)}, u32[]{:S(2)}) %collective-permute-start.90) | collective-permute-done | bytes 524320 | tf_op jit(solution)/shard_map/ppermute | solution.py:280
  595.1 5.9 place_mlp.1
  614.7 11.0 %collective-permute-start.120 = (bf16[128,2048]{1,0:T(8,128)(2,1)S(1)}, bf16[128,2048]{1,0:T(8,128)(2,1)S(1)}, u32[]{:S(2)}, u32[]{:S(2)}) collective-permute-start(bf16[128,2048]{1,0:T(8,128)(2,1)S(1)} %get-tuple-element.208), channel_id=1, source_target_pairs={{0,1},{1,0},{2,3},{3,2},{4,5},{5,4},{6,7},{7,6},{8,9},{9,8},{10,11... | collective-permute-start | bytes 1572872 | tf_op jit(solution)/shard_map/ppermute | solution.py:280
  675.7 5.7 collective-permute-done.109
  698.3 5.9 collective-permute-done.130
  705.6 8.4 collective-permute-done.113
  736.0 8.4 collective-permute-done.114
  749.2 9.0 collective-permute-done.143.refs_2_
  758.2 16.7 %collective-permute-done.144.refs_3_ = bf16[6,128,256]{2,1,0:T(8,128)(2,1)S(1)} collective-permute-done((bf16[6,128,256]{2,1,0:T(8,128)(2,1)}, bf16[6,128,256]{2,1,0:T(8,128)(2,1)S(1)}, u32[]{:S(2)}, u32[]{:S(2)}) %collective-permute-start.144) | collective-permute-done | bytes 393248 | tf_op jit(solution)/shard_map/ppermute | solution.py:280
  779.6 71.3 %collective-permute-done.147.refs_6_ = bf16[6,128,256]{2,1,0:T(8,128)(2,1)S(1)} collective-permute-done((bf16[6,128,256]{2,1,0:T(8,128)(2,1)S(1)}, bf16[6,128,256]{2,1,0:T(8,128)(2,1)S(1)}, u32[]{:S(2)}, u32[]{:S(2)}) %collective-permute-start.147) | collective-permute-done | bytes 393248 | tf_op jit(solution)/shard_map/ppermute | solution.py:280
  851.8 7.4 collective-permute-done.148.refs_7_
  862.2 18.8 %update.2 = (f32[12,128,2048]{2,1,0:T(8,128)}, f32[12,128,2048]{2,1,0:T(8,128)}, f32[12,128,2048]{2,1,0:T(8,128)}, bf16[12,128,2048]{2,1,0:T(8,128)(2,1)}) custom-call(s32[16]{0:T(128)} %mul.264.starts, s32[12]{0:T(128)} %convert_element_type.623.live, f32[12,128,2048]{2,1,0:T(8,128)} %mas.3, f32[12,128,2048]{2,1,0:T(8,128)} %one.3, f32[12,128,2048]{2,1,0:T(8,128)} %two.3, ...), custom_call_target="tpu_custom_call" | custom-call | tf_op jit(solution)/shard_map/update/pallas_call | solution.py:689
  881.8 19.0 %update.3 = (f32[12,128,2048]{2,1,0:T(8,128)}, f32[12,128,2048]{2,1,0:T(8,128)}, f32[12,128,2048]{2,1,0:T(8,128)}, bf16[12,128,2048]{2,1,0:T(8,128)(2,1)}) custom-call(s32[16]{0:T(128)} %mul.264.starts, s32[12]{0:T(128)} %convert_element_type.623.live, ...), custom_call_target="tpu_custom_call", output_to_operand_aliasing={{0}: (13, {}), {1}: (14, {}), {2}: (15, {}), {3}: (16, {})} | custom-call | tf_op jit(solution)/shard_map/update/pallas_call | solution.py:689
  900.8 9.1 collective-permute-start.133
  (648 shorter events, 478.1 us)
Async XLA Ops:
  40.8 90.7 %collective-permute-start = (bf16[12,128,256]{2,1,0:T(8,128)(2,1)}, bf16[12,128,256]{2,1,0:T(8,128)(2,1)S(1)}, u32[]{:S(2)}, u32[]{:S(2)}) collective-permute-start(bf16[12,128,256]{2,1,0:T(8,128)(2,1)} %get-tuple-element.87), channel_id=1, source_target_pairs={{0,28},{1,29},{2,30},{3,31},{4,24},{5,25},{6,26},{7,27},{8,20},{9,... | collective-permute-start | bytes 2359304 | tf_op jit(solution)/shard_map/ppermute | solution.py:280
  43.7 90.0 %collective-permute-start.29 = (bf16[12,128,256]{2,1,0:T(8,128)(2,1)}, bf16[12,128,256]{2,1,0:T(8,128)(2,1)S(1)}, u32[]{:S(2)}, u32[]{:S(2)}) collective-permute-start(bf16[12,128,256]{2,1,0:T(8,128)(2,1)} %get-tuple-element.90), channel_id=1, source_target_pairs={{0,4},{1,5},{2,6},{3,7},{4,0},{5,1},{6,2},{7,3},{8,12},{9,13},{10,... | collective-permute-start | bytes 2359304 | tf_op jit(solution)/shard_map/ppermute | solution.py:280
  45.7 37.0 %collective-permute-start.8 = (bf16[64,2048]{1,0:T(8,128)(2,1)}, bf16[64,2048]{1,0:T(8,128)(2,1)S(1)}, u32[]{:S(2)}, u32[]{:S(2)}) collective-permute-start(bf16[64,2048]{1,0:T(8,128)(2,1)} %copy-done.36), channel_id=1, source_target_pairs={{8,16},{9,17},{10,18},{11,19},{12,20},{13,21},{14,22},{15,23},{16,... | collective-permute-start | bytes 786440 | tf_op jit(solution)/shard_map/ppermute | solution.py:291
  114.2 29.3 %collective-permute-start.30 = (bf16[12,128,256]{2,1,0:T(8,128)(2,1)}, bf16[12,128,256]{2,1,0:T(8,128)(2,1)}, u32[]{:S(2)}, u32[]{:S(2)}) collective-permute-start(bf16[12,128,256]{2,1,0:T(8,128)(2,1)} %get-tuple-element.91), channel_id=1, source_target_pairs={{0,8},{1,9},{2,10},{3,11},{4,12},{5,13},{6,14},{7,15},{8,0},{9,1},... | collective-permute-start | bytes 2359304 | tf_op jit(solution)/shard_map/ppermute | solution.py:280
  131.5 36.5 %collective-permute-start.31 = (bf16[12,128,256]{2,1,0:T(8,128)(2,1)}, bf16[12,128,256]{2,1,0:T(8,128)(2,1)S(1)}, u32[]{:S(2)}, u32[]{:S(2)}) collective-permute-start(bf16[12,128,256]{2,1,0:T(8,128)(2,1)} %get-tuple-element.92), channel_id=1, source_target_pairs={{0,12},{1,13},{2,14},{3,15},{4,8},{5,9},{6,10},{7,11},{8,4},{9,5},... | collective-permute-start | bytes 2359304 | tf_op jit(solution)/shard_map/ppermute | solution.py:280
  133.7 70.1 %collective-permute-start.32 = (bf16[12,128,256]{2,1,0:T(8,128)(2,1)}, bf16[12,128,256]{2,1,0:T(8,128)(2,1)S(1)}, u32[]{:S(2)}, u32[]{:S(2)}) collective-permute-start(bf16[12,128,256]{2,1,0:T(8,128)(2,1)} %get-tuple-element.93), channel_id=1, source_target_pairs={{0,16},{1,17},{2,18},{3,19},{4,20},{5,21},{6,22},{7,23},{8,24},{9,... | collective-permute-start | bytes 2359304 | tf_op jit(solution)/shard_map/ppermute | solution.py:280
  136.0 84.6 %collective-permute-start.33 = (bf16[12,128,256]{2,1,0:T(8,128)(2,1)}, bf16[12,128,256]{2,1,0:T(8,128)(2,1)S(1)}, u32[]{:S(2)}, u32[]{:S(2)}) collective-permute-start(bf16[12,128,256]{2,1,0:T(8,128)(2,1)} %get-tuple-element.94), channel_id=1, source_target_pairs={{0,20},{1,21},{2,22},{3,23},{4,16},{5,17},{6,18},{7,19},{8,28},{9,... | collective-permute-start | bytes 2359304 | tf_op jit(solution)/shard_map/ppermute | solution.py:280
  137.0 101.2 %collective-permute-start.34 = (bf16[12,128,256]{2,1,0:T(8,128)(2,1)}, bf16[12,128,256]{2,1,0:T(8,128)(2,1)S(1)}, u32[]{:S(2)}, u32[]{:S(2)}) collective-permute-start(bf16[12,128,256]{2,1,0:T(8,128)(2,1)} %get-tuple-element.95), channel_id=1, source_target_pairs={{0,24},{1,25},{2,26},{3,27},{4,28},{5,29},{6,30},{7,31},{8,16},{9,... | collective-permute-start | bytes 2359304 | tf_op jit(solution)/shard_map/ppermute | solution.py:280
  330.8 26.8 %collective-permute-start.51 = (bf16[64,2048]{1,0:T(8,128)(2,1)S(1)}, bf16[64,2048]{1,0:T(8,128)(2,1)S(1)}, u32[]{:S(2)}, u32[]{:S(2)}) collective-permute-start(bf16[64,2048]{1,0:T(8,128)(2,1)S(1)} %fusion.75), channel_id=1, source_target_pairs={{0,24},{1,25},{2,26},{3,27},{4,28},{5,29},{6,30},{7,31},{8,16},{9,... | collective-permute-start | bytes 786440 | tf_op jit(solution)/shard_map/ppermute | solution.py:280
  335.4 30.1 %collective-permute-start.55 = (bf16[4,4,128,256]{3,2,1,0:T(8,128)(2,1)S(1)}, bf16[4,4,128,256]{3,2,1,0:T(8,128)(2,1)S(1)}, u32[]{:S(2)}, u32[]{:S(2)}) collective-permute-start(bf16[4,4,128,256]{3,2,1,0:T(8,128)(2,1)S(1)} %pad_maximum_fusion.4.own_ref), channel_id=1, source_target_pairs={{0,4},{1,5},{2,6},{3,7},{4,0},{5,1},{6,2},{7,3},{8,12},{9,13},{10,... | collective-permute-start | bytes 3145736 | tf_op jit(solution)/shard_map/ppermute | solution.py:280
  360.3 26.4 %collective-permute-start.58 = (bf16[64,2048]{1,0:T(8,128)(2,1)S(1)}, bf16[64,2048]{1,0:T(8,128)(2,1)S(1)}, u32[]{:S(2)}, u32[]{:S(2)}) collective-permute-start(bf16[64,2048]{1,0:T(8,128)(2,1)S(1)} %get-tuple-element.185), channel_id=1, source_target_pairs={{0,8},{1,9},{2,10},{3,11},{4,12},{5,13},{6,14},{7,15},{8,0},{9,1},... | collective-permute-start | bytes 786440 | tf_op jit(solution)/shard_map/ppermute | solution.py:280
  366.5 42.9 %collective-permute-start.67 = (bf16[32,128,256]{2,1,0:T(8,128)(2,1)}, bf16[32,128,256]{2,1,0:T(8,128)(2,1)}, u32[]{:S(2)}, u32[]{:S(2)}) collective-permute-start(bf16[32,128,256]{2,1,0:T(8,128)(2,1)} %get-tuple-element.111), channel_id=1, source_target_pairs={{0,4},{1,5},{2,6},{3,7},{4,0},{5,1},{6,2},{7,3},{8,12},{9,13},{10,... | collective-permute-start | bytes 6291464 | tf_op jit(solution)/shard_map/ppermute | solution.py:280
  373.7 28.8 %collective-permute-start.57 = (bf16[128,2048]{1,0:T(8,128)(2,1)S(1)}, bf16[128,2048]{1,0:T(8,128)(2,1)S(1)}, u32[]{:S(2)}, u32[]{:S(2)}) collective-permute-start(bf16[128,2048]{1,0:T(8,128)(2,1)S(1)} %pad_maximum_fusion.17), channel_id=1, source_target_pairs={{0,1},{1,0},{2,3},{3,2},{4,5},{5,4},{6,7},{7,6},{8,9},{9,8},{10,11... | collective-permute-start | bytes 1572872 | tf_op jit(solution)/shard_map/ppermute | solution.py:280
  495.7 51.8 %collective-permute-start.97 = (bf16[4,4,128,256]{3,2,1,0:T(8,128)(2,1)}, bf16[4,4,128,256]{3,2,1,0:T(8,128)(2,1)}, u32[]{:S(2)}, u32[]{:S(2)}) collective-permute-start(bf16[4,4,128,256]{3,2,1,0:T(8,128)(2,1)} %get-tuple-element.121), channel_id=1, source_target_pairs={{0,4},{1,5},{2,6},{3,7},{4,0},{5,1},{6,2},{7,3},{8,12},{9,13},{10,... | collective-permute-start | bytes 3145736 | tf_op jit(solution)/shard_map/ppermute | solution.py:280
  503.7 83.8 %collective-permute-start.96 = (bf16[2048,512]{1,0:T(8,128)(2,1)S(1)}, bf16[2048,512]{1,0:T(8,128)(2,1)}, u32[]{:S(2)}, u32[]{:S(2)}) collective-permute-start(bf16[2048,512]{1,0:T(8,128)(2,1)S(1)} %slice.834), channel_id=1, source_target_pairs={{0,4},{1,5},{2,6},{3,7},{4,0},{5,1},{6,2},{7,3},{8,12},{9,13},{10,... | collective-permute-start | bytes 6291464 | tf_op jit(solution)/shard_map/ppermute | solution.py:280
  550.6 43.3 %collective-permute-start.100 = (bf16[4,128,256]{2,1,0:T(8,128)(2,1)}, bf16[4,128,256]{2,1,0:T(8,128)(2,1)}, u32[]{:S(2)}, u32[]{:S(2)}) collective-permute-start(bf16[4,128,256]{2,1,0:T(8,128)(2,1)} %get-tuple-element.243), channel_id=1, source_target_pairs={{0,24},{1,25},{2,26},{3,27},{4,28},{5,29},{6,30},{7,31},{8,16},{9,... | collective-permute-start | bytes 786440 | tf_op jit(solution)/shard_map/ppermute | solution.py:280
  550.9 44.1 %collective-permute-start.99 = (bf16[4,128,256]{2,1,0:T(8,128)(2,1)}, bf16[4,128,256]{2,1,0:T(8,128)(2,1)}, u32[]{:S(2)}, u32[]{:S(2)}) collective-permute-start(bf16[4,128,256]{2,1,0:T(8,128)(2,1)} %get-tuple-element.244), channel_id=1, source_target_pairs={{0,16},{1,17},{2,18},{3,19},{4,20},{5,21},{6,22},{7,23},{8,24},{9,... | collective-permute-start | bytes 786440 | tf_op jit(solution)/shard_map/ppermute | solution.py:280
  553.8 41.3 %collective-permute-start.98 = (bf16[4,128,256]{2,1,0:T(8,128)(2,1)}, bf16[4,128,256]{2,1,0:T(8,128)(2,1)}, u32[]{:S(2)}, u32[]{:S(2)}) collective-permute-start(bf16[4,128,256]{2,1,0:T(8,128)(2,1)} %get-tuple-element.245), channel_id=1, source_target_pairs={{0,8},{1,9},{2,10},{3,11},{4,12},{5,13},{6,14},{7,15},{8,0},{9,1},... | collective-permute-start | bytes 786440 | tf_op jit(solution)/shard_map/ppermute | solution.py:280
  609.3 117.2 %collective-permute-start.135 = (bf16[6,128,256]{2,1,0:T(8,128)(2,1)}, bf16[6,128,256]{2,1,0:T(8,128)(2,1)S(1)}, u32[]{:S(2)}, u32[]{:S(2)}) collective-permute-start(bf16[6,128,256]{2,1,0:T(8,128)(2,1)} %get-tuple-element.142), channel_id=1, source_target_pairs={{0,4},{1,5},{2,6},{3,7},{4,0},{5,1},{6,2},{7,3},{8,12},{9,13},{10,... | collective-permute-start | bytes 1179656 | tf_op jit(solution)/shard_map/ppermute | solution.py:280
  631.0 97.4 %collective-permute-start.136 = (bf16[6,128,256]{2,1,0:T(8,128)(2,1)}, bf16[6,128,256]{2,1,0:T(8,128)(2,1)}, u32[]{:S(2)}, u32[]{:S(2)}) collective-permute-start(bf16[6,128,256]{2,1,0:T(8,128)(2,1)} %get-tuple-element.143), channel_id=1, source_target_pairs={{0,8},{1,9},{2,10},{3,11},{4,12},{5,13},{6,14},{7,15},{8,0},{9,1},... | collective-permute-start | bytes 1179656 | tf_op jit(solution)/shard_map/ppermute | solution.py:280
  655.9 60.9 %collective-permute-start.119 = (bf16[64,2048]{1,0:T(8,128)(2,1)S(1)}, bf16[64,2048]{1,0:T(8,128)(2,1)S(1)}, u32[]{:S(2)}, u32[]{:S(2)}) collective-permute-start(bf16[64,2048]{1,0:T(8,128)(2,1)S(1)} %slice.838), channel_id=1, source_target_pairs={{0,2},{1,3},{2,0},{3,1},{4,6},{5,7},{6,4},{7,5},{8,10},{9,11},{10,... | collective-permute-start | bytes 786440 | tf_op jit(solution)/shard_map/ppermute | solution.py:280
  690.6 26.1 %collective-permute-start.128 = (bf16[64,2048]{1,0:T(8,128)(2,1)S(1)}, bf16[64,2048]{1,0:T(8,128)(2,1)S(1)}, u32[]{:S(2)}, u32[]{:S(2)}) collective-permute-start(bf16[64,2048]{1,0:T(8,128)(2,1)S(1)} %get-tuple-element.255), channel_id=1, source_target_pairs={{0,8},{1,9},{2,10},{3,11},{4,12},{5,13},{6,14},{7,15},{8,16},{9,17... | collective-permute-start | bytes 786440 | tf_op jit(solution)/shard_map/ppermute | solution.py:291
  734.1 40.9 %collective-permute-start.144 = (bf16[6,128,256]{2,1,0:T(8,128)(2,1)}, bf16[6,128,256]{2,1,0:T(8,128)(2,1)S(1)}, u32[]{:S(2)}, u32[]{:S(2)}) collective-permute-start(bf16[6,128,256]{2,1,0:T(8,128)(2,1)} %get-tuple-element.151), channel_id=1, source_target_pairs={{0,12},{1,13},{2,14},{3,15},{4,8},{5,9},{6,10},{7,11},{8,4},{9,5},... | collective-permute-start | bytes 1179656 | tf_op jit(solution)/shard_map/ppermute | solution.py:280
  736.0 39.0 %collective-permute-start.145 = (bf16[6,128,256]{2,1,0:T(8,128)(2,1)}, bf16[6,128,256]{2,1,0:T(8,128)(2,1)S(1)}, u32[]{:S(2)}, u32[]{:S(2)}) collective-permute-start(bf16[6,128,256]{2,1,0:T(8,128)(2,1)} %get-tuple-element.152), channel_id=1, source_target_pairs={{0,16},{1,17},{2,18},{3,19},{4,20},{5,21},{6,22},{7,23},{8,24},{9,... | collective-permute-start | bytes 1179656 | tf_op jit(solution)/shard_map/ppermute | solution.py:280
  744.5 32.1 %collective-permute-start.146 = (bf16[6,128,256]{2,1,0:T(8,128)(2,1)}, bf16[6,128,256]{2,1,0:T(8,128)(2,1)S(1)}, u32[]{:S(2)}, u32[]{:S(2)}) collective-permute-start(bf16[6,128,256]{2,1,0:T(8,128)(2,1)} %get-tuple-element.153), channel_id=1, source_target_pairs={{0,20},{1,21},{2,22},{3,23},{4,16},{5,17},{6,18},{7,19},{8,28},{9,... | collective-permute-start | bytes 1179656 | tf_op jit(solution)/shard_map/ppermute | solution.py:280
  745.9 135.1 %collective-permute-start.139 = (bf16[6,128,256]{2,1,0:T(8,128)(2,1)}, bf16[6,128,256]{2,1,0:T(8,128)(2,1)S(1)}, u32[]{:S(2)}, u32[]{:S(2)}) collective-permute-start(bf16[6,128,256]{2,1,0:T(8,128)(2,1)} %get-tuple-element.146), channel_id=1, source_target_pairs={{0,20},{1,21},{2,22},{3,23},{4,16},{5,17},{6,18},{7,19},{8,28},{9,... | collective-permute-start | bytes 1179656 | tf_op jit(solution)/shard_map/ppermute | solution.py:280
  758.2 122.9 %collective-permute-start.140 = (bf16[6,128,256]{2,1,0:T(8,128)(2,1)}, bf16[6,128,256]{2,1,0:T(8,128)(2,1)}, u32[]{:S(2)}, u32[]{:S(2)}) collective-permute-start(bf16[6,128,256]{2,1,0:T(8,128)(2,1)} %get-tuple-element.147), channel_id=1, source_target_pairs={{0,24},{1,25},{2,26},{3,27},{4,28},{5,29},{6,30},{7,31},{8,16},{9,... | collective-permute-start | bytes 1179656 | tf_op jit(solution)/shard_map/ppermute | solution.py:280
  774.9 106.1 %collective-permute-start.141 = (bf16[6,128,256]{2,1,0:T(8,128)(2,1)}, bf16[6,128,256]{2,1,0:T(8,128)(2,1)}, u32[]{:S(2)}, u32[]{:S(2)}) collective-permute-start(bf16[6,128,256]{2,1,0:T(8,128)(2,1)} %get-tuple-element.148), channel_id=1, source_target_pairs={{0,28},{1,29},{2,30},{3,31},{4,24},{5,25},{6,26},{7,27},{8,20},{9,... | collective-permute-start | bytes 1179656 | tf_op jit(solution)/shard_map/ppermute | solution.py:280
  774.9 75.9 %collective-permute-start.147 = (bf16[6,128,256]{2,1,0:T(8,128)(2,1)S(1)}, bf16[6,128,256]{2,1,0:T(8,128)(2,1)S(1)}, u32[]{:S(2)}, u32[]{:S(2)}) collective-permute-start(bf16[6,128,256]{2,1,0:T(8,128)(2,1)S(1)} %copy-done.54), channel_id=1, source_target_pairs={{0,24},{1,25},{2,26},{3,27},{4,28},{5,29},{6,30},{7,31},{8,16},{9,... | collective-permute-start | bytes 1179656 | tf_op jit(solution)/shard_map/ppermute | solution.py:280
  776.6 82.7 %collective-permute-start.148 = (bf16[6,128,256]{2,1,0:T(8,128)(2,1)S(1)}, bf16[6,128,256]{2,1,0:T(8,128)(2,1)S(1)}, u32[]{:S(2)}, u32[]{:S(2)}) collective-permute-start(bf16[6,128,256]{2,1,0:T(8,128)(2,1)S(1)} %copy-done.55), channel_id=1, source_target_pairs={{0,28},{1,29},{2,30},{3,31},{4,24},{5,25},{6,26},{7,27},{8,20},{9,... | collective-permute-start | bytes 1179656 | tf_op jit(solution)/shard_map/ppermute | solution.py:280
  850.8 59.2 %collective-permute-start.132 = (bf16[64,2048]{1,0:T(8,128)(2,1)}, bf16[64,2048]{1,0:T(8,128)(2,1)S(1)}, u32[]{:S(2)}, u32[]{:S(2)}) collective-permute-start(bf16[64,2048]{1,0:T(8,128)(2,1)} %get-tuple-element.165), channel_id=1, source_target_pairs={{0,2},{1,3},{2,0},{3,1},{4,6},{5,7},{6,4},{7,5},{8,10},{9,11},{10,... | collective-permute-start | bytes 786440 | tf_op jit(solution)/shard_map/ppermute | solution.py:280
  860.1 50.4 %collective-permute-start.115 = (bf16[64,2048]{1,0:T(8,128)(2,1)S(1)}, bf16[64,2048]{1,0:T(8,128)(2,1)S(1)}, u32[]{:S(2)}, u32[]{:S(2)}) collective-permute-start(bf16[64,2048]{1,0:T(8,128)(2,1)S(1)} %get-tuple-element.171), channel_id=1, source_target_pairs={{0,2},{1,3},{2,0},{3,1},{4,6},{5,7},{6,4},{7,5},{8,10},{9,11},{10,... | collective-permute-start | bytes 786440 | tf_op jit(solution)/shard_map/ppermute | solution.py:280
  (193 other events, 3126.8 us)
where the time goes:
time: 922 us; the launch traced here: 915 us
  waiting for transfers between devices  412 us (45%)
  starting transfers between devices  219 us (24%)
  Pallas kernels  106 us (11%)
  local copies, waits for them, and re-layouts  63.9 us (7%)
  other arithmetic  60.3 us (7%)
  matrix products  50 us (5%)
    ppermute x125, waiting for transfers between devices, swap(): return lax.ppermute(value, AXES, pairs)  346 us
    ppermute x125, starting transfers between devices, swap(): return lax.ppermute(value, AXES, pairs)  172 us
    ppermute x24, waiting for transfers between devices, shift_z(): return lax.ppermute(value, AXES, pairs)  65.8 us
    ppermute x24, starting transfers between devices, shift_z(): return lax.ppermute(value, AXES, pairs)  47.3 us
    unnamed x188, local copies, waits for them, and re-layouts  41.4 us
    pallas_call x2, Pallas kernels, update(): pl.pallas_call(body, grid_spec=pltpu.PrefetchScalarGridSpec(num_scalar_pr...  37.8 us
    dot_general x5, matrix products, dot_tn(): lax.dot_general(left, right, (((0,), (0,)), ((), ())), preferred_element_...  21.4 us
  transfers between devices with their start and end apart: 149, of which 63 were waited for; matrix products, arithmetic and copies ran while one was open for 15% of the time, Pallas kernels for 8%

commit v1 on v0

--- a/solution.py
+++ b/solution.py
@@ -280,17 +280,6 @@
     return lax.ppermute(value, AXES, pairs)
 
 
-def shift_z(value, step, starts):
-    n_wt = lax.axis_size("wt")
-    pairs = [
-        ((2 * z + x) * n_wt + w, (2 * (z + step) + x) * n_wt + w)
-        for z in starts
-        for x in range(2)
-        for w in range(n_wt)
-    ]
-    return lax.ppermute(value, AXES, pairs)
-
-
 def dot(left, right):
     return jnp.dot(left, right, preferred_element_type=F32)
 
@@ -700,40 +689,8 @@
     )(lane_starts, used, *state, *pieces, *done)
 
 
-def z_hops(piece, z_at):
-    ups, downs = [piece], [piece]
-    for step in (1, 2, 3):
-        ups.append(shift_z(ups[-1], 1, range(step - 1, 3)))
-        downs.append(shift_z(downs[-1], -1, range(1, 5 - step)))
-    return [
-        piece,
-        jnp.where(z_at % 2 == 0, downs[1], ups[1]),
-        jnp.where(z_at < 2, downs[2], ups[2]),
-        jnp.where(
-            z_at < 2,
-            jnp.where(z_at == 0, downs[3], downs[1]),
-            jnp.where(z_at == 2, ups[1], ups[3]),
-        ),
-    ]
-
-
-def z_sums(kept, z_at):
-    def own(target):
-        bits = z_at ^ target
-        return jnp.where(bits == 1, kept[1], jnp.where(bits == 2, kept[2], kept[3]))
-
-    up = down = 0.0
-    for far in (3, 2, 1):
-        up = shift_z((own(z_at + far) + up).astype(LOW), 1, range(0, 4 - far)).astype(F32)
-        down = shift_z((own(z_at - far) + down).astype(LOW), -1, range(far, 4)).astype(F32)
-    return kept[0] + up + down
-
-
-def gather_rows(piece, z_at=None):
-    if z_at is None:
-        near = [piece] + [swap(piece, 2 * k, 0) for k in (1, 2, 3)]
-    else:
-        near = z_hops(piece, z_at)
+def gather_rows(piece):
+    near = [piece] + [swap(piece, 2 * k, 0) for k in (1, 2, 3)]
     blocks = []
     for part in near:
         pair = jnp.concatenate([part, swap(part, 0, 2)])
@@ -741,7 +698,7 @@
     return jnp.concatenate(blocks)
 
 
-def scatter_sum(partial_sum, z_at=None):
+def scatter_sum(partial_sum):
     quarter = partial_sum.shape[0] // 4
     half, rows = quarter // 2, quarter // 4
     kept = [None] * 4
@@ -751,12 +708,11 @@
         pair = chunk[:half].astype(F32) + other.astype(F32)
         other = swap(pair[rows:].astype(LOW), 0, 2)
         kept[k] = pair[:rows] + other.astype(F32)
-    if z_at is not None:
-        return z_sums(kept, z_at), kept[0]
     total = kept[0]
-    for k in (1, 2, 3):
-        total = total + swap(kept[k].astype(LOW), 2 * k, 0).astype(F32)
-    return total, kept[0]
+    came = [swap(kept[k].astype(LOW), 2 * k, 0) for k in (3, 2, 1)]
+    for part in came:
+        total = total + part.astype(F32)
+    return total, other
 
 
 def share_rows(piece, wt_index):
@@ -803,16 +759,15 @@
         cut_vals = jnp.where(x_at == 0, values, flipped)
         return cut_vals.reshape(-1, 4, width // 4).transpose(0, 2, 1).reshape(-1, width)
 
-    cut = lane_split(master, lane_starts)
-    came = [cut[0]] + [swap(cut[k], k, 0) for k in range(1, 8)]
-    tokens_later, grads_later = after(tokens, cut[0]), after(cotangent, cut[0])
-    inputs = lax.dynamic_slice(tokens_later, (wt * rows, 0), (rows, width)).astype(F32)
-    out_grad_low = lax.dynamic_slice(grads_later, (wt * rows, 0), (rows, width))
+    inputs = lax.dynamic_slice(tokens, (wt * rows, 0), (rows, width)).astype(F32)
     normed, norm_back = jax.vjp(layer_norm, inputs)
     normed_cut = to_cut_order(normed.astype(LOW))
-    normed_all = gather_rows(normed_cut, z_at)
-    grad_all = gather_rows(out_grad_low, z_at)
-    came[7], normed_all, grad_all = lax.optimization_barrier((came[7], normed_all, grad_all))
+    normed_all = gather_rows(normed_cut)
+    cut = lane_split(master, after(lane_starts, normed_cut))
+    came = [cut[0]] + [swap(cut[k], k, 0) for k in range(1, 8)]
+    out_grad_low = lax.dynamic_slice(cotangent, (wt * rows, 0), (rows, width))
+    grad_all = gather_rows(out_grad_low)
+    came[7], normed_all = lax.optimization_barrier((came[7], normed_all))
     w_qkv = pick_qkv(came, owner_bits[:12], slot_in_owner[:12])
     w_qkv_pair = swap(w_qkv, 1, 0)
     wanted = jnp.concatenate(
@@ -886,11 +841,13 @@
     two_grad, begun = scatter_sum(dot_nt(grad_gu, w_gu).astype(LOW))
     hidden_later, grad_gu_later = lax.optimization_barrier((hidden, grad_gu, begun))[:2]
     grad_w_gu = dot_tn(two_all, grad_gu_later)
+    grad_w_down = dot_tn(hidden_later, grad_all)
     gu_back = swap(grad_w_gu[:, 512:].astype(LOW), 1, 0)
-    grad_w_down = dot_tn(hidden_later, grad_all)
 
     resid_grad = out_grad_low.astype(F32) + norm_two_back(two_grad)[0]
     resid_all = gather_rows(resid_grad.astype(LOW))
+    down, _ = scatter_sum(dot(after(hidden, two_grad), w_down).astype(LOW))
+    output = share_rows((residual + down).astype(LOW), wt)
     gu_sum = (grad_w_gu[:, :512] + gu_back.astype(F32)).astype(LOW)
     down_came = return_halves(grad_w_down.reshape(4, tile_rows, width), lane_starts)
 
@@ -921,16 +878,13 @@
     qkv_sum = (dot_tn(normed_all[:, :half], qkv_grad) + qkv_back.astype(F32)).astype(LOW)
     sends = place_attention(sends, qkv_sum, out_grad_came, send_to, send_row, place)
 
-    qkv_grad_later, hidden_last = lax.optimization_barrier((qkv_grad, hidden, sends[0]))[:2]
+    qkv_grad_later = after(qkv_grad, sends[0])
     one_part = jnp.concatenate(
         [dot_nt(qkv_grad_later, w_qkv), dot_nt(qkv_grad_later, w_qkv_pair)], axis=1
     )
-    down_part = dot(hidden_last, w_down)
-    one_grad = from_cut_order(scatter_sum(one_part.astype(LOW), z_at)[0])
+    one_grad = from_cut_order(scatter_sum(one_part.astype(LOW))[0])
     input_grad = resid_grad + norm_back(one_grad)[0]
     input_grad = share_rows(input_grad.astype(LOW), wt).astype(F32)
-    down, _ = scatter_sum(down_part.astype(LOW), z_at)
-    output = share_rows((residual + down).astype(LOW), wt)
 
     slot_range = jnp.arange(cap, dtype=jnp.int32) + ctx * cap
     used = jnp.any(

time: 922 us -> 922 us (level)
  starting transfers between devices: 219 us -> 170 us
  local copies, waits for them, and re-layouts: 63.9 us -> 83.7 us
  waiting for transfers between devices: 412 us -> 430 us
    ppermute x125 -> x137, waiting for transfers between devices: 346 us -> 430 us  [swap(): return lax.ppermute(value, AXES, pairs)]
    ppermute x24 -> x0, waiting for transfers between devices: 65.8 us -> none  [shift_z(): return lax.ppermute(value, AXES, pairs)]
    ppermute x24 -> x0, starting transfers between devices: 47.3 us -> none  [shift_z(): return lax.ppermute(value, AXES, pairs)]
    concatenate x16, other arithmetic: 8.63 us -> 20.3 us  [gather_rows(): pair = jnp.concatenate([part, swap(part, 0, 2)])]
    ppermute x125 -> x137, starting transfers between devices: 172 us -> 170 us  [swap(): return lax.ppermute(value, AXES, pairs)]
    unnamed x188 -> x211, local copies, waits for them, and re-layouts: 41.4 us -> 41.9 us
  transfers between devices with their start and end apart: 149 -> 137, of which waited for: 63 -> 53; matrix products, arithmetic and copies ran while one was open for 15% -> 18% of each run, Pallas kernels for 8% -> 12%
where the time goes in v1:
time: 922 us; the launch traced here: 911 us
  waiting for transfers between devices  430 us (47%)
  starting transfers between devices  170 us (18%)
  Pallas kernels  106 us (11%)
  local copies, waits for them, and re-layouts  83.7 us (9%)
  other arithmetic  67.3 us (7%)
  matrix products  51.7 us (6%)
    ppermute x137, waiting for transfers between devices, swap(): return lax.ppermute(value, AXES, pairs)  430 us
    ppermute x137, starting transfers between devices, swap(): return lax.ppermute(value, AXES, pairs)  170 us
    unnamed x211, local copies, waits for them, and re-layouts  41.9 us
    pallas_call x2, Pallas kernels, update(): pl.pallas_call(body, grid_spec=pltpu.PrefetchScalarGridSpec(num_scalar_pr...  37.9 us
    dot_general x5, matrix products, dot_tn(): lax.dot_general(left, right, (((0,), (0,)), ((), ())), preferred_element_...  23.1 us
    concatenate x16, other arithmetic, gather_rows(): pair = jnp.concatenate([part, swap(part, 0, 2)])  20.3 us
  transfers between devices with their start and end apart: 137, of which 53 were waited for; matrix products, arithmetic and copies ran while one was open for 18% of the time, Pallas kernels for 12%

profile of v1, /device:TPU:9, one launch (start us, length us, event | category | flops | bytes accessed | tf_op | source)
XLA Modules:
  0.0 910.6 jit_solution(1422319369002541956)
XLA Ops:
  14.9 25.4 %collective-permute-done.9 = bf16[64,2048]{0,1:T(8,128)(2,1)S(1)} collective-permute-done((bf16[64,2048]{0,1:T(8,128)(2,1)S(1)}, bf16[64,2048]{0,1:T(8,128)(2,1)S(1)}, u32[]{:S(2)}, u32[]{:S(2)}) %collective-permute-start.9) | collective-permute-done | bytes 262176 | tf_op jit(solution)/shard_map/ppermute | solution.py:280
  40.3 21.3 %collective-permute-done.6 = bf16[64,2048]{0,1:T(8,128)(2,1)S(1)} collective-permute-done((bf16[64,2048]{0,1:T(8,128)(2,1)S(1)}, bf16[64,2048]{0,1:T(8,128)(2,1)S(1)}, u32[]{:S(2)}, u32[]{:S(2)}) %collective-permute-start.6) | collective-permute-done | bytes 262176 | tf_op jit(solution)/shard_map/ppermute | solution.py:280
  70.3 12.2 %lane_split.1 = (bf16[12,128,256]{2,1,0:T(8,128)(2,1)}, bf16[12,128,256]{2,1,0:T(8,128)(2,1)}, bf16[12,128,256]{2,1,0:T(8,128)(2,1)}, bf16[12,128,256]{2,1,0:T(8...) custom-call(s32[16]{0:T(128)} %mul.265.starts, ...), custom_call_target="tpu_custom_call" | custom-call | tf_op jit(solution)/shard_map/lane_split/pallas_call | solution.py:307
  93.1 9.9 %collective-permute-done.4 = bf16[64,2048]{0,1:T(8,128)(2,1)} collective-permute-done((bf16[64,2048]{0,1:T(8,128)(2,1)S(1)}, bf16[64,2048]{0,1:T(8,128)(2,1)}, u32[]{:S(2)}, u32[]{:S(2)}) %collective-permute-start.4) | collective-permute-done | bytes 262176 | tf_op jit(solution)/shard_map/ppermute | solution.py:280
  149.0 8.8 concatenate.111
  157.8 11.6 %collective-permute-done.14.refs_3_ = bf16[12,128,256]{2,1,0:T(8,128)(2,1)} collective-permute-done((bf16[12,128,256]{2,1,0:T(8,128)(2,1)}, bf16[12,128,256]{2,1,0:T(8,128)(2,1)}, u32[]{:S(2)}, u32[]{:S(2)}) %collective-permute-start.14) | collective-permute-done | bytes 786464 | tf_op jit(solution)/shard_map/ppermute | solution.py:280
  173.5 49.6 %collective-permute-done.16.refs_5_ = bf16[12,128,256]{2,1,0:T(8,128)(2,1)} collective-permute-done((bf16[12,128,256]{2,1,0:T(8,128)(2,1)}, bf16[12,128,256]{2,1,0:T(8,128)(2,1)}, u32[]{:S(2)}, u32[]{:S(2)}) %collective-permute-start.16) | collective-permute-done | bytes 786464 | tf_op jit(solution)/shard_map/ppermute | solution.py:280
  223.1 17.9 %collective-permute-done.17.refs_6_ = bf16[12,128,256]{2,1,0:T(8,128)(2,1)} collective-permute-done((bf16[12,128,256]{2,1,0:T(8,128)(2,1)}, bf16[12,128,256]{2,1,0:T(8,128)(2,1)}, u32[]{:S(2)}, u32[]{:S(2)}) %collective-permute-start.17) | collective-permute-done | bytes 786464 | tf_op jit(solution)/shard_map/ppermute | solution.py:280
  252.2 5.5 row_gather.1
  277.7 9.9 %collective-permute-done.23.other_ref = bf16[4,1,128,256]{3,2,1,0:T(8,128)(2,1)S(1)} collective-permute-done((bf16[4,1,128,256]{3,2,1,0:T(8,128)(2,1)S(1)}, bf16[4,1,128,256]{3,2,1,0:T(8,128)(2,1)S(1)}, u32[]{:S(2)}, u32[]{:S(2)}) %collective-permute-start.23) | collective-permute-done | bytes 262176 | tf_op jit(solution)/shard_map/ppermute | solution.py:280
  291.8 8.3 attend.1
  337.2 11.1 %collective-permute-start.57 = (bf16[128,2048]{1,0:T(8,128)(2,1)S(1)}, bf16[128,2048]{1,0:T(8,128)(2,1)S(1)}, u32[]{:S(2)}, u32[]{:S(2)}) collective-permute-start(bf16[128,2048]{1,0:T(8,128)(2,1)S(1)} %copy-done.53), channel_id=1, source_target_pairs={{0,1},{1,0},{2,3},{3,2},{4,5},{5,4},{6,7},{7,6},{8,9},{9,8},{10,11... | collective-permute-start | bytes 1572872 | tf_op jit(solution)/shard_map/ppermute | solution.py:280
  367.7 5.7 collective-permute-done.61.other_ref
  409.2 11.9 %collective-permute-done.46 = bf16[32,128,256]{2,1,0:T(8,128)(2,1)} collective-permute-done((bf16[32,128,256]{2,1,0:T(8,128)(2,1)}, bf16[32,128,256]{2,1,0:T(8,128)(2,1)}, u32[]{:S(2)}, u32[]{:S(2)}) %collective-permute-start.46) | collective-permute-done | bytes 2097184 | tf_op jit(solution)/shard_map/ppermute | solution.py:280
  467.0 5.5 collective-permute-done.71
  478.1 6.8 fusion.128
  516.8 5.9 collective-permute-done.89
  561.7 11.8 %attend_back.1 = (f32[1024,128]{1,0:T(8,128)}, f32[1024,256]{1,0:T(8,128)}, bf16[1024,256]{1,0:T(8,128)(2,1)}) custom-call(bf16[1024,128]{1,0:T(8,128)(2,1)} %pad_maximum_fusion.25.q, bf16[1024,256]{1,0:T(8,128)(2,1)} %copy-done.5, bf16[1024,256]{1,0:T(8,128)(2,1)} %copy-done.30, bf16[1024,128]{1,0:T(8,128)(2,1)} %convolution_convert_fusion.5.do, ...), custom_call_target="tpu_custom_call" | custom-call | tf_op jit(solution)/shard_map/attend_back/pallas_call | solution.py:634
  582.5 20.6 %collective-permute-done.98 = bf16[1024,256]{1,0:T(8,128)(2,1)} collective-permute-done((bf16[1024,256]{1,0:T(8,128)(2,1)}, bf16[1024,256]{1,0:T(8,128)(2,1)}, u32[]{:S(2)}, u32[]{:S(2)}) %collective-permute-start.98) | collective-permute-done | bytes 524320 | tf_op jit(solution)/shard_map/ppermute | solution.py:280
  627.5 6.3 place_mlp.1
  658.8 12.3 %collective-permute-done.77 = bf16[64,2048]{1,0:T(8,128)(2,1)S(1)} collective-permute-done((bf16[64,2048]{1,0:T(8,128)(2,1)S(1)}, bf16[64,2048]{1,0:T(8,128)(2,1)S(1)}, u32[]{:S(2)}, u32[]{:S(2)}) %collective-permute-start.77) | collective-permute-done | bytes 262176 | tf_op jit(solution)/shard_map/ppermute | solution.py:280
  684.5 10.5 %collective-permute-done.115 = bf16[64,2048]{0,1:T(8,128)(2,1)S(1)} collective-permute-done((bf16[64,2048]{0,1:T(8,128)(2,1)S(1)}, bf16[64,2048]{0,1:T(8,128)(2,1)S(1)}, u32[]{:S(2)}, u32[]{:S(2)}) %collective-permute-start.115) | collective-permute-done | bytes 262176 | tf_op jit(solution)/shard_map/ppermute | solution.py:280
  698.9 18.4 %collective-permute-done.112 = bf16[64,2048]{0,1:T(8,128)(2,1)S(1)} collective-permute-done((bf16[64,2048]{0,1:T(8,128)(2,1)S(1)}, bf16[64,2048]{0,1:T(8,128)(2,1)S(1)}, u32[]{:S(2)}, u32[]{:S(2)}) %collective-permute-start.112) | collective-permute-done | bytes 262176 | tf_op jit(solution)/shard_map/ppermute | solution.py:280
  727.9 16.4 %collective-permute-done.113 = bf16[64,2048]{0,1:T(8,128)(2,1)} collective-permute-done((bf16[64,2048]{0,1:T(8,128)(2,1)}, bf16[64,2048]{0,1:T(8,128)(2,1)}, u32[]{:S(2)}, u32[]{:S(2)}) %collective-permute-start.113) | collective-permute-done | bytes 262176 | tf_op jit(solution)/shard_map/ppermute | solution.py:280
  756.9 7.8 collective-permute-done.126.refs_4_
  769.2 10.9 %collective-permute-done.131.refs_2_ = bf16[6,128,256]{2,1,0:T(8,128)(2,1)S(1)} collective-permute-done((bf16[6,128,256]{2,1,0:T(8,128)(2,1)}, bf16[6,128,256]{2,1,0:T(8,128)(2,1)S(1)}, u32[]{:S(2)}, u32[]{:S(2)}) %collective-permute-start.131) | collective-permute-done | bytes 393248 | tf_op jit(solution)/shard_map/ppermute | solution.py:280
  781.9 8.2 collective-permute-done.132.refs_3_
  794.4 38.2 %collective-permute-done.134.refs_5_ = bf16[6,128,256]{2,1,0:T(8,128)(2,1)} collective-permute-done((bf16[6,128,256]{2,1,0:T(8,128)(2,1)}, bf16[6,128,256]{2,1,0:T(8,128)(2,1)}, u32[]{:S(2)}, u32[]{:S(2)}) %collective-permute-start.134) | collective-permute-done | bytes 393248 | tf_op jit(solution)/shard_map/ppermute | solution.py:280
  834.1 16.7 %collective-permute-done.135.refs_6_ = bf16[6,128,256]{2,1,0:T(8,128)(2,1)} collective-permute-done((bf16[6,128,256]{2,1,0:T(8,128)(2,1)}, bf16[6,128,256]{2,1,0:T(8,128)(2,1)}, u32[]{:S(2)}, u32[]{:S(2)}) %collective-permute-start.135) | collective-permute-done | bytes 393248 | tf_op jit(solution)/shard_map/ppermute | solution.py:280
  853.5 6.6 collective-permute-done.136.refs_7_
  866.6 19.0 %update.2 = (f32[12,128,2048]{2,1,0:T(8,128)}, f32[12,128,2048]{2,1,0:T(8,128)}, f32[12,128,2048]{2,1,0:T(8,128)}, bf16[12,128,2048]{2,1,0:T(8,128)(2,1)}) custom-call(s32[16]{0:T(128)} %mul.265.starts, s32[12]{0:T(128)} %convert_element_type.575.live, f32[12,128,2048]{2,1,0:T(8,128)} %mas.3, f32[12,128,2048]{2,1,0:T(8,128)} %one.3, f32[12,128,2048]{2,1,0:T(8,128)} %two.3, ...), custom_call_target="tpu_custom_call" | custom-call | tf_op jit(solution)/shard_map/update/pallas_call | solution.py:678
  886.7 18.9 %update.3 = (f32[12,128,2048]{2,1,0:T(8,128)}, f32[12,128,2048]{2,1,0:T(8,128)}, f32[12,128,2048]{2,1,0:T(8,128)}, bf16[12,128,2048]{2,1,0:T(8,128)(2,1)}) custom-call(s32[16]{0:T(128)} %mul.265.starts, s32[12]{0:T(128)} %convert_element_type.575.live, ...), custom_call_target="tpu_custom_call", output_to_operand_aliasing={{0}: (13, {}), {1}: (14, {}), {2}: (15, {}), {3}: (16, {})} | custom-call | tf_op jit(solution)/shard_map/update/pallas_call | solution.py:678
  (636 shorter events, 458.2 us)
Async XLA Ops:
  6.1 55.5 %collective-permute-start.6 = (bf16[64,2048]{0,1:T(8,128)(2,1)S(1)}, bf16[64,2048]{0,1:T(8,128)(2,1)S(1)}, u32[]{:S(2)}, u32[]{:S(2)}) collective-permute-start(bf16[64,2048]{0,1:T(8,128)(2,1)S(1)} %maximum_select_fusion.1), channel_id=1, source_target_pairs={{0,16},{1,17},{2,18},{3,19},{4,20},{5,21},{6,22},{7,23},{8,24},{9,... | collective-permute-start | bytes 786440 | tf_op jit(solution)/shard_map/ppermute | solution.py:280
  7.2 56.7 %collective-permute-start.3 = (bf16[64,2048]{0,1:T(8,128)(2,1)S(1)}, bf16[64,2048]{0,1:T(8,128)(2,1)S(1)}, u32[]{:S(2)}, u32[]{:S(2)}) collective-permute-start(bf16[64,2048]{0,1:T(8,128)(2,1)S(1)} %maximum_select_fusion.1), channel_id=1, source_target_pairs={{0,8},{1,9},{2,10},{3,11},{4,12},{5,13},{6,14},{7,15},{8,0},{9,1},... | collective-permute-start | bytes 786440 | tf_op jit(solution)/shard_map/ppermute | solution.py:280
  8.3 56.9 %collective-permute-start.1 = (bf16[64,2048]{0,1:T(8,128)(2,1)S(1)}, bf16[64,2048]{0,1:T(8,128)(2,1)S(1)}, u32[]{:S(2)}, u32[]{:S(2)}) collective-permute-start(bf16[64,2048]{0,1:T(8,128)(2,1)S(1)} %maximum_select_fusion.1), channel_id=1, source_target_pairs={{0,2},{1,3},{2,0},{3,1},{4,6},{5,7},{6,4},{7,5},{8,10},{9,11},{10,... | collective-permute-start | bytes 786440 | tf_op jit(solution)/shard_map/ppermute | solution.py:280
  11.2 57.2 %collective-permute-start.55 = (bf16[64,2048]{1,0:T(8,128)(2,1)S(1)}, bf16[64,2048]{1,0:T(8,128)(2,1)S(1)}, u32[]{:S(2)}, u32[]{:S(2)}) collective-permute-start(bf16[64,2048]{1,0:T(8,128)(2,1)S(1)} %get-tuple-element.173), channel_id=1, source_target_pairs={{0,24},{1,25},{2,26},{3,27},{4,28},{5,29},{6,30},{7,31},{8,16},{9,... | collective-permute-start | bytes 786440 | tf_op jit(solution)/shard_map/ppermute | solution.py:280
  40.2 42.3 %collective-permute-start.52 = (bf16[64,2048]{1,0:T(8,128)(2,1)S(1)}, bf16[64,2048]{1,0:T(8,128)(2,1)}, u32[]{:S(2)}, u32[]{:S(2)}) collective-permute-start(bf16[64,2048]{1,0:T(8,128)(2,1)S(1)} %get-tuple-element.173), channel_id=1, source_target_pairs={{0,16},{1,17},{2,18},{3,19},{4,20},{5,21},{6,22},{7,23},{8,24},{9,... | collective-permute-start | bytes 786440 | tf_op jit(solution)/shard_map/ppermute | solution.py:280
  84.0 42.1 %collective-permute-start = (bf16[12,128,256]{2,1,0:T(8,128)(2,1)}, bf16[12,128,256]{2,1,0:T(8,128)(2,1)S(1)}, u32[]{:S(2)}, u32[]{:S(2)}) collective-permute-start(bf16[12,128,256]{2,1,0:T(8,128)(2,1)} %get-tuple-element.84), channel_id=1, source_target_pairs={{0,28},{1,29},{2,30},{3,31},{4,24},{5,25},{6,26},{7,27},{8,20},{9,... | collective-permute-start | bytes 2359304 | tf_op jit(solution)/shard_map/ppermute | solution.py:280
  86.0 37.7 %collective-permute-start.2 = (bf16[128,2048]{0,1:T(8,128)(2,1)}, bf16[128,2048]{0,1:T(8,128)(2,1)}, u32[]{:S(2)}, u32[]{:S(2)}) collective-permute-start(bf16[128,2048]{0,1:T(8,128)(2,1)} %pad_maximum_fusion.8), channel_id=1, source_target_pairs={{0,1},{1,0},{2,3},{3,2},{4,5},{5,4},{6,7},{7,6},{8,9},{9,8},{10,11... | collective-permute-start | bytes 1572872 | tf_op jit(solution)/shard_map/ppermute | solution.py:280
  135.9 37.6 %collective-permute-start.15 = (bf16[12,128,256]{2,1,0:T(8,128)(2,1)}, bf16[12,128,256]{2,1,0:T(8,128)(2,1)}, u32[]{:S(2)}, u32[]{:S(2)}) collective-permute-start(bf16[12,128,256]{2,1,0:T(8,128)(2,1)} %get-tuple-element.90), channel_id=1, source_target_pairs={{0,16},{1,17},{2,18},{3,19},{4,20},{5,21},{6,22},{7,23},{8,24},{9,... | collective-permute-start | bytes 2359304 | tf_op jit(solution)/shard_map/ppermute | solution.py:280
  139.1 83.9 %collective-permute-start.16 = (bf16[12,128,256]{2,1,0:T(8,128)(2,1)}, bf16[12,128,256]{2,1,0:T(8,128)(2,1)}, u32[]{:S(2)}, u32[]{:S(2)}) collective-permute-start(bf16[12,128,256]{2,1,0:T(8,128)(2,1)} %get-tuple-element.91), channel_id=1, source_target_pairs={{0,20},{1,21},{2,22},{3,23},{4,16},{5,17},{6,18},{7,19},{8,28},{9,... | collective-permute-start | bytes 2359304 | tf_op jit(solution)/shard_map/ppermute | solution.py:280
  139.3 101.7 %collective-permute-start.17 = (bf16[12,128,256]{2,1,0:T(8,128)(2,1)}, bf16[12,128,256]{2,1,0:T(8,128)(2,1)}, u32[]{:S(2)}, u32[]{:S(2)}) collective-permute-start(bf16[12,128,256]{2,1,0:T(8,128)(2,1)} %get-tuple-element.92), channel_id=1, source_target_pairs={{0,24},{1,25},{2,26},{3,27},{4,28},{5,29},{6,30},{7,31},{8,16},{9,... | collective-permute-start | bytes 2359304 | tf_op jit(solution)/shard_map/ppermute | solution.py:280
  142.1 104.0 %collective-permute-start.48 = (bf16[128,2048]{1,0:T(8,128)(2,1)}, bf16[128,2048]{1,0:T(8,128)(2,1)}, u32[]{:S(2)}, u32[]{:S(2)}) collective-permute-start(bf16[128,2048]{1,0:T(8,128)(2,1)} %pad_maximum_fusion.17), channel_id=1, source_target_pairs={{0,1},{1,0},{2,3},{3,2},{4,5},{5,4},{6,7},{7,6},{8,9},{9,8},{10,11... | collective-permute-start | bytes 1572872 | tf_op jit(solution)/shard_map/ppermute | solution.py:280
  169.5 106.6 %collective-permute-start.51 = (bf16[128,2048]{1,0:T(8,128)(2,1)}, bf16[128,2048]{1,0:T(8,128)(2,1)S(1)}, u32[]{:S(2)}, u32[]{:S(2)}) collective-permute-start(bf16[128,2048]{1,0:T(8,128)(2,1)} %pad_maximum_fusion.18), channel_id=1, source_target_pairs={{0,1},{1,0},{2,3},{3,2},{4,5},{5,4},{6,7},{7,6},{8,9},{9,8},{10,11... | collective-permute-start | bytes 1572872 | tf_op jit(solution)/shard_map/ppermute | solution.py:280
  272.0 45.2 %collective-permute-start.54 = (bf16[128,2048]{1,0:T(8,128)(2,1)S(1)}, bf16[128,2048]{1,0:T(8,128)(2,1)}, u32[]{:S(2)}, u32[]{:S(2)}) collective-permute-start(bf16[128,2048]{1,0:T(8,128)(2,1)S(1)} %copy-done.54), channel_id=1, source_target_pairs={{0,1},{1,0},{2,3},{3,2},{4,5},{5,4},{6,7},{7,6},{8,9},{9,8},{10,11... | collective-permute-start | bytes 1572872 | tf_op jit(solution)/shard_map/ppermute | solution.py:280
  374.4 46.7 %collective-permute-start.46 = (bf16[32,128,256]{2,1,0:T(8,128)(2,1)}, bf16[32,128,256]{2,1,0:T(8,128)(2,1)}, u32[]{:S(2)}, u32[]{:S(2)}) collective-permute-start(bf16[32,128,256]{2,1,0:T(8,128)(2,1)} %get-tuple-element.102), channel_id=1, source_target_pairs={{0,4},{1,5},{2,6},{3,7},{4,0},{5,1},{6,2},{7,3},{8,12},{9,13},{10,... | collective-permute-start | bytes 6291464 | tf_op jit(solution)/shard_map/ppermute | solution.py:280
  522.9 94.2 %collective-permute-start.104 = (bf16[2048,512]{1,0:T(8,128)(2,1)}, bf16[2048,512]{1,0:T(8,128)(2,1)}, u32[]{:S(2)}, u32[]{:S(2)}) collective-permute-start(bf16[2048,512]{1,0:T(8,128)(2,1)} %slice.856), channel_id=1, source_target_pairs={{0,4},{1,5},{2,6},{3,7},{4,0},{5,1},{6,2},{7,3},{8,12},{9,13},{10,... | collective-permute-start | bytes 6291464 | tf_op jit(solution)/shard_map/ppermute | solution.py:280
  546.0 104.2 %collective-permute-start.79 = (bf16[64,2048]{1,0:T(8,128)(2,1)}, bf16[64,2048]{1,0:T(8,128)(2,1)}, u32[]{:S(2)}, u32[]{:S(2)}) collective-permute-start(bf16[64,2048]{1,0:T(8,128)(2,1)} %slice.863), channel_id=1, source_target_pairs={{0,2},{1,3},{2,0},{3,1},{4,6},{5,7},{6,4},{7,5},{8,10},{9,11},{10,... | collective-permute-start | bytes 786440 | tf_op jit(solution)/shard_map/ppermute | solution.py:280
  553.4 69.6 %collective-permute-start.108 = (bf16[4,128,256]{2,1,0:T(8,128)(2,1)}, bf16[4,128,256]{2,1,0:T(8,128)(2,1)}, u32[]{:S(2)}, u32[]{:S(2)}) collective-permute-start(bf16[4,128,256]{2,1,0:T(8,128)(2,1)} %get-tuple-element.217), channel_id=1, source_target_pairs={{0,24},{1,25},{2,26},{3,27},{4,28},{5,29},{6,30},{7,31},{8,16},{9,... | collective-permute-start | bytes 786440 | tf_op jit(solution)/shard_map/ppermute | solution.py:280
  554.6 69.6 %collective-permute-start.107 = (bf16[4,128,256]{2,1,0:T(8,128)(2,1)}, bf16[4,128,256]{2,1,0:T(8,128)(2,1)}, u32[]{:S(2)}, u32[]{:S(2)}) collective-permute-start(bf16[4,128,256]{2,1,0:T(8,128)(2,1)} %get-tuple-element.218), channel_id=1, source_target_pairs={{0,16},{1,17},{2,18},{3,19},{4,20},{5,21},{6,22},{7,23},{8,24},{9,... | collective-permute-start | bytes 786440 | tf_op jit(solution)/shard_map/ppermute | solution.py:280
  677.1 42.7 %collective-permute-start.84 = (bf16[64,2048]{1,0:T(8,128)(2,1)}, bf16[64,2048]{1,0:T(8,128)(2,1)}, u32[]{:S(2)}, u32[]{:S(2)}) collective-permute-start(bf16[64,2048]{1,0:T(8,128)(2,1)} %get-tuple-element.171), channel_id=1, source_target_pairs={{0,2},{1,3},{2,0},{3,1},{4,6},{5,7},{6,4},{7,5},{8,10},{9,11},{10,... | collective-permute-start | bytes 786440 | tf_op jit(solution)/shard_map/ppermute | solution.py:280
  679.3 44.9 %collective-permute-start.110 = (bf16[64,2048]{0,1:T(8,128)(2,1)S(1)}, bf16[64,2048]{0,1:T(8,128)(2,1)}, u32[]{:S(2)}, u32[]{:S(2)}) collective-permute-start(bf16[64,2048]{0,1:T(8,128)(2,1)S(1)} %slice.860), channel_id=1, source_target_pairs={{0,2},{1,3},{2,0},{3,1},{4,6},{5,7},{6,4},{7,5},{8,10},{9,11},{10,... | collective-permute-start | bytes 786440 | tf_op jit(solution)/shard_map/ppermute | solution.py:280
  680.3 37.0 %collective-permute-start.112 = (bf16[64,2048]{0,1:T(8,128)(2,1)S(1)}, bf16[64,2048]{0,1:T(8,128)(2,1)S(1)}, u32[]{:S(2)}, u32[]{:S(2)}) collective-permute-start(bf16[64,2048]{0,1:T(8,128)(2,1)S(1)} %slice.859), channel_id=1, source_target_pairs={{0,2},{1,3},{2,0},{3,1},{4,6},{5,7},{6,4},{7,5},{8,10},{9,11},{10,... | collective-permute-start | bytes 786440 | tf_op jit(solution)/shard_map/ppermute | solution.py:280
  681.6 42.6 %collective-permute-start.119 = (bf16[64,2048]{0,1:T(8,128)(2,1)}, bf16[64,2048]{0,1:T(8,128)(2,1)}, u32[]{:S(2)}, u32[]{:S(2)}) collective-permute-start(bf16[64,2048]{0,1:T(8,128)(2,1)} %fusion.18), channel_id=1, source_target_pairs={{0,8},{1,9},{2,10},{3,11},{4,12},{5,13},{6,14},{7,15},{8,0},{9,1},... | collective-permute-start | bytes 786440 | tf_op jit(solution)/shard_map/ppermute | solution.py:280
  751.2 38.9 %collective-permute-start.132 = (bf16[6,128,256]{2,1,0:T(8,128)(2,1)}, bf16[6,128,256]{2,1,0:T(8,128)(2,1)}, u32[]{:S(2)}, u32[]{:S(2)}) collective-permute-start(bf16[6,128,256]{2,1,0:T(8,128)(2,1)} %get-tuple-element.147), channel_id=1, source_target_pairs={{0,12},{1,13},{2,14},{3,15},{4,8},{5,9},{6,10},{7,11},{8,4},{9,5},... | collective-permute-start | bytes 1179656 | tf_op jit(solution)/shard_map/ppermute | solution.py:280
  754.8 38.7 %collective-permute-start.133 = (bf16[6,128,256]{2,1,0:T(8,128)(2,1)}, bf16[6,128,256]{2,1,0:T(8,128)(2,1)}, u32[]{:S(2)}, u32[]{:S(2)}) collective-permute-start(bf16[6,128,256]{2,1,0:T(8,128)(2,1)} %get-tuple-element.148), channel_id=1, source_target_pairs={{0,16},{1,17},{2,18},{3,19},{4,20},{5,21},{6,22},{7,23},{8,24},{9,... | collective-permute-start | bytes 1179656 | tf_op jit(solution)/shard_map/ppermute | solution.py:280
  764.7 68.0 %collective-permute-start.134 = (bf16[6,128,256]{2,1,0:T(8,128)(2,1)}, bf16[6,128,256]{2,1,0:T(8,128)(2,1)}, u32[]{:S(2)}, u32[]{:S(2)}) collective-permute-start(bf16[6,128,256]{2,1,0:T(8,128)(2,1)} %get-tuple-element.149), channel_id=1, source_target_pairs={{0,20},{1,21},{2,22},{3,23},{4,16},{5,17},{6,18},{7,19},{8,28},{9,... | collective-permute-start | bytes 1179656 | tf_op jit(solution)/shard_map/ppermute | solution.py:280
  769.1 81.7 %collective-permute-start.135 = (bf16[6,128,256]{2,1,0:T(8,128)(2,1)}, bf16[6,128,256]{2,1,0:T(8,128)(2,1)}, u32[]{:S(2)}, u32[]{:S(2)}) collective-permute-start(bf16[6,128,256]{2,1,0:T(8,128)(2,1)} %get-tuple-element.150), channel_id=1, source_target_pairs={{0,24},{1,25},{2,26},{3,27},{4,28},{5,29},{6,30},{7,31},{8,16},{9,... | collective-permute-start | bytes 1179656 | tf_op jit(solution)/shard_map/ppermute | solution.py:280
  780.8 79.3 %collective-permute-start.136 = (bf16[6,128,256]{2,1,0:T(8,128)(2,1)}, bf16[6,128,256]{2,1,0:T(8,128)(2,1)}, u32[]{:S(2)}, u32[]{:S(2)}) collective-permute-start(bf16[6,128,256]{2,1,0:T(8,128)(2,1)} %get-tuple-element.151), channel_id=1, source_target_pairs={{0,28},{1,29},{2,30},{3,31},{4,24},{5,25},{6,26},{7,27},{8,20},{9,... | collective-permute-start | bytes 1179656 | tf_op jit(solution)/shard_map/ppermute | solution.py:280
  790.1 95.5 %collective-permute-start.127 = (bf16[6,128,256]{2,1,0:T(8,128)(2,1)}, bf16[6,128,256]{2,1,0:T(8,128)(2,1)S(1)}, u32[]{:S(2)}, u32[]{:S(2)}) collective-permute-start(bf16[6,128,256]{2,1,0:T(8,128)(2,1)} %get-tuple-element.142), channel_id=1, source_target_pairs={{0,20},{1,21},{2,22},{3,23},{4,16},{5,17},{6,18},{7,19},{8,28},{9,... | collective-permute-start | bytes 1179656 | tf_op jit(solution)/shard_map/ppermute | solution.py:280
  793.5 92.1 %collective-permute-start.128 = (bf16[6,128,256]{2,1,0:T(8,128)(2,1)}, bf16[6,128,256]{2,1,0:T(8,128)(2,1)S(1)}, u32[]{:S(2)}, u32[]{:S(2)}) collective-permute-start(bf16[6,128,256]{2,1,0:T(8,128)(2,1)} %get-tuple-element.143), channel_id=1, source_target_pairs={{0,24},{1,25},{2,26},{3,27},{4,28},{5,29},{6,30},{7,31},{8,16},{9,... | collective-permute-start | bytes 1179656 | tf_op jit(solution)/shard_map/ppermute | solution.py:280
  832.6 53.0 %collective-permute-start.129 = (bf16[6,128,256]{2,1,0:T(8,128)(2,1)}, bf16[6,128,256]{2,1,0:T(8,128)(2,1)S(1)}, u32[]{:S(2)}, u32[]{:S(2)}) collective-permute-start(bf16[6,128,256]{2,1,0:T(8,128)(2,1)} %get-tuple-element.144), channel_id=1, source_target_pairs={{0,28},{1,29},{2,30},{3,31},{4,24},{5,25},{6,26},{7,27},{8,20},{9,... | collective-permute-start | bytes 1179656 | tf_op jit(solution)/shard_map/ppermute | solution.py:280
  850.8 54.8 %collective-permute-start.120 = (bf16[64,2048]{1,0:T(8,128)(2,1)}, bf16[64,2048]{1,0:T(8,128)(2,1)S(1)}, u32[]{:S(2)}, u32[]{:S(2)}) collective-permute-start(bf16[64,2048]{1,0:T(8,128)(2,1)} %get-tuple-element.161), channel_id=1, source_target_pairs={{0,2},{1,3},{2,0},{3,1},{4,6},{5,7},{6,4},{7,5},{8,10},{9,11},{10,... | collective-permute-start | bytes 786440 | tf_op jit(solution)/shard_map/ppermute | solution.py:280
  860.1 47.6 %collective-permute-start.121 = (bf16[64,2048]{1,0:T(8,128)(2,1)}, bf16[64,2048]{1,0:T(8,128)(2,1)S(1)}, u32[]{:S(2)}, u32[]{:S(2)}) collective-permute-start(bf16[64,2048]{1,0:T(8,128)(2,1)} %get-tuple-element.161), channel_id=1, source_target_pairs={{0,1},{1,0},{2,3},{3,2},{4,5},{5,4},{6,7},{7,6},{8,9},{9,8},{10,11... | collective-permute-start | bytes 786440 | tf_op jit(solution)/shard_map/ppermute | solution.py:280
  (195 other events, 3054.0 us)

commit v2 on v1

--- a/solution.py
+++ b/solution.py
@@ -689,13 +689,29 @@
     )(lane_starts, used, *state, *pieces, *done)
 
 
-def gather_rows(piece):
+def stack_rows(blocks):
+    rows, width = blocks[0].shape
+
+    def body(*refs):
+        for n, ref in enumerate(refs[:-1]):
+            refs[-1][n * rows : (n + 1) * rows] = ref[...]
+
+    return pl.pallas_call(
+        body,
+        in_specs=[VMEM_SPEC] * len(blocks),
+        out_specs=VMEM_SPEC,
+        out_shape=jax.ShapeDtypeStruct((len(blocks) * rows, width), LOW),
+        name="stack_rows",
+    )(*blocks)
+
+
+def gather_rows(piece, stack=stack_rows):
     near = [piece] + [swap(piece, 2 * k, 0) for k in (1, 2, 3)]
     blocks = []
     for part in near:
         pair = jnp.concatenate([part, swap(part, 0, 2)])
         blocks += [pair, swap(pair, 0, 1)]
-    return jnp.concatenate(blocks)
+    return stack(blocks)
 
 
 def scatter_sum(partial_sum):
@@ -719,7 +735,8 @@
     rows = piece.shape[0]
     out = jnp.zeros((4 * rows,) + piece.shape[1:], piece.dtype)
     over_y = swap(piece, 0, 2)
-    for bits, part in ((0, piece), (2, over_y), (1, swap(piece, 0, 1)), (3, swap(over_y, 0, 1))):
+    over_core, over_both = swap(piece, 0, 1), swap(over_y, 0, 1)
+    for bits, part in ((0, piece), (2, over_y), (1, over_core), (3, over_both)):
         out = lax.dynamic_update_slice(out, part, ((wt_index ^ bits) * rows, 0))
     return out
 
@@ -762,14 +779,14 @@
     inputs = lax.dynamic_slice(tokens, (wt * rows, 0), (rows, width)).astype(F32)
     normed, norm_back = jax.vjp(layer_norm, inputs)
     normed_cut = to_cut_order(normed.astype(LOW))
-    normed_all = gather_rows(normed_cut)
+    normed_all = gather_rows(normed_cut, jnp.concatenate)
     cut = lane_split(master, after(lane_starts, normed_cut))
     came = [cut[0]] + [swap(cut[k], k, 0) for k in range(1, 8)]
-    out_grad_low = lax.dynamic_slice(cotangent, (wt * rows, 0), (rows, width))
-    grad_all = gather_rows(out_grad_low)
     came[7], normed_all = lax.optimization_barrier((came[7], normed_all))
     w_qkv = pick_qkv(came, owner_bits[:12], slot_in_owner[:12])
     w_qkv_pair = swap(w_qkv, 1, 0)
+    out_grad_low = lax.dynamic_slice(after(cotangent, w_qkv), (wt * rows, 0), (rows, width))
+    grad_all = gather_rows(out_grad_low)
     wanted = jnp.concatenate(
         [
             jnp.arange(16, 48, dtype=jnp.int32),
@@ -884,18 +901,21 @@
     )
     one_grad = from_cut_order(scatter_sum(one_part.astype(LOW))[0])
     input_grad = resid_grad + norm_back(one_grad)[0]
-    input_grad = share_rows(input_grad.astype(LOW), wt).astype(F32)
+    input_grad = share_rows(input_grad.astype(LOW), wt)
+    input_grad = input_grad.astype(F32)
 
     slot_range = jnp.arange(cap, dtype=jnp.int32) + ctx * cap
     used = jnp.any(
         (owner_col * cap + slot_in_owner)[None, :] == slot_range[:, None], axis=1
     ).astype(jnp.int32)
-    state, done = (master, moment_one, moment_two), ()
-    for part in range(2):
-        mine = sends[8 * part : 8 * part + 8]
-        pieces = [mine[0]] + [swap(mine[k], k, 0) for k in range(1, 8)]
-        done = tuple(update(state, pieces, lane_starts, used, part * part_slots, done))
-    return (output, input_grad) + done
+    state = (master, moment_one, moment_two)
+    first, second = [sends[0]], [sends[8]]
+    first += [swap(sends[k], k, 0) for k in range(1, 8)]
+    for k in range(1, 8):
+        second.append(swap(after(sends[8 + k], first[k]), k, 0))
+    done = update(state, first, lane_starts, used, 0, ())
+    done = update(state, second, lane_starts, used, part_slots, tuple(done))
+    return (output, input_grad) + tuple(done)
 
 
 def choose_shards(*args):

time: 922 us -> 964 us (1.046)
  the two profiles are of different devices: /device:TPU:9 before, /device:TPU:0 now
where the time goes in v2:
time: 964 us; the launch traced here: 952 us
  waiting for transfers between devices  472 us (49%)
  starting transfers between devices  184 us (19%)
  Pallas kernels  119 us (12%)
  local copies, waits for them, and re-layouts  61.9 us (6%)
  matrix products  57.4 us (6%)
  other arithmetic  54.2 us (6%)
    ppermute x137, waiting for transfers between devices, swap(): return lax.ppermute(value, AXES, pairs)  472 us
    ppermute x137, starting transfers between devices, swap(): return lax.ppermute(value, AXES, pairs)  184 us
    pallas_call x2, Pallas kernels, update(): pl.pallas_call(body, grid_spec=pltpu.PrefetchScalarGridSpec(num_scalar_pr...  37.8 us
    dot_general x5, matrix products, dot_tn(): lax.dot_general(left, right, (((0,), (0,)), ((), ())), preferred_element_...  23.3 us
  transfers between devices with their start and end apart: 137, of which 45 were waited for; matrix products, arithmetic and copies ran while one was open for 13% of the time, Pallas kernels for 12%

profile of v2, /device:TPU:0, one launch (start us, length us, event | category | flops | bytes accessed | tf_op | source)
XLA Modules:
  0.0 951.5 jit_solution(3552985917588598416)
XLA Ops:
  12.9 12.4 %lane_split.1 = (bf16[12,128,256]{2,1,0:T(8,128)(2,1)}, bf16[12,128,256]{2,1,0:T(8,128)(2,1)}, bf16[12,128,256]{2,1,0:T(8,128)(2,1)}, bf16[12,128,256]{2,1,0:T(8...) custom-call(s32[16]{0:T(128)} %mul.265.starts, ...), custom_call_target="tpu_custom_call" | custom-call | tf_op jit(solution)/shard_map/lane_split/pallas_call | solution.py:307
  31.3 41.1 %collective-permute-done.6 = bf16[64,2048]{0,1:T(8,128)(2,1)S(1)} collective-permute-done((bf16[64,2048]{0,1:T(8,128)(2,1)S(1)}, bf16[64,2048]{0,1:T(8,128)(2,1)S(1)}, u32[]{:S(2)}, u32[]{:S(2)}) %collective-permute-start.6) | collective-permute-done | bytes 262176 | tf_op jit(solution)/shard_map/ppermute | solution.py:280
  78.8 9.9 %collective-permute-done.7 = bf16[64,2048]{0,1:T(8,128)(2,1)S(1)} collective-permute-done((bf16[64,2048]{0,1:T(8,128)(2,1)S(1)}, bf16[64,2048]{0,1:T(8,128)(2,1)S(1)}, u32[]{:S(2)}, u32[]{:S(2)}) %collective-permute-start.7) | collective-permute-done | bytes 262176 | tf_op jit(solution)/shard_map/ppermute | solution.py:280
  89.0 7.9 collective-permute-done.4
  99.0 7.6 collective-permute-start.14
  112.8 8.8 concatenate.99
  121.6 24.2 %collective-permute-done.13.refs_2_ = bf16[12,128,256]{2,1,0:T(8,128)(2,1)S(1)} collective-permute-done((bf16[12,128,256]{2,1,0:T(8,128)(2,1)}, bf16[12,128,256]{2,1,0:T(8,128)(2,1)S(1)}, u32[]{:S(2)}, u32[]{:S(2)}) %collective-permute-start.13) | collective-permute-done | bytes 786464 | tf_op jit(solution)/shard_map/ppermute | solution.py:280
  145.9 16.2 %collective-permute-done.14.refs_3_ = bf16[12,128,256]{2,1,0:T(8,128)(2,1)} collective-permute-done((bf16[12,128,256]{2,1,0:T(8,128)(2,1)}, bf16[12,128,256]{2,1,0:T(8,128)(2,1)}, u32[]{:S(2)}, u32[]{:S(2)}) %collective-permute-start.14) | collective-permute-done | bytes 786464 | tf_op jit(solution)/shard_map/ppermute | solution.py:280
  162.0 34.1 %collective-permute-done.16.refs_5_ = bf16[12,128,256]{2,1,0:T(8,128)(2,1)} collective-permute-done((bf16[12,128,256]{2,1,0:T(8,128)(2,1)}, bf16[12,128,256]{2,1,0:T(8,128)(2,1)}, u32[]{:S(2)}, u32[]{:S(2)}) %collective-permute-start.16) | collective-permute-done | bytes 786464 | tf_op jit(solution)/shard_map/ppermute | solution.py:280
  210.9 15.3 %collective-permute-start.20 = (bf16[1,128,256]{2,1,0:T(8,128)(2,1)}, bf16[1,128,256]{2,1,0:T(8,128)(2,1)S(1)}, u32[]{:S(2)}, u32[]{:S(2)}) collective-permute-start(bf16[1,128,256]{2,1,0:T(8,128)(2,1)} %get-tuple-element.105), channel_id=1, source_target_pairs={{0,8},{1,9},{2,10},{3,11},{4,12},{5,13},{6,14},{7,15},{8,0},{9,1},... | collective-permute-start | bytes 196616 | tf_op jit(solution)/shard_map/ppermute | solution.py:280
  257.5 8.3 attend.1
  276.1 11.2 %collective-permute-done.52 = bf16[64,2048]{1,0:T(8,128)(2,1)S(1)} collective-permute-done((bf16[64,2048]{1,0:T(8,128)(2,1)S(1)}, bf16[64,2048]{1,0:T(8,128)(2,1)S(1)}, u32[]{:S(2)}, u32[]{:S(2)}) %collective-permute-start.52) | collective-permute-done | bytes 262176 | tf_op jit(solution)/shard_map/ppermute | solution.py:280
  336.4 10.9 %collective-permute-done.31 = bf16[64,2048]{1,0:T(8,128)(2,1)S(1)} collective-permute-done((bf16[64,2048]{1,0:T(8,128)(2,1)S(1)}, bf16[64,2048]{1,0:T(8,128)(2,1)S(1)}, u32[]{:S(2)}, u32[]{:S(2)}) %collective-permute-start.31) | collective-permute-done | bytes 262176 | tf_op jit(solution)/shard_map/ppermute | solution.py:280
  360.5 10.5 %collective-permute-done.40 = bf16[64,2048]{1,0:T(8,128)(2,1)S(1)} collective-permute-done((bf16[64,2048]{1,0:T(8,128)(2,1)S(1)}, bf16[64,2048]{1,0:T(8,128)(2,1)S(1)}, u32[]{:S(2)}, u32[]{:S(2)}) %collective-permute-start.40) | collective-permute-done | bytes 262176 | tf_op jit(solution)/shard_map/ppermute | solution.py:280
  376.1 13.5 %collective-permute-done.44 = bf16[64,2048]{1,0:T(8,128)(2,1)S(1)} collective-permute-done((bf16[64,2048]{1,0:T(8,128)(2,1)S(1)}, bf16[64,2048]{1,0:T(8,128)(2,1)S(1)}, u32[]{:S(2)}, u32[]{:S(2)}) %collective-permute-start.44) | collective-permute-done | bytes 262176 | tf_op jit(solution)/shard_map/ppermute | solution.py:280
  393.1 25.3 %collective-permute-done.61.other_ref = bf16[4,4,128,256]{3,2,1,0:T(8,128)(2,1)S(1)} collective-permute-done((bf16[4,4,128,256]{3,2,1,0:T(8,128)(2,1)S(1)}, bf16[4,4,128,256]{3,2,1,0:T(8,128)(2,1)S(1)}, u32[]{:S(2)}, u32[]{:S(2)}) %collective-permute-start.61) | collective-permute-done | bytes 1048608 | tf_op jit(solution)/shard_map/ppermute | solution.py:280
  439.5 7.9 fusion.45
  498.6 7.0 fusion.127
  531.6 12.1 %collective-permute-done.89 = bf16[64,2048]{1,0:T(8,128)(2,1)S(1)} collective-permute-done((bf16[64,2048]{1,0:T(8,128)(2,1)S(1)}, bf16[64,2048]{1,0:T(8,128)(2,1)S(1)}, u32[]{:S(2)}, u32[]{:S(2)}) %collective-permute-start.89) | collective-permute-done | bytes 262176 | tf_op jit(solution)/shard_map/ppermute | solution.py:280
  552.3 7.0 collective-permute-done.96
  569.8 18.1 %collective-permute-done.105 = bf16[4,4,128,256]{3,2,1,0:T(8,128)(2,1)S(1)} collective-permute-done((bf16[4,4,128,256]{3,2,1,0:T(8,128)(2,1)S(1)}, bf16[4,4,128,256]{3,2,1,0:T(8,128)(2,1)S(1)}, u32[]{:S(2)}, u32[]{:S(2)}) %collective-permute-start.105) | collective-permute-done | bytes 1048608 | tf_op jit(solution)/shard_map/ppermute | solution.py:280
  605.4 11.7 %attend_back.1 = (f32[1024,128]{1,0:T(8,128)}, f32[1024,256]{1,0:T(8,128)}, bf16[1024,256]{1,0:T(8,128)(2,1)}) custom-call(bf16[1024,128]{1,0:T(8,128)(2,1)} %pad_maximum_fusion.16.q, bf16[1024,256]{1,0:T(8,128)(2,1)} %copy-done.3, bf16[1024,256]{1,0:T(8,128)(2,1)} %copy-done.30, bf16[1024,128]{1,0:T(8,128)(2,1)} %convolution_convert_fusion.5.do, ...), custom_call_target="tpu_custom_call" | custom-call | tf_op jit(solution)/shard_map/attend_back/pallas_call | solution.py:634
  627.7 17.4 %collective-permute-done.98 = bf16[1024,256]{1,0:T(8,128)(2,1)S(1)} collective-permute-done((bf16[1024,256]{1,0:T(8,128)(2,1)}, bf16[1024,256]{1,0:T(8,128)(2,1)S(1)}, u32[]{:S(2)}, u32[]{:S(2)}) %collective-permute-start.98) | collective-permute-done | bytes 524320 | tf_op jit(solution)/shard_map/ppermute | solution.py:280
  706.9 13.5 %collective-permute-done.80 = bf16[64,2048]{1,0:T(8,128)(2,1)S(1)} collective-permute-done((bf16[64,2048]{1,0:T(8,128)(2,1)S(1)}, bf16[64,2048]{1,0:T(8,128)(2,1)S(1)}, u32[]{:S(2)}, u32[]{:S(2)}) %collective-permute-start.80) | collective-permute-done | bytes 262176 | tf_op jit(solution)/shard_map/ppermute | solution.py:280
  729.7 11.2 %collective-permute-done.115 = bf16[64,2048]{0,1:T(8,128)(2,1)S(1)} collective-permute-done((bf16[64,2048]{0,1:T(8,128)(2,1)S(1)}, bf16[64,2048]{0,1:T(8,128)(2,1)S(1)}, u32[]{:S(2)}, u32[]{:S(2)}) %collective-permute-start.115) | collective-permute-done | bytes 262176 | tf_op jit(solution)/shard_map/ppermute | solution.py:280
  756.6 29.9 %collective-permute-done.129.refs_4_ = bf16[6,128,256]{2,1,0:T(8,128)(2,1)S(1)} collective-permute-done((bf16[6,128,256]{2,1,0:T(8,128)(2,1)S(1)}, bf16[6,128,256]{2,1,0:T(8,128)(2,1)S(1)}, u32[]{:S(2)}, u32[]{:S(2)}) %collective-permute-start.129) | collective-permute-done | bytes 393248 | tf_op jit(solution)/shard_map/ppermute | solution.py:280
  787.3 7.5 collective-permute-done.131.refs_5_
  806.4 39.2 %collective-permute-done.116 = bf16[64,2048]{0,1:T(8,128)(2,1)} collective-permute-done((bf16[64,2048]{0,1:T(8,128)(2,1)}, bf16[64,2048]{0,1:T(8,128)(2,1)}, u32[]{:S(2)}, u32[]{:S(2)}) %collective-permute-start.116) | collective-permute-done | bytes 262176 | tf_op jit(solution)/shard_map/ppermute | solution.py:280
  845.6 11.4 %collective-permute-start.128 = (bf16[6,128,256]{2,1,0:T(8,128)(2,1)}, bf16[6,128,256]{2,1,0:T(8,128)(2,1)}, u32[]{:S(2)}, u32[]{:S(2)}) collective-permute-start(bf16[6,128,256]{2,1,0:T(8,128)(2,1)} %get-tuple-element.155), channel_id=1, source_target_pairs={{0,12},{1,13},{2,14},{3,15},{4,8},{5,9},{6,10},{7,11},{8,4},{9,5},... | collective-permute-start | bytes 1179656 | tf_op jit(solution)/shard_map/ppermute | solution.py:280
  873.7 33.7 %collective-permute-done.130.refs_4_ = bf16[6,128,256]{2,1,0:T(8,128)(2,1)S(1)} collective-permute-done((bf16[6,128,256]{2,1,0:T(8,128)(2,1)}, bf16[6,128,256]{2,1,0:T(8,128)(2,1)S(1)}, u32[]{:S(2)}, u32[]{:S(2)}) %collective-permute-start.130) | collective-permute-done | bytes 393248 | tf_op jit(solution)/shard_map/ppermute | solution.py:280
  909.3 18.9 %update.2 = (f32[12,128,2048]{2,1,0:T(8,128)}, f32[12,128,2048]{2,1,0:T(8,128)}, f32[12,128,2048]{2,1,0:T(8,128)}, bf16[12,128,2048]{2,1,0:T(8,128)(2,1)}) custom-call(s32[16]{0:T(128)} %mul.265.starts, s32[12]{0:T(128)} %convert_element_type.575.live, f32[12,128,2048]{2,1,0:T(8,128)} %mas.3, f32[12,128,2048]{2,1,0:T(8,128)} %one.3, f32[12,128,2048]{2,1,0:T(8,128)} %two.3, ...), custom_call_target="tpu_custom_call" | custom-call | tf_op jit(solution)/shard_map/update/pallas_call | solution.py:678
  929.2 18.9 %update.3 = (f32[12,128,2048]{2,1,0:T(8,128)}, f32[12,128,2048]{2,1,0:T(8,128)}, f32[12,128,2048]{2,1,0:T(8,128)}, bf16[12,128,2048]{2,1,0:T(8,128)(2,1)}) custom-call(s32[16]{0:T(128)} %mul.265.starts, s32[12]{0:T(128)} %convert_element_type.575.live, ...), custom_call_target="tpu_custom_call", output_to_operand_aliasing={{0}: (13, {}), {1}: (14, {}), {2}: (15, {}), {3}: (16, {})} | custom-call | tf_op jit(solution)/shard_map/update/pallas_call | solution.py:678
  (663 shorter events, 426.3 us)
Async XLA Ops:
  9.8 62.6 %collective-permute-start.6 = (bf16[64,2048]{0,1:T(8,128)(2,1)S(1)}, bf16[64,2048]{0,1:T(8,128)(2,1)S(1)}, u32[]{:S(2)}, u32[]{:S(2)}) collective-permute-start(bf16[64,2048]{0,1:T(8,128)(2,1)S(1)} %maximum_select_fusion.1), channel_id=1, source_target_pairs={{0,16},{1,17},{2,18},{3,19},{4,20},{5,21},{6,22},{7,23},{8,24},{9,... | collective-permute-start | bytes 786440 | tf_op jit(solution)/shard_map/ppermute | solution.py:280
  9.8 66.9 %collective-permute-start.3 = (bf16[64,2048]{0,1:T(8,128)(2,1)S(1)}, bf16[64,2048]{0,1:T(8,128)(2,1)}, u32[]{:S(2)}, u32[]{:S(2)}) collective-permute-start(bf16[64,2048]{0,1:T(8,128)(2,1)S(1)} %maximum_select_fusion.1), channel_id=1, source_target_pairs={{0,8},{1,9},{2,10},{3,11},{4,12},{5,13},{6,14},{7,15},{8,0},{9,1},... | collective-permute-start | bytes 786440 | tf_op jit(solution)/shard_map/ppermute | solution.py:280
  10.5 63.4 %collective-permute-start.1 = (bf16[64,2048]{0,1:T(8,128)(2,1)S(1)}, bf16[64,2048]{0,1:T(8,128)(2,1)}, u32[]{:S(2)}, u32[]{:S(2)}) collective-permute-start(bf16[64,2048]{0,1:T(8,128)(2,1)S(1)} %maximum_select_fusion.1), channel_id=1, source_target_pairs={{0,2},{1,3},{2,0},{3,1},{4,6},{5,7},{6,4},{7,5},{8,10},{9,11},{10,... | collective-permute-start | bytes 786440 | tf_op jit(solution)/shard_map/ppermute | solution.py:280
  25.2 73.6 %collective-permute-start = (bf16[12,128,256]{2,1,0:T(8,128)(2,1)}, bf16[12,128,256]{2,1,0:T(8,128)(2,1)S(1)}, u32[]{:S(2)}, u32[]{:S(2)}) collective-permute-start(bf16[12,128,256]{2,1,0:T(8,128)(2,1)} %get-tuple-element.92), channel_id=1, source_target_pairs={{0,28},{1,29},{2,30},{3,31},{4,24},{5,25},{6,26},{7,27},{8,20},{9,... | collective-permute-start | bytes 2359304 | tf_op jit(solution)/shard_map/ppermute | solution.py:280
  30.3 46.6 %collective-permute-start.10 = (bf16[64,2048]{0,1:T(8,128)(2,1)S(1)}, bf16[64,2048]{0,1:T(8,128)(2,1)}, u32[]{:S(2)}, u32[]{:S(2)}) collective-permute-start(bf16[64,2048]{0,1:T(8,128)(2,1)S(1)} %collective-permute-done.9), channel_id=1, source_target_pairs={{0,2},{1,3},{2,0},{3,1},{4,6},{5,7},{6,4},{7,5},{8,10},{9,11},{10,... | collective-permute-start | bytes 786440 | tf_op jit(solution)/shard_map/ppermute | solution.py:280
  98.9 46.9 %collective-permute-start.13 = (bf16[12,128,256]{2,1,0:T(8,128)(2,1)}, bf16[12,128,256]{2,1,0:T(8,128)(2,1)S(1)}, u32[]{:S(2)}, u32[]{:S(2)}) collective-permute-start(bf16[12,128,256]{2,1,0:T(8,128)(2,1)} %get-tuple-element.96), channel_id=1, source_target_pairs={{0,8},{1,9},{2,10},{3,11},{4,12},{5,13},{6,14},{7,15},{8,0},{9,1},... | collective-permute-start | bytes 2359304 | tf_op jit(solution)/shard_map/ppermute | solution.py:280
  99.0 63.0 %collective-permute-start.14 = (bf16[12,128,256]{2,1,0:T(8,128)(2,1)}, bf16[12,128,256]{2,1,0:T(8,128)(2,1)}, u32[]{:S(2)}, u32[]{:S(2)}) collective-permute-start(bf16[12,128,256]{2,1,0:T(8,128)(2,1)} %get-tuple-element.97), channel_id=1, source_target_pairs={{0,12},{1,13},{2,14},{3,15},{4,8},{5,9},{6,10},{7,11},{8,4},{9,5},... | collective-permute-start | bytes 2359304 | tf_op jit(solution)/shard_map/ppermute | solution.py:280
  106.6 55.4 %collective-permute-start.15 = (bf16[12,128,256]{2,1,0:T(8,128)(2,1)}, bf16[12,128,256]{2,1,0:T(8,128)(2,1)}, u32[]{:S(2)}, u32[]{:S(2)}) collective-permute-start(bf16[12,128,256]{2,1,0:T(8,128)(2,1)} %get-tuple-element.98), channel_id=1, source_target_pairs={{0,16},{1,17},{2,18},{3,19},{4,20},{5,21},{6,22},{7,23},{8,24},{9,... | collective-permute-start | bytes 2359304 | tf_op jit(solution)/shard_map/ppermute | solution.py:280
  106.7 89.4 %collective-permute-start.16 = (bf16[12,128,256]{2,1,0:T(8,128)(2,1)}, bf16[12,128,256]{2,1,0:T(8,128)(2,1)}, u32[]{:S(2)}, u32[]{:S(2)}) collective-permute-start(bf16[12,128,256]{2,1,0:T(8,128)(2,1)} %get-tuple-element.99), channel_id=1, source_target_pairs={{0,20},{1,21},{2,22},{3,23},{4,16},{5,17},{6,18},{7,19},{8,28},{9,... | collective-permute-start | bytes 2359304 | tf_op jit(solution)/shard_map/ppermute | solution.py:280
  110.0 86.1 %collective-permute-start.17 = (bf16[12,128,256]{2,1,0:T(8,128)(2,1)}, bf16[12,128,256]{2,1,0:T(8,128)(2,1)}, u32[]{:S(2)}, u32[]{:S(2)}) collective-permute-start(bf16[12,128,256]{2,1,0:T(8,128)(2,1)} %get-tuple-element.100), channel_id=1, source_target_pairs={{0,24},{1,25},{2,26},{3,27},{4,28},{5,29},{6,30},{7,31},{8,16},{9,... | collective-permute-start | bytes 2359304 | tf_op jit(solution)/shard_map/ppermute | solution.py:280
  348.4 83.5 %collective-permute-start.46 = (bf16[32,128,256]{2,1,0:T(8,128)(2,1)}, bf16[32,128,256]{2,1,0:T(8,128)(2,1)}, u32[]{:S(2)}, u32[]{:S(2)}) collective-permute-start(bf16[32,128,256]{2,1,0:T(8,128)(2,1)} %get-tuple-element.110), channel_id=1, source_target_pairs={{0,4},{1,5},{2,6},{3,7},{4,0},{5,1},{6,2},{7,3},{8,12},{9,13},{10,... | collective-permute-start | bytes 6291464 | tf_op jit(solution)/shard_map/ppermute | solution.py:280
  371.0 47.5 %collective-permute-start.61 = (bf16[4,4,128,256]{3,2,1,0:T(8,128)(2,1)S(1)}, bf16[4,4,128,256]{3,2,1,0:T(8,128)(2,1)S(1)}, u32[]{:S(2)}, u32[]{:S(2)}) collective-permute-start(bf16[4,4,128,256]{3,2,1,0:T(8,128)(2,1)S(1)} %pad_maximum_fusion.4.own_ref), channel_id=1, source_target_pairs={{0,4},{1,5},{2,6},{3,7},{4,0},{5,1},{6,2},{7,3},{8,12},{9,13},{10,... | collective-permute-start | bytes 3145736 | tf_op jit(solution)/shard_map/ppermute | solution.py:280
  391.5 43.5 %collective-permute-start.36 = (bf16[128,2048]{1,0:T(8,128)(2,1)S(1)}, bf16[128,2048]{1,0:T(8,128)(2,1)}, u32[]{:S(2)}, u32[]{:S(2)}) collective-permute-start(bf16[128,2048]{1,0:T(8,128)(2,1)S(1)} %pad_maximum_fusion.13.refs_0_), channel_id=1, source_target_pairs={{0,1},{1,0},{2,3},{3,2},{4,5},{5,4},{6,7},{7,6},{8,9},{9,8},{10,11... | collective-permute-start | bytes 1572872 | tf_op jit(solution)/shard_map/ppermute | solution.py:280
  587.9 71.6 %collective-permute-start.104 = (bf16[2048,512]{1,0:T(8,128)(2,1)}, bf16[2048,512]{1,0:T(8,128)(2,1)}, u32[]{:S(2)}, u32[]{:S(2)}) collective-permute-start(bf16[2048,512]{1,0:T(8,128)(2,1)} %slice.856), channel_id=1, source_target_pairs={{0,4},{1,5},{2,6},{3,7},{4,0},{5,1},{6,2},{7,3},{8,12},{9,13},{10,... | collective-permute-start | bytes 6291464 | tf_op jit(solution)/shard_map/ppermute | solution.py:280
  589.9 101.9 %collective-permute-start.79 = (bf16[64,2048]{1,0:T(8,128)(2,1)}, bf16[64,2048]{1,0:T(8,128)(2,1)}, u32[]{:S(2)}, u32[]{:S(2)}) collective-permute-start(bf16[64,2048]{1,0:T(8,128)(2,1)} %slice.863), channel_id=1, source_target_pairs={{0,2},{1,3},{2,0},{3,1},{4,6},{5,7},{6,4},{7,5},{8,10},{9,11},{10,... | collective-permute-start | bytes 786440 | tf_op jit(solution)/shard_map/ppermute | solution.py:280
  591.4 76.8 %collective-permute-start.108 = (bf16[4,128,256]{2,1,0:T(8,128)(2,1)}, bf16[4,128,256]{2,1,0:T(8,128)(2,1)}, u32[]{:S(2)}, u32[]{:S(2)}) collective-permute-start(bf16[4,128,256]{2,1,0:T(8,128)(2,1)} %get-tuple-element.227), channel_id=1, source_target_pairs={{0,24},{1,25},{2,26},{3,27},{4,28},{5,29},{6,30},{7,31},{8,16},{9,... | collective-permute-start | bytes 786440 | tf_op jit(solution)/shard_map/ppermute | solution.py:280
  593.8 74.8 %collective-permute-start.107 = (bf16[4,128,256]{2,1,0:T(8,128)(2,1)}, bf16[4,128,256]{2,1,0:T(8,128)(2,1)}, u32[]{:S(2)}, u32[]{:S(2)}) collective-permute-start(bf16[4,128,256]{2,1,0:T(8,128)(2,1)} %get-tuple-element.228), channel_id=1, source_target_pairs={{0,16},{1,17},{2,18},{3,19},{4,20},{5,21},{6,22},{7,23},{8,24},{9,... | collective-permute-start | bytes 786440 | tf_op jit(solution)/shard_map/ppermute | solution.py:280
  743.0 43.5 %collective-permute-start.129 = (bf16[6,128,256]{2,1,0:T(8,128)(2,1)S(1)}, bf16[6,128,256]{2,1,0:T(8,128)(2,1)S(1)}, u32[]{:S(2)}, u32[]{:S(2)}) collective-permute-start(bf16[6,128,256]{2,1,0:T(8,128)(2,1)S(1)} %copy-done.83), channel_id=1, source_target_pairs={{0,16},{1,17},{2,18},{3,19},{4,20},{5,21},{6,22},{7,23},{8,24},{9,... | collective-permute-start | bytes 1179656 | tf_op jit(solution)/shard_map/ppermute | solution.py:280
  743.2 51.6 %collective-permute-start.131 = (bf16[6,128,256]{2,1,0:T(8,128)(2,1)S(1)}, bf16[6,128,256]{2,1,0:T(8,128)(2,1)S(1)}, u32[]{:S(2)}, u32[]{:S(2)}) collective-permute-start(bf16[6,128,256]{2,1,0:T(8,128)(2,1)S(1)} %copy-done.84), channel_id=1, source_target_pairs={{0,20},{1,21},{2,22},{3,23},{4,16},{5,17},{6,18},{7,19},{8,28},{9,... | collective-permute-start | bytes 1179656 | tf_op jit(solution)/shard_map/ppermute | solution.py:280
  745.8 49.8 %collective-permute-start.133 = (bf16[6,128,256]{2,1,0:T(8,128)(2,1)S(1)}, bf16[6,128,256]{2,1,0:T(8,128)(2,1)}, u32[]{:S(2)}, u32[]{:S(2)}) collective-permute-start(bf16[6,128,256]{2,1,0:T(8,128)(2,1)S(1)} %copy-done.85), channel_id=1, source_target_pairs={{0,24},{1,25},{2,26},{3,27},{4,28},{5,29},{6,30},{7,31},{8,16},{9,... | collective-permute-start | bytes 1179656 | tf_op jit(solution)/shard_map/ppermute | solution.py:280
  752.8 47.3 %collective-permute-start.135 = (bf16[6,128,256]{2,1,0:T(8,128)(2,1)}, bf16[6,128,256]{2,1,0:T(8,128)(2,1)}, u32[]{:S(2)}, u32[]{:S(2)}) collective-permute-start(bf16[6,128,256]{2,1,0:T(8,128)(2,1)} %get-tuple-element.166), channel_id=1, source_target_pairs={{0,28},{1,29},{2,30},{3,31},{4,24},{5,25},{6,26},{7,27},{8,20},{9,... | collective-permute-start | bytes 1179656 | tf_op jit(solution)/shard_map/ppermute | solution.py:280
  756.2 43.9 %collective-permute-start.110 = (bf16[64,2048]{0,1:T(8,128)(2,1)S(1)}, bf16[64,2048]{0,1:T(8,128)(2,1)}, u32[]{:S(2)}, u32[]{:S(2)}) collective-permute-start(bf16[64,2048]{0,1:T(8,128)(2,1)S(1)} %slice.860), channel_id=1, source_target_pairs={{0,2},{1,3},{2,0},{3,1},{4,6},{5,7},{6,4},{7,5},{8,10},{9,11},{10,... | collective-permute-start | bytes 786440 | tf_op jit(solution)/shard_map/ppermute | solution.py:280
  795.5 50.1 %collective-permute-start.116 = (bf16[64,2048]{0,1:T(8,128)(2,1)}, bf16[64,2048]{0,1:T(8,128)(2,1)}, u32[]{:S(2)}, u32[]{:S(2)}) collective-permute-start(bf16[64,2048]{0,1:T(8,128)(2,1)} %fusion.19), channel_id=1, source_target_pairs={{0,16},{1,17},{2,18},{3,19},{4,20},{5,21},{6,22},{7,23},{8,24},{9,... | collective-permute-start | bytes 786440 | tf_op jit(solution)/shard_map/ppermute | solution.py:280
  795.5 50.1 %collective-permute-start.113 = (bf16[64,2048]{0,1:T(8,128)(2,1)}, bf16[64,2048]{0,1:T(8,128)(2,1)}, u32[]{:S(2)}, u32[]{:S(2)}) collective-permute-start(bf16[64,2048]{0,1:T(8,128)(2,1)} %fusion.20), channel_id=1, source_target_pairs={{0,24},{1,25},{2,26},{3,27},{4,28},{5,29},{6,30},{7,31},{8,16},{9,... | collective-permute-start | bytes 786440 | tf_op jit(solution)/shard_map/ppermute | solution.py:280
  800.1 60.5 %collective-permute-start.85 = (bf16[64,2048]{1,0:T(8,128)(2,1)}, bf16[64,2048]{1,0:T(8,128)(2,1)}, u32[]{:S(2)}, u32[]{:S(2)}) collective-permute-start(bf16[64,2048]{1,0:T(8,128)(2,1)} %copy-done.95), channel_id=1, source_target_pairs={{0,1},{1,0},{2,3},{3,2},{4,5},{5,4},{6,7},{7,6},{8,9},{9,8},{10,11... | collective-permute-start | bytes 786440 | tf_op jit(solution)/shard_map/ppermute | solution.py:280
  800.1 62.6 %collective-permute-start.86 = (bf16[64,2048]{1,0:T(8,128)(2,1)}, bf16[64,2048]{1,0:T(8,128)(2,1)}, u32[]{:S(2)}, u32[]{:S(2)}) collective-permute-start(bf16[64,2048]{1,0:T(8,128)(2,1)} %copy-done.90), channel_id=1, source_target_pairs={{0,1},{1,0},{2,3},{3,2},{4,5},{5,4},{6,7},{7,6},{8,9},{9,8},{10,11... | collective-permute-start | bytes 786440 | tf_op jit(solution)/shard_map/ppermute | solution.py:280
  806.1 60.7 %collective-permute-start.124 = (bf16[6,128,256]{2,1,0:T(8,128)(2,1)}, bf16[6,128,256]{2,1,0:T(8,128)(2,1)}, u32[]{:S(2)}, u32[]{:S(2)}) collective-permute-start(bf16[6,128,256]{2,1,0:T(8,128)(2,1)} %get-tuple-element.149), channel_id=1, source_target_pairs={{0,4},{1,5},{2,6},{3,7},{4,0},{5,1},{6,2},{7,3},{8,12},{9,13},{10,... | collective-permute-start | bytes 1179656 | tf_op jit(solution)/shard_map/ppermute | solution.py:280
  860.6 46.9 %collective-permute-start.130 = (bf16[6,128,256]{2,1,0:T(8,128)(2,1)}, bf16[6,128,256]{2,1,0:T(8,128)(2,1)S(1)}, u32[]{:S(2)}, u32[]{:S(2)}) collective-permute-start(bf16[6,128,256]{2,1,0:T(8,128)(2,1)} %get-tuple-element.158), channel_id=1, source_target_pairs={{0,16},{1,17},{2,18},{3,19},{4,20},{5,21},{6,22},{7,23},{8,24},{9,... | collective-permute-start | bytes 1179656 | tf_op jit(solution)/shard_map/ppermute | solution.py:280
  862.7 65.4 %collective-permute-start.132 = (bf16[6,128,256]{2,1,0:T(8,128)(2,1)}, bf16[6,128,256]{2,1,0:T(8,128)(2,1)S(1)}, u32[]{:S(2)}, u32[]{:S(2)}) collective-permute-start(bf16[6,128,256]{2,1,0:T(8,128)(2,1)} %get-tuple-element.161), channel_id=1, source_target_pairs={{0,20},{1,21},{2,22},{3,23},{4,16},{5,17},{6,18},{7,19},{8,28},{9,... | collective-permute-start | bytes 1179656 | tf_op jit(solution)/shard_map/ppermute | solution.py:280
  866.8 61.4 %collective-permute-start.134 = (bf16[6,128,256]{2,1,0:T(8,128)(2,1)}, bf16[6,128,256]{2,1,0:T(8,128)(2,1)S(1)}, u32[]{:S(2)}, u32[]{:S(2)}) collective-permute-start(bf16[6,128,256]{2,1,0:T(8,128)(2,1)} %get-tuple-element.164), channel_id=1, source_target_pairs={{0,24},{1,25},{2,26},{3,27},{4,28},{5,29},{6,30},{7,31},{8,16},{9,... | collective-permute-start | bytes 1179656 | tf_op jit(solution)/shard_map/ppermute | solution.py:280
  868.0 60.2 %collective-permute-start.136 = (bf16[6,128,256]{2,1,0:T(8,128)(2,1)}, bf16[6,128,256]{2,1,0:T(8,128)(2,1)S(1)}, u32[]{:S(2)}, u32[]{:S(2)}) collective-permute-start(bf16[6,128,256]{2,1,0:T(8,128)(2,1)} %get-tuple-element.167), channel_id=1, source_target_pairs={{0,28},{1,29},{2,30},{3,31},{4,24},{5,25},{6,26},{7,27},{8,20},{9,... | collective-permute-start | bytes 1179656 | tf_op jit(solution)/shard_map/ppermute | solution.py:280
  870.4 77.8 %collective-permute-start.120 = (bf16[64,2048]{1,0:T(8,128)(2,1)}, bf16[64,2048]{1,0:T(8,128)(2,1)S(1)}, u32[]{:S(2)}, u32[]{:S(2)}) collective-permute-start(bf16[64,2048]{1,0:T(8,128)(2,1)} %get-tuple-element.177), channel_id=1, source_target_pairs={{0,2},{1,3},{2,0},{3,1},{4,6},{5,7},{6,4},{7,5},{8,10},{9,11},{10,... | collective-permute-start | bytes 786440 | tf_op jit(solution)/shard_map/ppermute | solution.py:280
  (219 other events, 4142.3 us)

commit v3 on v2

--- a/solution.py
+++ b/solution.py
@@ -386,6 +386,25 @@
     return [sums[0]] + [swap(sums[m], 2 * m, 0) for m in (1, 2, 3)]
 
 
+def join_grads(query, kv, kv_back, cosine, sine):
+    def body(q, here, there, cos, sin, out):
+        def undo(values):
+            return values * cos[...] + pltpu.roll(values, 64, 1) * sin[...]
+
+        total = here[...] + there[...].astype(F32)
+        out[:, :128] = undo(q[...]).astype(LOW)
+        out[:, 128:256] = undo(total[:, :128]).astype(LOW)
+        out[:, 256:] = total[:, 128:].astype(LOW)
+
+    return pl.pallas_call(
+        body,
+        in_specs=[VMEM_SPEC] * 5,
+        out_specs=VMEM_SPEC,
+        out_shape=jax.ShapeDtypeStruct((query.shape[0], 384), LOW),
+        name="join_grads",
+    )(query, kv, kv_back, cosine, sine)
+
+
 VMEM_SPEC = pl.BlockSpec(memory_space=pltpu.VMEM)
 SMEM_SPEC = pl.BlockSpec(memory_space=pltpu.SMEM)
 ANY_SPEC = pl.BlockSpec(memory_space=pl.ANY)
@@ -472,7 +491,7 @@
             pltpu.make_async_copy(src, out.at[row[tile]], sem.at[tile]).start()
 
 
-def place_mlp(gate_up, downs, to, row, place, count, size):
+def place_mlp(gate_up, downs, to, row, place, sizes):
     def body(to_ref, row_ref, z_ref, gu_ref, *refs):
         down_refs, outs, sem = refs[:4], refs[4:-1], refs[-1]
         down_tile = lambda m, k: 48 + 4 * ((k + 2 * z_ref[1]) % 4) + (z_ref[0] ^ m)
@@ -502,8 +521,8 @@
     return pl.pallas_call(
         body,
         in_specs=[SMEM_SPEC] * 3 + [VMEM_SPEC] * 5,
-        out_specs=[ANY_SPEC] * count,
-        out_shape=[jax.ShapeDtypeStruct((size, 128, 256), LOW)] * count,
+        out_specs=[ANY_SPEC] * len(sizes),
+        out_shape=[jax.ShapeDtypeStruct((size, 128, 256), LOW) for size in sizes],
         scratch_shapes=[pltpu.SemaphoreType.DMA((64,))],
         name="place_mlp",
     )(to, row, place, gate_up, *downs)
@@ -705,13 +724,13 @@
     )(*blocks)
 
 
-def gather_rows(piece, stack=stack_rows):
+def gather_rows(piece):
     near = [piece] + [swap(piece, 2 * k, 0) for k in (1, 2, 3)]
     blocks = []
     for part in near:
         pair = jnp.concatenate([part, swap(part, 0, 2)])
         blocks += [pair, swap(pair, 0, 1)]
-    return stack(blocks)
+    return stack_rows(blocks)
 
 
 def scatter_sum(partial_sum):
@@ -776,16 +795,16 @@
         cut_vals = jnp.where(x_at == 0, values, flipped)
         return cut_vals.reshape(-1, 4, width // 4).transpose(0, 2, 1).reshape(-1, width)
 
-    inputs = lax.dynamic_slice(tokens, (wt * rows, 0), (rows, width)).astype(F32)
+    cut = lane_split(master, lane_starts)
+    came = [cut[0]] + [swap(cut[k], k, 0) for k in range(1, 8)]
+    tokens_later = after(tokens, cut[0])
+    inputs = lax.dynamic_slice(tokens_later, (wt * rows, 0), (rows, width)).astype(F32)
     normed, norm_back = jax.vjp(layer_norm, inputs)
     normed_cut = to_cut_order(normed.astype(LOW))
-    normed_all = gather_rows(normed_cut, jnp.concatenate)
-    cut = lane_split(master, after(lane_starts, normed_cut))
-    came = [cut[0]] + [swap(cut[k], k, 0) for k in range(1, 8)]
-    came[7], normed_all = lax.optimization_barrier((came[7], normed_all))
+    normed_all = gather_rows(after(normed_cut, came[4], came[5], came[6]))
     w_qkv = pick_qkv(came, owner_bits[:12], slot_in_owner[:12])
     w_qkv_pair = swap(w_qkv, 1, 0)
-    out_grad_low = lax.dynamic_slice(after(cotangent, w_qkv), (wt * rows, 0), (rows, width))
+    out_grad_low = lax.dynamic_slice(after(cotangent, w_qkv_pair), (wt * rows, 0), (rows, width))
     grad_all = gather_rows(out_grad_low)
     wanted = jnp.concatenate(
         [
@@ -795,8 +814,8 @@
         ]
     )
     wanted = after(wanted, w_qkv)
-    home_gu, *sends = row_gather(
-        came, owner_bits[wanted], slot_in_owner[wanted], [32] + [1] * 4 + [4] * 4
+    home_gate, home_up, *sends = row_gather(
+        came, owner_bits[wanted], slot_in_owner[wanted], [16, 16] + [1] * 4 + [4] * 4
     )
     out_came = [sends[0]] + [swap(sends[m], 2 * m, 0) for m in (1, 2, 3)]
     down_here = [sends[4]] + [swap(sends[4 + m], 2 * m, 0) for m in (1, 2, 3)]
@@ -830,12 +849,12 @@
     att_low, lse = attend(query, kv_here, kv_there, masks, 4)
     w_out = lane_join(out_here, out_there, lane_starts).reshape(tile_rows, width)
 
-    pair_gu = swap(after(home_gu, kv_there), 1, 0)
-    w_down = lane_join(down_here, swap(after(down_here, kv_there), 1, 0), lane_starts)
-    w_down = w_down.reshape(512, width)
+    gate_later, up_later = lax.optimization_barrier((home_gate, home_up, kv_there))[:2]
+    pair_gate, pair_up = swap(gate_later, 1, 0), swap(up_later, 1, 0)
+    down_there = swap(after(down_here, kv_there), 1, 0)
+    w_down = lane_join(down_here, down_there, lane_starts).reshape(512, width)
     w_gu = jnp.concatenate(
-        [part.reshape(width, 256) for half_gu in (home_gu, pair_gu) for part in (half_gu[:16], half_gu[16:])],
-        axis=1,
+        [part.reshape(width, 256) for part in (home_gate, home_up, pair_gate, pair_up)], axis=1
     )
     att_out, _ = scatter_sum(dot(att_low, w_out).astype(LOW))
     residual = inputs + att_out
@@ -858,21 +877,23 @@
     two_grad, begun = scatter_sum(dot_nt(grad_gu, w_gu).astype(LOW))
     hidden_later, grad_gu_later = lax.optimization_barrier((hidden, grad_gu, begun))[:2]
     grad_w_gu = dot_tn(two_all, grad_gu_later)
-    grad_w_down = dot_tn(hidden_later, grad_all)
     gu_back = swap(grad_w_gu[:, 512:].astype(LOW), 1, 0)
 
     resid_grad = out_grad_low.astype(F32) + norm_two_back(two_grad)[0]
     resid_all = gather_rows(resid_grad.astype(LOW))
+    grad_w_down = dot_tn(after(hidden_later, two_grad), grad_all)
     down, _ = scatter_sum(dot(after(hidden, two_grad), w_down).astype(LOW))
     output = share_rows((residual + down).astype(LOW), wt)
     gu_sum = (grad_w_gu[:, :512] + gu_back.astype(F32)).astype(LOW)
     down_came = return_halves(grad_w_down.reshape(4, tile_rows, width), lane_starts)
 
-    part_slots = cap // 2
+    part_slots = cap * 2 // 3
     send_to = owner_bits + 8 * (slot_in_owner // part_slots)
     send_row = slot_in_owner % part_slots
     place = jnp.stack([z_at, x_at])
-    sends = place_mlp(gu_sum, down_came, send_to, send_row, place, 16, part_slots)
+    sends = place_mlp(
+        gu_sum, down_came, send_to, send_row, place, [part_slots] * 8 + [cap - part_slots] * 8
+    )
 
     att_grad = dot_nt(resid_all, w_out).astype(LOW)
     out_grad_came = return_halves(
@@ -882,15 +903,13 @@
         query, kv_here, kv_there, att_grad, lse, masks, 4
     )
     kv_grad_back = swap(kv_grad_there, 1, 0)
-    kv_grad = kv_grad + kv_grad_back.astype(F32)
-    qkv_grad = jnp.concatenate(
-        [
-            rotate(query_grad, cosine, -sine),
-            rotate(kv_grad[:, :128], cosine, -sine),
-            kv_grad[:, 128:],
-        ],
-        axis=1,
-    ).astype(LOW)
+    qkv_grad = join_grads(
+        query_grad,
+        kv_grad,
+        kv_grad_back,
+        jnp.concatenate([cosine, cosine], axis=1),
+        jnp.concatenate([sine, -sine], axis=1),
+    )
     qkv_back = swap(dot_tn(normed_all[:, half:], qkv_grad).astype(LOW), 1, 0)
     qkv_sum = (dot_tn(normed_all[:, :half], qkv_grad) + qkv_back.astype(F32)).astype(LOW)
     sends = place_attention(sends, qkv_sum, out_grad_came, send_to, send_row, place)

time: 964 us -> 877 us (0.910)
  waiting for transfers between devices: 472 us -> 396 us
  local copies, waits for them, and re-layouts: 61.9 us -> 48.9 us
  other arithmetic: 54.2 us -> 43.4 us
    ppermute x137 -> x138, waiting for transfers between devices: 472 us -> 396 us  [swap(): return lax.ppermute(value, AXES, pairs)]
    concatenate x2 -> x0, local copies, waits for them, and re-layouts: 11 us -> none  [the longest x1 8.75 us: gather_rows(): return stack(blocks)]
    ppermute x137 -> x138, starting transfers between devices: 184 us -> 193 us  [swap(): return lax.ppermute(value, AXES, pairs)]
    unnamed x237 -> x216, local copies, waits for them, and re-layouts: 17.9 us -> 21.2 us
  transfers between devices with their start and end apart: 137 -> 138, of which waited for: 45 -> 45; matrix products, arithmetic and copies ran while one was open for 13% -> 12% of each run, Pallas kernels for 12% -> 13%
where the time goes in v3:
time: 877 us; the launch traced here: 868 us
  waiting for transfers between devices  396 us (45%)
  starting transfers between devices  193 us (22%)
  Pallas kernels  126 us (14%)
  matrix products  57.1 us (7%)
  local copies, waits for them, and re-layouts  48.9 us (6%)
  other arithmetic  43.4 us (5%)
    ppermute x138, waiting for transfers between devices, swap(): return lax.ppermute(value, AXES, pairs)  396 us
    ppermute x138, starting transfers between devices, swap(): return lax.ppermute(value, AXES, pairs)  193 us
    pallas_call x2, Pallas kernels, update(): pl.pallas_call(body, grid_spec=pltpu.PrefetchScalarGridSpec(num_scalar_pr...  37.8 us
    unnamed x216, local copies, waits for them, and re-layouts  21.2 us
    dot_general x5, matrix products, dot_nt(): lax.dot_general(left, right, (((1,), (1,)), ((), ())), preferred_element_...  20.9 us
    dot_general x5, matrix products, dot_tn(): lax.dot_general(left, right, (((0,), (0,)), ((), ())), preferred_element_...  18.8 us
    pallas_call x4, Pallas kernels, stack_rows(): pl.pallas_call(body, in_specs=[VMEM_SPEC] * len(blocks), out_specs=VMEM_S...  17.7 us
  transfers between devices with their start and end apart: 138, of which 45 were waited for; matrix products, arithmetic and copies ran while one was open for 12% of the time, Pallas kernels for 13%

profile of v3, /device:TPU:0, one launch (start us, length us, event | category | flops | bytes accessed | tf_op | source)
XLA Modules:
  0.0 867.9 jit_solution(5554639363260640942)
XLA Ops:
  1.3 12.4 %lane_split.1 = (bf16[12,128,256]{2,1,0:T(8,128)(2,1)}, bf16[12,128,256]{2,1,0:T(8,128)(2,1)}, bf16[12,128,256]{2,1,0:T(8,128)(2,1)}, bf16[12,128,256]{2,1,0:T(8...) custom-call(s32[16]{0:T(128)} %mul.238.starts, ...), custom_call_target="tpu_custom_call" | custom-call | tf_op jit(solution)/shard_map/lane_split/pallas_call | solution.py:307
  28.0 59.0 %collective-permute-done.refs_4_ = bf16[12,128,256]{2,1,0:T(8,128)(2,1)S(1)} collective-permute-done((bf16[12,128,256]{2,1,0:T(8,128)(2,1)}, bf16[12,128,256]{2,1,0:T(8,128)(2,1)S(1)}, u32[]{:S(2)}, u32[]{:S(2)}) %collective-permute-start) | collective-permute-done | bytes 786464 | tf_op jit(solution)/shard_map/ppermute | solution.py:280
  88.0 17.1 %collective-permute-done.1.refs_5_ = bf16[12,128,256]{2,1,0:T(8,128)(2,1)S(1)} collective-permute-done((bf16[12,128,256]{2,1,0:T(8,128)(2,1)}, bf16[12,128,256]{2,1,0:T(8,128)(2,1)S(1)}, u32[]{:S(2)}, u32[]{:S(2)}) %collective-permute-start.1) | collective-permute-done | bytes 786464 | tf_op jit(solution)/shard_map/ppermute | solution.py:280
  113.1 36.7 %collective-permute-start.5 = (bf16[64,2048]{1,0:T(8,128)(2,1)S(1)}, bf16[64,2048]{1,0:T(8,128)(2,1)S(1)}, u32[]{:S(2)}, u32[]{:S(2)}) collective-permute-start(bf16[64,2048]{1,0:T(8,128)(2,1)S(1)} %maximum_select_fusion.1), channel_id=1, source_target_pairs={{0,8},{1,9},{2,10},{3,11},{4,12},{5,13},{6,14},{7,15},{8,0},{9,1},... | collective-permute-start | bytes 786440 | tf_op jit(solution)/shard_map/ppermute | solution.py:280
  160.6 15.6 %collective-permute-done.8 = bf16[64,2048]{1,0:T(8,128)(2,1)} collective-permute-done((bf16[64,2048]{1,0:T(8,128)(2,1)S(1)}, bf16[64,2048]{1,0:T(8,128)(2,1)}, u32[]{:S(2)}, u32[]{:S(2)}) %collective-permute-start.8) | collective-permute-done | bytes 262176 | tf_op jit(solution)/shard_map/ppermute | solution.py:280
  193.5 10.8 %collective-permute-start.20 = (bf16[1,128,256]{2,1,0:T(8,128)(2,1)}, bf16[1,128,256]{2,1,0:T(8,128)(2,1)S(1)}, u32[]{:S(2)}, u32[]{:S(2)}) collective-permute-start(bf16[1,128,256]{2,1,0:T(8,128)(2,1)} %get-tuple-element.106), channel_id=1, source_target_pairs={{0,8},{1,9},{2,10},{3,11},{4,12},{5,13},{6,14},{7,15},{8,0},{9,1},... | collective-permute-start | bytes 196616 | tf_op jit(solution)/shard_map/ppermute | solution.py:280
  227.9 10.8 %collective-permute-done.23.other_ref = bf16[4,1,128,256]{3,2,1,0:T(8,128)(2,1)S(1)} collective-permute-done((bf16[4,1,128,256]{3,2,1,0:T(8,128)(2,1)S(1)}, bf16[4,1,128,256]{3,2,1,0:T(8,128)(2,1)S(1)}, u32[]{:S(2)}, u32[]{:S(2)}) %collective-permute-start.23) | collective-permute-done | bytes 262176 | tf_op jit(solution)/shard_map/ppermute | solution.py:280
  242.8 8.1 attend.1
  259.3 6.6 collective-permute-done.56
  275.9 7.2 collective-permute-done.50
  285.4 6.4 collective-permute-done.27
  309.5 10.0 %collective-permute-done.31 = bf16[64,2048]{1,0:T(8,128)(2,1)S(1)} collective-permute-done((bf16[64,2048]{1,0:T(8,128)(2,1)S(1)}, bf16[64,2048]{1,0:T(8,128)(2,1)S(1)}, u32[]{:S(2)}, u32[]{:S(2)}) %collective-permute-start.31) | collective-permute-done | bytes 262176 | tf_op jit(solution)/shard_map/ppermute | solution.py:280
  326.0 7.0 collective-permute-done.37
  334.7 7.0 collective-permute-done.40
  347.8 15.9 %collective-permute-done.44 = bf16[64,2048]{1,0:T(8,128)(2,1)S(1)} collective-permute-done((bf16[64,2048]{1,0:T(8,128)(2,1)S(1)}, bf16[64,2048]{1,0:T(8,128)(2,1)S(1)}, u32[]{:S(2)}, u32[]{:S(2)}) %collective-permute-start.44) | collective-permute-done | bytes 262176 | tf_op jit(solution)/shard_map/ppermute | solution.py:280
  383.8 7.3 collective-permute-done.46
  391.0 22.0 %collective-permute-done.47 = bf16[16,128,256]{2,1,0:T(8,128)(2,1)} collective-permute-done((bf16[16,128,256]{2,1,0:T(8,128)(2,1)}, bf16[16,128,256]{2,1,0:T(8,128)(2,1)}, u32[]{:S(2)}, u32[]{:S(2)}) %collective-permute-start.47) | collective-permute-done | bytes 1048608 | tf_op jit(solution)/shard_map/ppermute | solution.py:280
  413.0 8.2 fusion.31
  428.4 7.4 convolution_convert_fusion.2
  514.6 10.1 %collective-permute-done.91 = bf16[64,2048]{1,0:T(8,128)(2,1)S(1)} collective-permute-done((bf16[64,2048]{1,0:T(8,128)(2,1)}, bf16[64,2048]{1,0:T(8,128)(2,1)S(1)}, u32[]{:S(2)}, u32[]{:S(2)}) %collective-permute-start.91) | collective-permute-done | bytes 262176 | tf_op jit(solution)/shard_map/ppermute | solution.py:280
  526.8 7.0 collective-permute-done.94
  553.3 11.7 %attend_back.1 = (f32[1024,128]{1,0:T(8,128)}, f32[1024,256]{1,0:T(8,128)}, bf16[1024,256]{1,0:T(8,128)(2,1)}) custom-call(bf16[1024,128]{1,0:T(8,128)(2,1)} %pad_maximum_fusion.14.q, bf16[1024,256]{1,0:T(8,128)(2,1)} %copy-done.5, bf16[1024,256]{1,0:T(8,128)(2,1)} %copy-done.28, bf16[1024,128]{1,0:T(8,128)(2,1)} %convolution_convert_fusion.5.do, ...), custom_call_target="tpu_custom_call" | custom-call | tf_op jit(solution)/shard_map/attend_back/pallas_call | solution.py:653
  566.6 12.7 %collective-permute-done.106 = bf16[4,4,128,256]{3,2,1,0:T(8,128)(2,1)} collective-permute-done((bf16[4,4,128,256]{3,2,1,0:T(8,128)(2,1)}, bf16[4,4,128,256]{3,2,1,0:T(8,128)(2,1)}, u32[]{:S(2)}, u32[]{:S(2)}) %collective-permute-start.106) | collective-permute-done | bytes 1048608 | tf_op jit(solution)/shard_map/ppermute | solution.py:280
  612.9 6.2 place_mlp.1
  651.2 12.3 %collective-permute-done.81 = bf16[64,2048]{1,0:T(8,128)(2,1)S(1)} collective-permute-done((bf16[64,2048]{1,0:T(8,128)(2,1)S(1)}, bf16[64,2048]{1,0:T(8,128)(2,1)S(1)}, u32[]{:S(2)}, u32[]{:S(2)}) %collective-permute-start.81) | collective-permute-done | bytes 262176 | tf_op jit(solution)/shard_map/ppermute | solution.py:280
  669.1 5.7 collective-permute-done.85
  692.5 42.9 %collective-permute-done.130.refs_4_ = bf16[8,128,256]{2,1,0:T(8,128)(2,1)S(1)} collective-permute-done((bf16[8,128,256]{2,1,0:T(8,128)(2,1)S(1)}, bf16[8,128,256]{2,1,0:T(8,128)(2,1)S(1)}, u32[]{:S(2)}, u32[]{:S(2)}) %collective-permute-start.130) | collective-permute-done | bytes 524320 | tf_op jit(solution)/shard_map/ppermute | solution.py:280
  736.2 17.1 %collective-permute-done.132.refs_5_ = bf16[8,128,256]{2,1,0:T(8,128)(2,1)} collective-permute-done((bf16[8,128,256]{2,1,0:T(8,128)(2,1)S(1)}, bf16[8,128,256]{2,1,0:T(8,128)(2,1)}, u32[]{:S(2)}, u32[]{:S(2)}) %collective-permute-start.132) | collective-permute-done | bytes 524320 | tf_op jit(solution)/shard_map/ppermute | solution.py:280
  759.5 24.4 %collective-permute-done.117 = bf16[64,2048]{1,0:T(8,128)(2,1)} collective-permute-done((bf16[64,2048]{1,0:T(8,128)(2,1)}, bf16[64,2048]{1,0:T(8,128)(2,1)}, u32[]{:S(2)}, u32[]{:S(2)}) %collective-permute-start.117) | collective-permute-done | bytes 262176 | tf_op jit(solution)/shard_map/ppermute | solution.py:280
  804.3 19.5 %collective-permute-done.131.refs_4_ = bf16[4,128,256]{2,1,0:T(8,128)(2,1)} collective-permute-done((bf16[4,128,256]{2,1,0:T(8,128)(2,1)}, bf16[4,128,256]{2,1,0:T(8,128)(2,1)}, u32[]{:S(2)}, u32[]{:S(2)}) %collective-permute-start.131) | collective-permute-done | bytes 262176 | tf_op jit(solution)/shard_map/ppermute | solution.py:280
  825.4 24.6 %update.2 = (f32[12,128,2048]{2,1,0:T(8,128)}, f32[12,128,2048]{2,1,0:T(8,128)}, f32[12,128,2048]{2,1,0:T(8,128)}, bf16[12,128,2048]{2,1,0:T(8,128)(2,1)}) custom-call(s32[16]{0:T(128)} %mul.238.starts, s32[12]{0:T(128)} %convert_element_type.570.live, f32[12,128,2048]{2,1,0:T(8,128)} %mas.3, f32[12,128,2048]{2,1,0:T(8,128)} %one.3, f32[12,128,2048]{2,1,0:T(8,128)} %two.3, ...), custom_call_target="tpu_custom_call" | custom-call | tf_op jit(solution)/shard_map/update/pallas_call | solution.py:697
  851.0 13.1 %update.3 = (f32[12,128,2048]{2,1,0:T(8,128)}, f32[12,128,2048]{2,1,0:T(8,128)}, f32[12,128,2048]{2,1,0:T(8,128)}, bf16[12,128,2048]{2,1,0:T(8,128)(2,1)}) custom-call(s32[16]{0:T(128)} %mul.238.starts, s32[12]{0:T(128)} %convert_element_type.570.live, ...), custom_call_target="tpu_custom_call", output_to_operand_aliasing={{0}: (13, {}), {1}: (14, {}), {2}: (15, {}), {3}: (16, {})} | custom-call | tf_op jit(solution)/shard_map/update/pallas_call | solution.py:697
  (641 shorter events, 382.1 us)
Async XLA Ops:
  13.7 73.3 %collective-permute-start = (bf16[12,128,256]{2,1,0:T(8,128)(2,1)}, bf16[12,128,256]{2,1,0:T(8,128)(2,1)S(1)}, u32[]{:S(2)}, u32[]{:S(2)}) collective-permute-start(bf16[12,128,256]{2,1,0:T(8,128)(2,1)} %get-tuple-element.95), channel_id=1, source_target_pairs={{0,16},{1,17},{2,18},{3,19},{4,20},{5,21},{6,22},{7,23},{8,24},{9,... | collective-permute-start | bytes 2359304 | tf_op jit(solution)/shard_map/ppermute | solution.py:280
  17.8 87.3 %collective-permute-start.1 = (bf16[12,128,256]{2,1,0:T(8,128)(2,1)}, bf16[12,128,256]{2,1,0:T(8,128)(2,1)S(1)}, u32[]{:S(2)}, u32[]{:S(2)}) collective-permute-start(bf16[12,128,256]{2,1,0:T(8,128)(2,1)} %get-tuple-element.96), channel_id=1, source_target_pairs={{0,20},{1,21},{2,22},{3,23},{4,16},{5,17},{6,18},{7,19},{8,28},{9,... | collective-permute-start | bytes 2359304 | tf_op jit(solution)/shard_map/ppermute | solution.py:280
  19.1 88.5 %collective-permute-start.2 = (bf16[12,128,256]{2,1,0:T(8,128)(2,1)}, bf16[12,128,256]{2,1,0:T(8,128)(2,1)}, u32[]{:S(2)}, u32[]{:S(2)}) collective-permute-start(bf16[12,128,256]{2,1,0:T(8,128)(2,1)} %get-tuple-element.97), channel_id=1, source_target_pairs={{0,24},{1,25},{2,26},{3,27},{4,28},{5,29},{6,30},{7,31},{8,16},{9,... | collective-permute-start | bytes 2359304 | tf_op jit(solution)/shard_map/ppermute | solution.py:280
  22.7 89.0 %collective-permute-start.14 = (bf16[12,128,256]{2,1,0:T(8,128)(2,1)}, bf16[12,128,256]{2,1,0:T(8,128)(2,1)}, u32[]{:S(2)}, u32[]{:S(2)}) collective-permute-start(bf16[12,128,256]{2,1,0:T(8,128)(2,1)} %get-tuple-element.99), channel_id=1, source_target_pairs={{0,4},{1,5},{2,6},{3,7},{4,0},{5,1},{6,2},{7,3},{8,12},{9,13},{10,... | collective-permute-start | bytes 2359304 | tf_op jit(solution)/shard_map/ppermute | solution.py:280
  23.2 89.8 %collective-permute-start.15 = (bf16[12,128,256]{2,1,0:T(8,128)(2,1)}, bf16[12,128,256]{2,1,0:T(8,128)(2,1)}, u32[]{:S(2)}, u32[]{:S(2)}) collective-permute-start(bf16[12,128,256]{2,1,0:T(8,128)(2,1)} %get-tuple-element.100), channel_id=1, source_target_pairs={{0,8},{1,9},{2,10},{3,11},{4,12},{5,13},{6,14},{7,15},{8,0},{9,1},... | collective-permute-start | bytes 2359304 | tf_op jit(solution)/shard_map/ppermute | solution.py:280
  87.0 63.5 %collective-permute-start.16 = (bf16[12,128,256]{2,1,0:T(8,128)(2,1)}, bf16[12,128,256]{2,1,0:T(8,128)(2,1)}, u32[]{:S(2)}, u32[]{:S(2)}) collective-permute-start(bf16[12,128,256]{2,1,0:T(8,128)(2,1)} %get-tuple-element.101), channel_id=1, source_target_pairs={{0,12},{1,13},{2,14},{3,15},{4,8},{5,9},{6,10},{7,11},{8,4},{9,5},... | collective-permute-start | bytes 2359304 | tf_op jit(solution)/shard_map/ppermute | solution.py:280
  105.1 45.4 %collective-permute-start.17 = (bf16[12,128,256]{2,1,0:T(8,128)(2,1)}, bf16[12,128,256]{2,1,0:T(8,128)(2,1)}, u32[]{:S(2)}, u32[]{:S(2)}) collective-permute-start(bf16[12,128,256]{2,1,0:T(8,128)(2,1)} %get-tuple-element.102), channel_id=1, source_target_pairs={{0,28},{1,29},{2,30},{3,31},{4,24},{5,25},{6,26},{7,27},{8,20},{9,... | collective-permute-start | bytes 2359304 | tf_op jit(solution)/shard_map/ppermute | solution.py:280
  107.6 49.2 %collective-permute-start.3 = (bf16[64,2048]{1,0:T(8,128)(2,1)S(1)}, bf16[64,2048]{1,0:T(8,128)(2,1)}, u32[]{:S(2)}, u32[]{:S(2)}) collective-permute-start(bf16[64,2048]{1,0:T(8,128)(2,1)S(1)} %maximum_select_fusion.1), channel_id=1, source_target_pairs={{0,2},{1,3},{2,0},{3,1},{4,6},{5,7},{6,4},{7,5},{8,10},{9,11},{10,... | collective-permute-start | bytes 786440 | tf_op jit(solution)/shard_map/ppermute | solution.py:280
  111.7 46.8 %collective-permute-start.11 = (bf16[64,2048]{1,0:T(8,128)(2,1)S(1)}, bf16[64,2048]{1,0:T(8,128)(2,1)}, u32[]{:S(2)}, u32[]{:S(2)}) collective-permute-start(bf16[64,2048]{1,0:T(8,128)(2,1)S(1)} %maximum_select_fusion.1), channel_id=1, source_target_pairs={{0,24},{1,25},{2,26},{3,27},{4,28},{5,29},{6,30},{7,31},{8,16},{9,... | collective-permute-start | bytes 786440 | tf_op jit(solution)/shard_map/ppermute | solution.py:280
  113.1 45.9 %collective-permute-start.5 = (bf16[64,2048]{1,0:T(8,128)(2,1)S(1)}, bf16[64,2048]{1,0:T(8,128)(2,1)S(1)}, u32[]{:S(2)}, u32[]{:S(2)}) collective-permute-start(bf16[64,2048]{1,0:T(8,128)(2,1)S(1)} %maximum_select_fusion.1), channel_id=1, source_target_pairs={{0,8},{1,9},{2,10},{3,11},{4,12},{5,13},{6,14},{7,15},{8,0},{9,1},... | collective-permute-start | bytes 786440 | tf_op jit(solution)/shard_map/ppermute | solution.py:280
  155.3 56.1 %collective-permute-start.18 = (bf16[1024,384]{1,0:T(8,128)(2,1)}, bf16[1024,384]{1,0:T(8,128)(2,1)}, u32[]{:S(2)}, u32[]{:S(2)}) collective-permute-start(bf16[1024,384]{1,0:T(8,128)(2,1)} %pick_qkv.1), channel_id=1, source_target_pairs={{0,4},{1,5},{2,6},{3,7},{4,0},{5,1},{6,2},{7,3},{8,12},{9,13},{10,... | collective-permute-start | bytes 2359304 | tf_op jit(solution)/shard_map/ppermute | solution.py:280
  158.5 35.0 %collective-permute-start.4 = (bf16[128,2048]{1,0:T(8,128)(2,1)}, bf16[128,2048]{1,0:T(8,128)(2,1)}, u32[]{:S(2)}, u32[]{:S(2)}) collective-permute-start(bf16[128,2048]{1,0:T(8,128)(2,1)} %constant_dynamic-update-slice_fusion.refs_0_), channel_id=1, source_target_pairs={{0,1},{1,0},{2,3},{3,2},{4,5},{5,4},{6,7},{7,6},{8,9},{9,8},{10,11... | collective-permute-start | bytes 1572872 | tf_op jit(solution)/shard_map/ppermute | solution.py:280
  265.9 39.0 %collective-permute-start.53 = (bf16[64,2048]{1,0:T(8,128)(2,1)S(1)}, bf16[64,2048]{1,0:T(8,128)(2,1)S(1)}, u32[]{:S(2)}, u32[]{:S(2)}) collective-permute-start(bf16[64,2048]{1,0:T(8,128)(2,1)S(1)} %constant_dynamic-slice_fusion), channel_id=1, source_target_pairs={{0,16},{1,17},{2,18},{3,19},{4,20},{5,21},{6,22},{7,23},{8,24},{9,... | collective-permute-start | bytes 786440 | tf_op jit(solution)/shard_map/ppermute | solution.py:280
  305.2 37.2 %collective-permute-start.49 = (bf16[128,2048]{1,0:T(8,128)(2,1)S(1)}, bf16[128,2048]{1,0:T(8,128)(2,1)}, u32[]{:S(2)}, u32[]{:S(2)}) collective-permute-start(bf16[128,2048]{1,0:T(8,128)(2,1)S(1)} %pad_maximum_fusion.10.refs_0_), channel_id=1, source_target_pairs={{0,1},{1,0},{2,3},{3,2},{4,5},{5,4},{6,7},{7,6},{8,9},{9,8},{10,11... | collective-permute-start | bytes 1572872 | tf_op jit(solution)/shard_map/ppermute | solution.py:280
  364.1 48.9 %collective-permute-start.47 = (bf16[16,128,256]{2,1,0:T(8,128)(2,1)}, bf16[16,128,256]{2,1,0:T(8,128)(2,1)}, u32[]{:S(2)}, u32[]{:S(2)}) collective-permute-start(bf16[16,128,256]{2,1,0:T(8,128)(2,1)} %get-tuple-element.113), channel_id=1, source_target_pairs={{0,4},{1,5},{2,6},{3,7},{4,0},{5,1},{6,2},{7,3},{8,12},{9,13},{10,... | collective-permute-start | bytes 3145736 | tf_op jit(solution)/shard_map/ppermute | solution.py:280
  507.9 93.2 %collective-permute-start.105 = (bf16[2048,512]{1,0:T(8,128)(2,1)}, bf16[2048,512]{1,0:T(8,128)(2,1)}, u32[]{:S(2)}, u32[]{:S(2)}) collective-permute-start(bf16[2048,512]{1,0:T(8,128)(2,1)} %slice.804), channel_id=1, source_target_pairs={{0,4},{1,5},{2,6},{3,7},{4,0},{5,1},{6,2},{7,3},{8,12},{9,13},{10,... | collective-permute-start | bytes 6291464 | tf_op jit(solution)/shard_map/ppermute | solution.py:280
  509.5 69.7 %collective-permute-start.106 = (bf16[4,4,128,256]{3,2,1,0:T(8,128)(2,1)}, bf16[4,4,128,256]{3,2,1,0:T(8,128)(2,1)}, u32[]{:S(2)}, u32[]{:S(2)}) collective-permute-start(bf16[4,4,128,256]{3,2,1,0:T(8,128)(2,1)} %get-tuple-element.131), channel_id=1, source_target_pairs={{0,4},{1,5},{2,6},{3,7},{4,0},{5,1},{6,2},{7,3},{8,12},{9,13},{10,... | collective-permute-start | bytes 3145736 | tf_op jit(solution)/shard_map/ppermute | solution.py:280
  542.2 93.3 %collective-permute-start.80 = (bf16[64,2048]{1,0:T(8,128)(2,1)}, bf16[64,2048]{1,0:T(8,128)(2,1)}, u32[]{:S(2)}, u32[]{:S(2)}) collective-permute-start(bf16[64,2048]{1,0:T(8,128)(2,1)} %slice.810), channel_id=1, source_target_pairs={{0,2},{1,3},{2,0},{3,1},{4,6},{5,7},{6,4},{7,5},{8,10},{9,11},{10,... | collective-permute-start | bytes 786440 | tf_op jit(solution)/shard_map/ppermute | solution.py:280
  645.5 33.2 %collective-permute-start.126 = (bf16[8,128,256]{2,1,0:T(8,128)(2,1)S(1)}, bf16[8,128,256]{2,1,0:T(8,128)(2,1)S(1)}, u32[]{:S(2)}, u32[]{:S(2)}) collective-permute-start(bf16[8,128,256]{2,1,0:T(8,128)(2,1)S(1)} %copy-done.72), channel_id=1, source_target_pairs={{0,8},{1,9},{2,10},{3,11},{4,12},{5,13},{6,14},{7,15},{8,0},{9,1},... | collective-permute-start | bytes 1572872 | tf_op jit(solution)/shard_map/ppermute | solution.py:280
  674.8 60.6 %collective-permute-start.130 = (bf16[8,128,256]{2,1,0:T(8,128)(2,1)S(1)}, bf16[8,128,256]{2,1,0:T(8,128)(2,1)S(1)}, u32[]{:S(2)}, u32[]{:S(2)}) collective-permute-start(bf16[8,128,256]{2,1,0:T(8,128)(2,1)S(1)} %copy-done.74), channel_id=1, source_target_pairs={{0,16},{1,17},{2,18},{3,19},{4,20},{5,21},{6,22},{7,23},{8,24},{9,... | collective-permute-start | bytes 1572872 | tf_op jit(solution)/shard_map/ppermute | solution.py:280
  674.8 78.5 %collective-permute-start.132 = (bf16[8,128,256]{2,1,0:T(8,128)(2,1)S(1)}, bf16[8,128,256]{2,1,0:T(8,128)(2,1)}, u32[]{:S(2)}, u32[]{:S(2)}) collective-permute-start(bf16[8,128,256]{2,1,0:T(8,128)(2,1)S(1)} %copy-done.75), channel_id=1, source_target_pairs={{0,20},{1,21},{2,22},{3,23},{4,16},{5,17},{6,18},{7,19},{8,28},{9,... | collective-permute-start | bytes 1572872 | tf_op jit(solution)/shard_map/ppermute | solution.py:280
  678.7 74.6 %collective-permute-start.134 = (bf16[8,128,256]{2,1,0:T(8,128)(2,1)S(1)}, bf16[8,128,256]{2,1,0:T(8,128)(2,1)}, u32[]{:S(2)}, u32[]{:S(2)}) collective-permute-start(bf16[8,128,256]{2,1,0:T(8,128)(2,1)S(1)} %copy-done.76), channel_id=1, source_target_pairs={{0,24},{1,25},{2,26},{3,27},{4,28},{5,29},{6,30},{7,31},{8,16},{9,... | collective-permute-start | bytes 1572872 | tf_op jit(solution)/shard_map/ppermute | solution.py:280
  687.7 70.7 %collective-permute-start.136 = (bf16[8,128,256]{2,1,0:T(8,128)(2,1)}, bf16[8,128,256]{2,1,0:T(8,128)(2,1)S(1)}, u32[]{:S(2)}, u32[]{:S(2)}) collective-permute-start(bf16[8,128,256]{2,1,0:T(8,128)(2,1)} %get-tuple-element.170), channel_id=1, source_target_pairs={{0,28},{1,29},{2,30},{3,31},{4,24},{5,25},{6,26},{7,27},{8,20},{9,... | collective-permute-start | bytes 1572872 | tf_op jit(solution)/shard_map/ppermute | solution.py:280
  691.3 67.2 %collective-permute-start.111 = (bf16[64,2048]{1,0:T(8,128)(2,1)S(1)}, bf16[64,2048]{1,0:T(8,128)(2,1)}, u32[]{:S(2)}, u32[]{:S(2)}) collective-permute-start(bf16[64,2048]{1,0:T(8,128)(2,1)S(1)} %slice.808), channel_id=1, source_target_pairs={{0,2},{1,3},{2,0},{3,1},{4,6},{5,7},{6,4},{7,5},{8,10},{9,11},{10,... | collective-permute-start | bytes 786440 | tf_op jit(solution)/shard_map/ppermute | solution.py:280
  758.5 32.8 %collective-permute-start.86 = (bf16[64,2048]{1,0:T(8,128)(2,1)}, bf16[64,2048]{1,0:T(8,128)(2,1)}, u32[]{:S(2)}, u32[]{:S(2)}) collective-permute-start(bf16[64,2048]{1,0:T(8,128)(2,1)} %copy-done.88), channel_id=1, source_target_pairs={{0,1},{1,0},{2,3},{3,2},{4,5},{5,4},{6,7},{7,6},{8,9},{9,8},{10,11... | collective-permute-start | bytes 786440 | tf_op jit(solution)/shard_map/ppermute | solution.py:280
  758.5 35.2 %collective-permute-start.87 = (bf16[64,2048]{1,0:T(8,128)(2,1)}, bf16[64,2048]{1,0:T(8,128)(2,1)}, u32[]{:S(2)}, u32[]{:S(2)}) collective-permute-start(bf16[64,2048]{1,0:T(8,128)(2,1)} %collective-permute-done.85), channel_id=1, source_target_pairs={{0,1},{1,0},{2,3},{3,2},{4,5},{5,4},{6,7},{7,6},{8,9},{9,8},{10,11... | collective-permute-start | bytes 786440 | tf_op jit(solution)/shard_map/ppermute | solution.py:280
  759.0 37.4 %collective-permute-start.125 = (bf16[4,128,256]{2,1,0:T(8,128)(2,1)}, bf16[4,128,256]{2,1,0:T(8,128)(2,1)S(1)}, u32[]{:S(2)}, u32[]{:S(2)}) collective-permute-start(bf16[4,128,256]{2,1,0:T(8,128)(2,1)} %get-tuple-element.153), channel_id=1, source_target_pairs={{0,4},{1,5},{2,6},{3,7},{4,0},{5,1},{6,2},{7,3},{8,12},{9,13},{10,... | collective-permute-start | bytes 786440 | tf_op jit(solution)/shard_map/ppermute | solution.py:280
  793.7 56.4 %collective-permute-start.133 = (bf16[4,128,256]{2,1,0:T(8,128)(2,1)}, bf16[4,128,256]{2,1,0:T(8,128)(2,1)S(1)}, u32[]{:S(2)}, u32[]{:S(2)}) collective-permute-start(bf16[4,128,256]{2,1,0:T(8,128)(2,1)} %get-tuple-element.165), channel_id=1, source_target_pairs={{0,20},{1,21},{2,22},{3,23},{4,16},{5,17},{6,18},{7,19},{8,28},{9,... | collective-permute-start | bytes 786440 | tf_op jit(solution)/shard_map/ppermute | solution.py:280
  796.4 53.7 %collective-permute-start.135 = (bf16[4,128,256]{2,1,0:T(8,128)(2,1)}, bf16[4,128,256]{2,1,0:T(8,128)(2,1)S(1)}, u32[]{:S(2)}, u32[]{:S(2)}) collective-permute-start(bf16[4,128,256]{2,1,0:T(8,128)(2,1)} %get-tuple-element.168), channel_id=1, source_target_pairs={{0,24},{1,25},{2,26},{3,27},{4,28},{5,29},{6,30},{7,31},{8,16},{9,... | collective-permute-start | bytes 786440 | tf_op jit(solution)/shard_map/ppermute | solution.py:280
  798.9 51.2 %collective-permute-start.137 = (bf16[4,128,256]{2,1,0:T(8,128)(2,1)}, bf16[4,128,256]{2,1,0:T(8,128)(2,1)S(1)}, u32[]{:S(2)}, u32[]{:S(2)}) collective-permute-start(bf16[4,128,256]{2,1,0:T(8,128)(2,1)} %get-tuple-element.171), channel_id=1, source_target_pairs={{0,28},{1,29},{2,30},{3,31},{4,24},{5,25},{6,26},{7,27},{8,20},{9,... | collective-permute-start | bytes 786440 | tf_op jit(solution)/shard_map/ppermute | solution.py:280
  801.4 62.7 %collective-permute-start.121 = (bf16[64,2048]{1,0:T(8,128)(2,1)}, bf16[64,2048]{1,0:T(8,128)(2,1)S(1)}, u32[]{:S(2)}, u32[]{:S(2)}) collective-permute-start(bf16[64,2048]{1,0:T(8,128)(2,1)} %get-tuple-element.181), channel_id=1, source_target_pairs={{0,2},{1,3},{2,0},{3,1},{4,6},{5,7},{6,4},{7,5},{8,10},{9,11},{10,... | collective-permute-start | bytes 786440 | tf_op jit(solution)/shard_map/ppermute | solution.py:280
  823.8 41.0 %collective-permute-start.122 = (bf16[64,2048]{1,0:T(8,128)(2,1)}, bf16[64,2048]{1,0:T(8,128)(2,1)S(1)}, u32[]{:S(2)}, u32[]{:S(2)}) collective-permute-start(bf16[64,2048]{1,0:T(8,128)(2,1)} %get-tuple-element.181), channel_id=1, source_target_pairs={{0,1},{1,0},{2,3},{3,2},{4,5},{5,4},{6,7},{7,6},{8,9},{9,8},{10,11... | collective-permute-start | bytes 786440 | tf_op jit(solution)/shard_map/ppermute | solution.py:280
  (207 other events, 3642.6 us)

commit v4 on v3

--- a/solution.py
+++ b/solution.py
@@ -730,7 +730,7 @@
     for part in near:
         pair = jnp.concatenate([part, swap(part, 0, 2)])
         blocks += [pair, swap(pair, 0, 1)]
-    return stack_rows(blocks)
+    return stack_rows(blocks), near[1:]
 
 
 def scatter_sum(partial_sum):
@@ -801,11 +801,11 @@
     inputs = lax.dynamic_slice(tokens_later, (wt * rows, 0), (rows, width)).astype(F32)
     normed, norm_back = jax.vjp(layer_norm, inputs)
     normed_cut = to_cut_order(normed.astype(LOW))
-    normed_all = gather_rows(after(normed_cut, came[4], came[5], came[6]))
+    normed_all, normed_came = gather_rows(after(normed_cut, came[4], came[5], came[6]))
     w_qkv = pick_qkv(came, owner_bits[:12], slot_in_owner[:12])
     w_qkv_pair = swap(w_qkv, 1, 0)
-    out_grad_low = lax.dynamic_slice(after(cotangent, w_qkv_pair), (wt * rows, 0), (rows, width))
-    grad_all = gather_rows(out_grad_low)
+    out_grad_low = lax.dynamic_slice(cotangent, (wt * rows, 0), (rows, width))
+    grad_all, _ = gather_rows(after(out_grad_low, w_qkv, *normed_came))
     wanted = jnp.concatenate(
         [
             jnp.arange(16, 48, dtype=jnp.int32),
@@ -856,11 +856,12 @@
     w_gu = jnp.concatenate(
         [part.reshape(width, 256) for part in (home_gate, home_up, pair_gate, pair_up)], axis=1
     )
-    att_out, _ = scatter_sum(dot(att_low, w_out).astype(LOW))
+    att_part = dot(att_low, w_out).astype(LOW)
+    att_out, _ = scatter_sum(att_part)
     residual = inputs + att_out
 
     normed_two, norm_two_back = jax.vjp(layer_norm, residual)
-    two_all = gather_rows(normed_two.astype(LOW))
+    two_all, _ = gather_rows(normed_two.astype(LOW))
     gu = dot(two_all, w_gu)
     gate = jnp.concatenate([gu[:, :256], gu[:, 512:768]], axis=1)
     up = jnp.concatenate([gu[:, 256:512], gu[:, 768:]], axis=1)
@@ -875,13 +876,13 @@
         [grad_gate[:, :256], grad_up[:, :256], grad_gate[:, 256:], grad_up[:, 256:]], axis=1
     )
     two_grad, begun = scatter_sum(dot_nt(grad_gu, w_gu).astype(LOW))
-    hidden_later, grad_gu_later = lax.optimization_barrier((hidden, grad_gu, begun))[:2]
-    grad_w_gu = dot_tn(two_all, grad_gu_later)
+    hidden_later = after(hidden, begun)
+    grad_w_down = dot_tn(hidden_later, grad_all)
+
+    resid_grad = out_grad_low.astype(F32) + norm_two_back(two_grad)[0]
+    resid_all, _ = gather_rows(resid_grad.astype(LOW))
+    grad_w_gu = dot_tn(two_all, after(grad_gu, two_grad))
     gu_back = swap(grad_w_gu[:, 512:].astype(LOW), 1, 0)
-
-    resid_grad = out_grad_low.astype(F32) + norm_two_back(two_grad)[0]
-    resid_all = gather_rows(resid_grad.astype(LOW))
-    grad_w_down = dot_tn(after(hidden_later, two_grad), grad_all)
     down, _ = scatter_sum(dot(after(hidden, two_grad), w_down).astype(LOW))
     output = share_rows((residual + down).astype(LOW), wt)
     gu_sum = (grad_w_gu[:, :512] + gu_back.astype(F32)).astype(LOW)

time: 877 us -> 861 us (0.982)
  waiting for transfers between devices: 396 us -> 384 us
    ppermute x138, waiting for transfers between devices: 396 us -> 384 us  [swap(): return lax.ppermute(value, AXES, pairs)]
    unnamed x216 -> x231, local copies, waits for them, and re-layouts: 21.2 us -> 19.7 us
  transfers between devices with their start and end apart: 138 -> 138, of which waited for: 45 -> 45; matrix products, arithmetic and copies ran while one was open for 12% -> 13% of each run, Pallas kernels for 13% -> 13%
where the time goes in v4:
time: 861 us; the launch traced here: 852 us
  waiting for transfers between devices  384 us (45%)
  starting transfers between devices  187 us (22%)
  Pallas kernels  126 us (15%)
  matrix products  59 us (7%)
  local copies, waits for them, and re-layouts  48.4 us (6%)
  other arithmetic  45.4 us (5%)
    ppermute x138, waiting for transfers between devices, swap(): return lax.ppermute(value, AXES, pairs)  384 us
    ppermute x138, starting transfers between devices, swap(): return lax.ppermute(value, AXES, pairs)  187 us
    pallas_call x2, Pallas kernels, update(): pl.pallas_call(body, grid_spec=pltpu.PrefetchScalarGridSpec(num_scalar_pr...  37.8 us
    dot_general x5, matrix products, dot_tn(): lax.dot_general(left, right, (((0,), (0,)), ((), ())), preferred_element_...  21 us
    dot_general x5, matrix products, dot_nt(): lax.dot_general(left, right, (((1,), (1,)), ((), ())), preferred_element_...  20.5 us
    unnamed x231, local copies, waits for them, and re-layouts  19.7 us
    pallas_call x4, Pallas kernels, stack_rows(): pl.pallas_call(body, in_specs=[VMEM_SPEC] * len(blocks), out_specs=VMEM_S...  17.7 us
    dot_general x5, matrix products, dot(): return jnp.dot(left, right, preferred_element_type=F32)  17.4 us
  transfers between devices with their start and end apart: 138, of which 45 were waited for; matrix products, arithmetic and copies ran while one was open for 13% of the time, Pallas kernels for 13%

profile of v4, /device:TPU:0, one launch (start us, length us, event | category | flops | bytes accessed | tf_op | source)
XLA Modules:
  0.0 851.7 jit_solution(15933056278114459837)
XLA Ops:
  1.4 12.4 %lane_split.1 = (bf16[12,128,256]{2,1,0:T(8,128)(2,1)}, bf16[12,128,256]{2,1,0:T(8,128)(2,1)}, bf16[12,128,256]{2,1,0:T(8,128)(2,1)}, bf16[12,128,256]{2,1,0:T(8...) custom-call(s32[16]{0:T(128)} %mul.238.starts, ...), custom_call_target="tpu_custom_call" | custom-call | tf_op jit(solution)/shard_map/lane_split/pallas_call | solution.py:307
  28.9 58.2 %collective-permute-done.refs_4_ = bf16[12,128,256]{2,1,0:T(8,128)(2,1)S(1)} collective-permute-done((bf16[12,128,256]{2,1,0:T(8,128)(2,1)}, bf16[12,128,256]{2,1,0:T(8,128)(2,1)S(1)}, u32[]{:S(2)}, u32[]{:S(2)}) %collective-permute-start) | collective-permute-done | bytes 786464 | tf_op jit(solution)/shard_map/ppermute | solution.py:280
  88.1 17.1 %collective-permute-done.1.refs_5_ = bf16[12,128,256]{2,1,0:T(8,128)(2,1)S(1)} collective-permute-done((bf16[12,128,256]{2,1,0:T(8,128)(2,1)}, bf16[12,128,256]{2,1,0:T(8,128)(2,1)S(1)}, u32[]{:S(2)}, u32[]{:S(2)}) %collective-permute-start.1) | collective-permute-done | bytes 786464 | tf_op jit(solution)/shard_map/ppermute | solution.py:280
  113.0 36.7 %collective-permute-start.5 = (bf16[64,2048]{1,0:T(8,128)(2,1)S(1)}, bf16[64,2048]{1,0:T(8,128)(2,1)S(1)}, u32[]{:S(2)}, u32[]{:S(2)}) collective-permute-start(bf16[64,2048]{1,0:T(8,128)(2,1)S(1)} %maximum_select_fusion.1), channel_id=1, source_target_pairs={{0,8},{1,9},{2,10},{3,11},{4,12},{5,13},{6,14},{7,15},{8,0},{9,1},... | collective-permute-start | bytes 786440 | tf_op jit(solution)/shard_map/ppermute | solution.py:280
  160.6 15.6 %collective-permute-done.8 = bf16[64,2048]{1,0:T(8,128)(2,1)} collective-permute-done((bf16[64,2048]{1,0:T(8,128)(2,1)S(1)}, bf16[64,2048]{1,0:T(8,128)(2,1)}, u32[]{:S(2)}, u32[]{:S(2)}) %collective-permute-start.8) | collective-permute-done | bytes 262176 | tf_op jit(solution)/shard_map/ppermute | solution.py:280
  188.2 5.5 row_gather.1
  193.7 10.9 %collective-permute-start.20 = (bf16[1,128,256]{2,1,0:T(8,128)(2,1)}, bf16[1,128,256]{2,1,0:T(8,128)(2,1)S(1)}, u32[]{:S(2)}, u32[]{:S(2)}) collective-permute-start(bf16[1,128,256]{2,1,0:T(8,128)(2,1)} %get-tuple-element.105), channel_id=1, source_target_pairs={{0,8},{1,9},{2,10},{3,11},{4,12},{5,13},{6,14},{7,15},{8,0},{9,1},... | collective-permute-start | bytes 196616 | tf_op jit(solution)/shard_map/ppermute | solution.py:280
  228.9 10.1 %collective-permute-done.23.other_ref = bf16[4,1,128,256]{3,2,1,0:T(8,128)(2,1)S(1)} collective-permute-done((bf16[4,1,128,256]{3,2,1,0:T(8,128)(2,1)S(1)}, bf16[4,1,128,256]{3,2,1,0:T(8,128)(2,1)S(1)}, u32[]{:S(2)}, u32[]{:S(2)}) %collective-permute-start.23) | collective-permute-done | bytes 262176 | tf_op jit(solution)/shard_map/ppermute | solution.py:280
  245.5 8.1 attend.1
  267.8 7.0 collective-permute-done.50
  277.1 6.7 collective-permute-done.27
  301.9 8.0 collective-permute-done.31
  316.6 7.4 collective-permute-done.37
  325.6 7.8 collective-permute-done.40
  340.2 15.2 %collective-permute-done.44 = bf16[64,2048]{1,0:T(8,128)(2,1)S(1)} collective-permute-done((bf16[64,2048]{1,0:T(8,128)(2,1)S(1)}, bf16[64,2048]{1,0:T(8,128)(2,1)S(1)}, u32[]{:S(2)}, u32[]{:S(2)}) %collective-permute-start.44) | collective-permute-done | bytes 262176 | tf_op jit(solution)/shard_map/ppermute | solution.py:280
  375.5 7.3 collective-permute-done.46
  382.8 22.0 %collective-permute-done.47 = bf16[16,128,256]{2,1,0:T(8,128)(2,1)} collective-permute-done((bf16[16,128,256]{2,1,0:T(8,128)(2,1)}, bf16[16,128,256]{2,1,0:T(8,128)(2,1)}, u32[]{:S(2)}, u32[]{:S(2)}) %collective-permute-start.47) | collective-permute-done | bytes 1048608 | tf_op jit(solution)/shard_map/ppermute | solution.py:280
  404.8 8.2 fusion.31
  420.8 6.7 convolution_convert_fusion.2
  468.3 5.2 lane_halves.3
  504.4 10.7 %collective-permute-done.97 = bf16[64,2048]{1,0:T(8,128)(2,1)S(1)} collective-permute-done((bf16[64,2048]{1,0:T(8,128)(2,1)S(1)}, bf16[64,2048]{1,0:T(8,128)(2,1)S(1)}, u32[]{:S(2)}, u32[]{:S(2)}) %collective-permute-start.97) | collective-permute-done | bytes 262176 | tf_op jit(solution)/shard_map/ppermute | solution.py:280
  540.6 11.7 %attend_back.1 = (f32[1024,128]{1,0:T(8,128)}, f32[1024,256]{1,0:T(8,128)}, bf16[1024,256]{1,0:T(8,128)(2,1)}) custom-call(bf16[1024,128]{1,0:T(8,128)(2,1)} %pad_maximum_fusion.13.q, bf16[1024,256]{1,0:T(8,128)(2,1)} %copy-done.5, bf16[1024,256]{1,0:T(8,128)(2,1)} %copy-done.29, bf16[1024,128]{1,0:T(8,128)(2,1)} %convolution_convert_fusion.5.do, ...), custom_call_target="tpu_custom_call" | custom-call | tf_op jit(solution)/shard_map/attend_back/pallas_call | solution.py:653
  561.5 13.8 %collective-permute-done.99.there = bf16[1024,256]{1,0:T(8,128)(2,1)S(1)} collective-permute-done((bf16[1024,256]{1,0:T(8,128)(2,1)}, bf16[1024,256]{1,0:T(8,128)(2,1)S(1)}, u32[]{:S(2)}, u32[]{:S(2)}) %collective-permute-start.99) | collective-permute-done | bytes 524320 | tf_op jit(solution)/shard_map/ppermute | solution.py:280
  596.7 5.9 place_mlp.1
  634.8 13.1 %collective-permute-done.81 = bf16[64,2048]{1,0:T(8,128)(2,1)S(1)} collective-permute-done((bf16[64,2048]{1,0:T(8,128)(2,1)S(1)}, bf16[64,2048]{1,0:T(8,128)(2,1)S(1)}, u32[]{:S(2)}, u32[]{:S(2)}) %collective-permute-start.81) | collective-permute-done | bytes 262176 | tf_op jit(solution)/shard_map/ppermute | solution.py:280
  652.9 6.3 collective-permute-done.85
  676.3 43.5 %collective-permute-done.130.refs_4_ = bf16[8,128,256]{2,1,0:T(8,128)(2,1)S(1)} collective-permute-done((bf16[8,128,256]{2,1,0:T(8,128)(2,1)S(1)}, bf16[8,128,256]{2,1,0:T(8,128)(2,1)S(1)}, u32[]{:S(2)}, u32[]{:S(2)}) %collective-permute-start.130) | collective-permute-done | bytes 524320 | tf_op jit(solution)/shard_map/ppermute | solution.py:280
  720.6 16.5 %collective-permute-done.132.refs_5_ = bf16[8,128,256]{2,1,0:T(8,128)(2,1)} collective-permute-done((bf16[8,128,256]{2,1,0:T(8,128)(2,1)S(1)}, bf16[8,128,256]{2,1,0:T(8,128)(2,1)}, u32[]{:S(2)}, u32[]{:S(2)}) %collective-permute-start.132) | collective-permute-done | bytes 524320 | tf_op jit(solution)/shard_map/ppermute | solution.py:280
  743.1 25.2 %collective-permute-done.117 = bf16[64,2048]{1,0:T(8,128)(2,1)} collective-permute-done((bf16[64,2048]{1,0:T(8,128)(2,1)}, bf16[64,2048]{1,0:T(8,128)(2,1)}, u32[]{:S(2)}, u32[]{:S(2)}) %collective-permute-start.117) | collective-permute-done | bytes 262176 | tf_op jit(solution)/shard_map/ppermute | solution.py:280
  787.4 20.2 %collective-permute-done.131.refs_4_ = bf16[4,128,256]{2,1,0:T(8,128)(2,1)} collective-permute-done((bf16[4,128,256]{2,1,0:T(8,128)(2,1)}, bf16[4,128,256]{2,1,0:T(8,128)(2,1)}, u32[]{:S(2)}, u32[]{:S(2)}) %collective-permute-start.131) | collective-permute-done | bytes 262176 | tf_op jit(solution)/shard_map/ppermute | solution.py:280
  809.2 24.6 %update.2 = (f32[12,128,2048]{2,1,0:T(8,128)}, f32[12,128,2048]{2,1,0:T(8,128)}, f32[12,128,2048]{2,1,0:T(8,128)}, bf16[12,128,2048]{2,1,0:T(8,128)(2,1)}) custom-call(s32[16]{0:T(128)} %mul.238.starts, s32[12]{0:T(128)} %convert_element_type.570.live, f32[12,128,2048]{2,1,0:T(8,128)} %mas.3, f32[12,128,2048]{2,1,0:T(8,128)} %one.3, f32[12,128,2048]{2,1,0:T(8,128)} %two.3, ...), custom_call_target="tpu_custom_call" | custom-call | tf_op jit(solution)/shard_map/update/pallas_call | solution.py:697
  834.8 13.1 %update.3 = (f32[12,128,2048]{2,1,0:T(8,128)}, f32[12,128,2048]{2,1,0:T(8,128)}, f32[12,128,2048]{2,1,0:T(8,128)}, bf16[12,128,2048]{2,1,0:T(8,128)(2,1)}) custom-call(s32[16]{0:T(128)} %mul.238.starts, s32[12]{0:T(128)} %convert_element_type.570.live, ...), custom_call_target="tpu_custom_call", output_to_operand_aliasing={{0}: (13, {}), {1}: (14, {}), {2}: (15, {}), {3}: (16, {})} | custom-call | tf_op jit(solution)/shard_map/update/pallas_call | solution.py:697
  (656 shorter events, 367.9 us)
Async XLA Ops:
  13.8 73.3 %collective-permute-start = (bf16[12,128,256]{2,1,0:T(8,128)(2,1)}, bf16[12,128,256]{2,1,0:T(8,128)(2,1)S(1)}, u32[]{:S(2)}, u32[]{:S(2)}) collective-permute-start(bf16[12,128,256]{2,1,0:T(8,128)(2,1)} %get-tuple-element.94), channel_id=1, source_target_pairs={{0,16},{1,17},{2,18},{3,19},{4,20},{5,21},{6,22},{7,23},{8,24},{9,... | collective-permute-start | bytes 2359304 | tf_op jit(solution)/shard_map/ppermute | solution.py:280
  17.9 87.3 %collective-permute-start.1 = (bf16[12,128,256]{2,1,0:T(8,128)(2,1)}, bf16[12,128,256]{2,1,0:T(8,128)(2,1)S(1)}, u32[]{:S(2)}, u32[]{:S(2)}) collective-permute-start(bf16[12,128,256]{2,1,0:T(8,128)(2,1)} %get-tuple-element.95), channel_id=1, source_target_pairs={{0,20},{1,21},{2,22},{3,23},{4,16},{5,17},{6,18},{7,19},{8,28},{9,... | collective-permute-start | bytes 2359304 | tf_op jit(solution)/shard_map/ppermute | solution.py:280
  19.2 88.5 %collective-permute-start.2 = (bf16[12,128,256]{2,1,0:T(8,128)(2,1)}, bf16[12,128,256]{2,1,0:T(8,128)(2,1)}, u32[]{:S(2)}, u32[]{:S(2)}) collective-permute-start(bf16[12,128,256]{2,1,0:T(8,128)(2,1)} %get-tuple-element.96), channel_id=1, source_target_pairs={{0,24},{1,25},{2,26},{3,27},{4,28},{5,29},{6,30},{7,31},{8,16},{9,... | collective-permute-start | bytes 2359304 | tf_op jit(solution)/shard_map/ppermute | solution.py:280
  22.8 88.9 %collective-permute-start.14 = (bf16[12,128,256]{2,1,0:T(8,128)(2,1)}, bf16[12,128,256]{2,1,0:T(8,128)(2,1)}, u32[]{:S(2)}, u32[]{:S(2)}) collective-permute-start(bf16[12,128,256]{2,1,0:T(8,128)(2,1)} %get-tuple-element.98), channel_id=1, source_target_pairs={{0,4},{1,5},{2,6},{3,7},{4,0},{5,1},{6,2},{7,3},{8,12},{9,13},{10,... | collective-permute-start | bytes 2359304 | tf_op jit(solution)/shard_map/ppermute | solution.py:280
  23.3 89.7 %collective-permute-start.15 = (bf16[12,128,256]{2,1,0:T(8,128)(2,1)}, bf16[12,128,256]{2,1,0:T(8,128)(2,1)}, u32[]{:S(2)}, u32[]{:S(2)}) collective-permute-start(bf16[12,128,256]{2,1,0:T(8,128)(2,1)} %get-tuple-element.99), channel_id=1, source_target_pairs={{0,8},{1,9},{2,10},{3,11},{4,12},{5,13},{6,14},{7,15},{8,0},{9,1},... | collective-permute-start | bytes 2359304 | tf_op jit(solution)/shard_map/ppermute | solution.py:280
  87.1 63.4 %collective-permute-start.16 = (bf16[12,128,256]{2,1,0:T(8,128)(2,1)}, bf16[12,128,256]{2,1,0:T(8,128)(2,1)}, u32[]{:S(2)}, u32[]{:S(2)}) collective-permute-start(bf16[12,128,256]{2,1,0:T(8,128)(2,1)} %get-tuple-element.100), channel_id=1, source_target_pairs={{0,12},{1,13},{2,14},{3,15},{4,8},{5,9},{6,10},{7,11},{8,4},{9,5},... | collective-permute-start | bytes 2359304 | tf_op jit(solution)/shard_map/ppermute | solution.py:280
  105.2 45.3 %collective-permute-start.17 = (bf16[12,128,256]{2,1,0:T(8,128)(2,1)}, bf16[12,128,256]{2,1,0:T(8,128)(2,1)}, u32[]{:S(2)}, u32[]{:S(2)}) collective-permute-start(bf16[12,128,256]{2,1,0:T(8,128)(2,1)} %get-tuple-element.101), channel_id=1, source_target_pairs={{0,28},{1,29},{2,30},{3,31},{4,24},{5,25},{6,26},{7,27},{8,20},{9,... | collective-permute-start | bytes 2359304 | tf_op jit(solution)/shard_map/ppermute | solution.py:280
  107.7 49.2 %collective-permute-start.3 = (bf16[64,2048]{1,0:T(8,128)(2,1)S(1)}, bf16[64,2048]{1,0:T(8,128)(2,1)}, u32[]{:S(2)}, u32[]{:S(2)}) collective-permute-start(bf16[64,2048]{1,0:T(8,128)(2,1)S(1)} %maximum_select_fusion.1), channel_id=1, source_target_pairs={{0,2},{1,3},{2,0},{3,1},{4,6},{5,7},{6,4},{7,5},{8,10},{9,11},{10,... | collective-permute-start | bytes 786440 | tf_op jit(solution)/shard_map/ppermute | solution.py:280
  111.7 46.9 %collective-permute-start.11 = (bf16[64,2048]{1,0:T(8,128)(2,1)S(1)}, bf16[64,2048]{1,0:T(8,128)(2,1)}, u32[]{:S(2)}, u32[]{:S(2)}) collective-permute-start(bf16[64,2048]{1,0:T(8,128)(2,1)S(1)} %maximum_select_fusion.1), channel_id=1, source_target_pairs={{0,24},{1,25},{2,26},{3,27},{4,28},{5,29},{6,30},{7,31},{8,16},{9,... | collective-permute-start | bytes 786440 | tf_op jit(solution)/shard_map/ppermute | solution.py:280
  113.0 46.0 %collective-permute-start.5 = (bf16[64,2048]{1,0:T(8,128)(2,1)S(1)}, bf16[64,2048]{1,0:T(8,128)(2,1)S(1)}, u32[]{:S(2)}, u32[]{:S(2)}) collective-permute-start(bf16[64,2048]{1,0:T(8,128)(2,1)S(1)} %maximum_select_fusion.1), channel_id=1, source_target_pairs={{0,8},{1,9},{2,10},{3,11},{4,12},{5,13},{6,14},{7,15},{8,0},{9,1},... | collective-permute-start | bytes 786440 | tf_op jit(solution)/shard_map/ppermute | solution.py:280
  155.3 56.5 %collective-permute-start.18 = (bf16[1024,384]{1,0:T(8,128)(2,1)}, bf16[1024,384]{1,0:T(8,128)(2,1)}, u32[]{:S(2)}, u32[]{:S(2)}) collective-permute-start(bf16[1024,384]{1,0:T(8,128)(2,1)} %pick_qkv.1), channel_id=1, source_target_pairs={{0,4},{1,5},{2,6},{3,7},{4,0},{5,1},{6,2},{7,3},{8,12},{9,13},{10,... | collective-permute-start | bytes 2359304 | tf_op jit(solution)/shard_map/ppermute | solution.py:280
  158.6 35.1 %collective-permute-start.4 = (bf16[128,2048]{1,0:T(8,128)(2,1)}, bf16[128,2048]{1,0:T(8,128)(2,1)}, u32[]{:S(2)}, u32[]{:S(2)}) collective-permute-start(bf16[128,2048]{1,0:T(8,128)(2,1)} %constant_dynamic-update-slice_fusion.refs_0_), channel_id=1, source_target_pairs={{0,1},{1,0},{2,3},{3,2},{4,5},{5,4},{6,7},{7,6},{8,9},{9,8},{10,11... | collective-permute-start | bytes 1572872 | tf_op jit(solution)/shard_map/ppermute | solution.py:280
  297.1 37.0 %collective-permute-start.49 = (bf16[128,2048]{1,0:T(8,128)(2,1)S(1)}, bf16[128,2048]{1,0:T(8,128)(2,1)}, u32[]{:S(2)}, u32[]{:S(2)}) collective-permute-start(bf16[128,2048]{1,0:T(8,128)(2,1)S(1)} %constant_dynamic-update-slice_fusion.15.refs_0_), channel_id=1, source_target_pairs={{0,1},{1,0},{2,3},{3,2},{4,5},{5,4},{6,7},{7,6},{8,9},{9,8},{10,11... | collective-permute-start | bytes 1572872 | tf_op jit(solution)/shard_map/ppermute | solution.py:280
  355.9 48.9 %collective-permute-start.47 = (bf16[16,128,256]{2,1,0:T(8,128)(2,1)}, bf16[16,128,256]{2,1,0:T(8,128)(2,1)}, u32[]{:S(2)}, u32[]{:S(2)}) collective-permute-start(bf16[16,128,256]{2,1,0:T(8,128)(2,1)} %get-tuple-element.112), channel_id=1, source_target_pairs={{0,4},{1,5},{2,6},{3,7},{4,0},{5,1},{6,2},{7,3},{8,12},{9,13},{10,... | collective-permute-start | bytes 3145736 | tf_op jit(solution)/shard_map/ppermute | solution.py:280
  473.5 45.1 %collective-permute-start.106 = (bf16[4,4,128,256]{3,2,1,0:T(8,128)(2,1)}, bf16[4,4,128,256]{3,2,1,0:T(8,128)(2,1)S(1)}, u32[]{:S(2)}, u32[]{:S(2)}) collective-permute-start(bf16[4,4,128,256]{3,2,1,0:T(8,128)(2,1)} %get-tuple-element.129), channel_id=1, source_target_pairs={{0,4},{1,5},{2,6},{3,7},{4,0},{5,1},{6,2},{7,3},{8,12},{9,13},{10,... | collective-permute-start | bytes 3145736 | tf_op jit(solution)/shard_map/ppermute | solution.py:280
  515.8 69.3 %collective-permute-start.105 = (bf16[2048,512]{1,0:T(8,128)(2,1)}, bf16[2048,512]{1,0:T(8,128)(2,1)}, u32[]{:S(2)}, u32[]{:S(2)}) collective-permute-start(bf16[2048,512]{1,0:T(8,128)(2,1)} %slice.804), channel_id=1, source_target_pairs={{0,4},{1,5},{2,6},{3,7},{4,0},{5,1},{6,2},{7,3},{8,12},{9,13},{10,... | collective-permute-start | bytes 6291464 | tf_op jit(solution)/shard_map/ppermute | solution.py:280
  526.3 92.8 %collective-permute-start.80 = (bf16[64,2048]{1,0:T(8,128)(2,1)}, bf16[64,2048]{1,0:T(8,128)(2,1)}, u32[]{:S(2)}, u32[]{:S(2)}) collective-permute-start(bf16[64,2048]{1,0:T(8,128)(2,1)} %slice.810), channel_id=1, source_target_pairs={{0,2},{1,3},{2,0},{3,1},{4,6},{5,7},{6,4},{7,5},{8,10},{9,11},{10,... | collective-permute-start | bytes 786440 | tf_op jit(solution)/shard_map/ppermute | solution.py:280
  526.9 65.7 %collective-permute-start.109 = (bf16[4,128,256]{2,1,0:T(8,128)(2,1)}, bf16[4,128,256]{2,1,0:T(8,128)(2,1)}, u32[]{:S(2)}, u32[]{:S(2)}) collective-permute-start(bf16[4,128,256]{2,1,0:T(8,128)(2,1)} %get-tuple-element.229), channel_id=1, source_target_pairs={{0,24},{1,25},{2,26},{3,27},{4,28},{5,29},{6,30},{7,31},{8,16},{9,... | collective-permute-start | bytes 786440 | tf_op jit(solution)/shard_map/ppermute | solution.py:280
  529.5 64.6 %collective-permute-start.108 = (bf16[4,128,256]{2,1,0:T(8,128)(2,1)}, bf16[4,128,256]{2,1,0:T(8,128)(2,1)}, u32[]{:S(2)}, u32[]{:S(2)}) collective-permute-start(bf16[4,128,256]{2,1,0:T(8,128)(2,1)} %get-tuple-element.230), channel_id=1, source_target_pairs={{0,16},{1,17},{2,18},{3,19},{4,20},{5,21},{6,22},{7,23},{8,24},{9,... | collective-permute-start | bytes 786440 | tf_op jit(solution)/shard_map/ppermute | solution.py:280
  659.2 60.6 %collective-permute-start.130 = (bf16[8,128,256]{2,1,0:T(8,128)(2,1)S(1)}, bf16[8,128,256]{2,1,0:T(8,128)(2,1)S(1)}, u32[]{:S(2)}, u32[]{:S(2)}) collective-permute-start(bf16[8,128,256]{2,1,0:T(8,128)(2,1)S(1)} %copy-done.74), channel_id=1, source_target_pairs={{0,16},{1,17},{2,18},{3,19},{4,20},{5,21},{6,22},{7,23},{8,24},{9,... | collective-permute-start | bytes 1572872 | tf_op jit(solution)/shard_map/ppermute | solution.py:280
  659.2 77.9 %collective-permute-start.132 = (bf16[8,128,256]{2,1,0:T(8,128)(2,1)S(1)}, bf16[8,128,256]{2,1,0:T(8,128)(2,1)}, u32[]{:S(2)}, u32[]{:S(2)}) collective-permute-start(bf16[8,128,256]{2,1,0:T(8,128)(2,1)S(1)} %copy-done.75), channel_id=1, source_target_pairs={{0,20},{1,21},{2,22},{3,23},{4,16},{5,17},{6,18},{7,19},{8,28},{9,... | collective-permute-start | bytes 1572872 | tf_op jit(solution)/shard_map/ppermute | solution.py:280
  662.6 74.6 %collective-permute-start.134 = (bf16[8,128,256]{2,1,0:T(8,128)(2,1)S(1)}, bf16[8,128,256]{2,1,0:T(8,128)(2,1)}, u32[]{:S(2)}, u32[]{:S(2)}) collective-permute-start(bf16[8,128,256]{2,1,0:T(8,128)(2,1)S(1)} %copy-done.76), channel_id=1, source_target_pairs={{0,24},{1,25},{2,26},{3,27},{4,28},{5,29},{6,30},{7,31},{8,16},{9,... | collective-permute-start | bytes 1572872 | tf_op jit(solution)/shard_map/ppermute | solution.py:280
  670.9 70.6 %collective-permute-start.136 = (bf16[8,128,256]{2,1,0:T(8,128)(2,1)}, bf16[8,128,256]{2,1,0:T(8,128)(2,1)S(1)}, u32[]{:S(2)}, u32[]{:S(2)}) collective-permute-start(bf16[8,128,256]{2,1,0:T(8,128)(2,1)} %get-tuple-element.168), channel_id=1, source_target_pairs={{0,28},{1,29},{2,30},{3,31},{4,24},{5,25},{6,26},{7,27},{8,20},{9,... | collective-permute-start | bytes 1572872 | tf_op jit(solution)/shard_map/ppermute | solution.py:280
  675.5 65.9 %collective-permute-start.111 = (bf16[64,2048]{1,0:T(8,128)(2,1)S(1)}, bf16[64,2048]{1,0:T(8,128)(2,1)}, u32[]{:S(2)}, u32[]{:S(2)}) collective-permute-start(bf16[64,2048]{1,0:T(8,128)(2,1)S(1)} %slice.808), channel_id=1, source_target_pairs={{0,2},{1,3},{2,0},{3,1},{4,6},{5,7},{6,4},{7,5},{8,10},{9,11},{10,... | collective-permute-start | bytes 786440 | tf_op jit(solution)/shard_map/ppermute | solution.py:280
  741.5 33.7 %collective-permute-start.86 = (bf16[64,2048]{1,0:T(8,128)(2,1)}, bf16[64,2048]{1,0:T(8,128)(2,1)}, u32[]{:S(2)}, u32[]{:S(2)}) collective-permute-start(bf16[64,2048]{1,0:T(8,128)(2,1)} %copy-done.88), channel_id=1, source_target_pairs={{0,1},{1,0},{2,3},{3,2},{4,5},{5,4},{6,7},{7,6},{8,9},{9,8},{10,11... | collective-permute-start | bytes 786440 | tf_op jit(solution)/shard_map/ppermute | solution.py:280
  741.5 35.9 %collective-permute-start.87 = (bf16[64,2048]{1,0:T(8,128)(2,1)}, bf16[64,2048]{1,0:T(8,128)(2,1)}, u32[]{:S(2)}, u32[]{:S(2)}) collective-permute-start(bf16[64,2048]{1,0:T(8,128)(2,1)} %collective-permute-done.85), channel_id=1, source_target_pairs={{0,1},{1,0},{2,3},{3,2},{4,5},{5,4},{6,7},{7,6},{8,9},{9,8},{10,11... | collective-permute-start | bytes 786440 | tf_op jit(solution)/shard_map/ppermute | solution.py:280
  742.0 38.8 %collective-permute-start.125 = (bf16[4,128,256]{2,1,0:T(8,128)(2,1)}, bf16[4,128,256]{2,1,0:T(8,128)(2,1)S(1)}, u32[]{:S(2)}, u32[]{:S(2)}) collective-permute-start(bf16[4,128,256]{2,1,0:T(8,128)(2,1)} %get-tuple-element.151), channel_id=1, source_target_pairs={{0,4},{1,5},{2,6},{3,7},{4,0},{5,1},{6,2},{7,3},{8,12},{9,13},{10,... | collective-permute-start | bytes 786440 | tf_op jit(solution)/shard_map/ppermute | solution.py:280
  777.4 56.5 %collective-permute-start.133 = (bf16[4,128,256]{2,1,0:T(8,128)(2,1)}, bf16[4,128,256]{2,1,0:T(8,128)(2,1)S(1)}, u32[]{:S(2)}, u32[]{:S(2)}) collective-permute-start(bf16[4,128,256]{2,1,0:T(8,128)(2,1)} %get-tuple-element.163), channel_id=1, source_target_pairs={{0,20},{1,21},{2,22},{3,23},{4,16},{5,17},{6,18},{7,19},{8,28},{9,... | collective-permute-start | bytes 786440 | tf_op jit(solution)/shard_map/ppermute | solution.py:280
  780.8 53.1 %collective-permute-start.135 = (bf16[4,128,256]{2,1,0:T(8,128)(2,1)}, bf16[4,128,256]{2,1,0:T(8,128)(2,1)S(1)}, u32[]{:S(2)}, u32[]{:S(2)}) collective-permute-start(bf16[4,128,256]{2,1,0:T(8,128)(2,1)} %get-tuple-element.166), channel_id=1, source_target_pairs={{0,24},{1,25},{2,26},{3,27},{4,28},{5,29},{6,30},{7,31},{8,16},{9,... | collective-permute-start | bytes 786440 | tf_op jit(solution)/shard_map/ppermute | solution.py:280
  782.7 51.2 %collective-permute-start.137 = (bf16[4,128,256]{2,1,0:T(8,128)(2,1)}, bf16[4,128,256]{2,1,0:T(8,128)(2,1)S(1)}, u32[]{:S(2)}, u32[]{:S(2)}) collective-permute-start(bf16[4,128,256]{2,1,0:T(8,128)(2,1)} %get-tuple-element.169), channel_id=1, source_target_pairs={{0,28},{1,29},{2,30},{3,31},{4,24},{5,25},{6,26},{7,27},{8,20},{9,... | collective-permute-start | bytes 786440 | tf_op jit(solution)/shard_map/ppermute | solution.py:280
  785.2 62.7 %collective-permute-start.121 = (bf16[64,2048]{1,0:T(8,128)(2,1)}, bf16[64,2048]{1,0:T(8,128)(2,1)S(1)}, u32[]{:S(2)}, u32[]{:S(2)}) collective-permute-start(bf16[64,2048]{1,0:T(8,128)(2,1)} %get-tuple-element.179), channel_id=1, source_target_pairs={{0,2},{1,3},{2,0},{3,1},{4,6},{5,7},{6,4},{7,5},{8,10},{9,11},{10,... | collective-permute-start | bytes 786440 | tf_op jit(solution)/shard_map/ppermute | solution.py:280
  807.6 41.0 %collective-permute-start.122 = (bf16[64,2048]{1,0:T(8,128)(2,1)}, bf16[64,2048]{1,0:T(8,128)(2,1)S(1)}, u32[]{:S(2)}, u32[]{:S(2)}) collective-permute-start(bf16[64,2048]{1,0:T(8,128)(2,1)} %get-tuple-element.179), channel_id=1, source_target_pairs={{0,1},{1,0},{2,3},{3,2},{4,5},{5,4},{6,7},{7,6},{8,9},{9,8},{10,11... | collective-permute-start | bytes 786440 | tf_op jit(solution)/shard_map/ppermute | solution.py:280
  (214 other events, 3852.4 us)

commit v5 on v4

--- a/solution.py
+++ b/solution.py
@@ -681,11 +681,12 @@
                 at = (0, slice(None), pl.ds(pl.multiple_of(starts[2 * home + half], 128), 128))
                 grad = grads[home][0, :, half * 128 : half * 128 + 128].astype(F32)
                 grad = jnp.where(alive, grad, 0.0)
-                mean = adam_beta * one[at] + (1.0 - adam_beta) * grad
-                square = adam_beta * two[at] + (1.0 - adam_beta) * grad * grad
-                ratio = (mean * (1.0 / bias)) / (jnp.sqrt(square * (1.0 / bias)) + adam_eps)
-                old = mas[at]
-                new = old - learn_rate * (ratio + decay_rate * old)
+                mean = adam_beta * (one[at] + grad)
+                square = adam_beta * (two[at] + grad * grad)
+                spread = square * (1.0 / bias)
+                root = spread * lax.rsqrt(spread) + adam_eps
+                step = mean * (learn_rate / bias) / root
+                new = mas[at] * (1.0 - learn_rate * decay_rate) - step
                 new_mas[at] = new
                 new_one[at] = mean
                 new_two[at] = square
@@ -801,7 +802,7 @@
     inputs = lax.dynamic_slice(tokens_later, (wt * rows, 0), (rows, width)).astype(F32)
     normed, norm_back = jax.vjp(layer_norm, inputs)
     normed_cut = to_cut_order(normed.astype(LOW))
-    normed_all, normed_came = gather_rows(after(normed_cut, came[4], came[5], came[6]))
+    normed_all, normed_came = gather_rows(after(normed_cut, came[4], came[5]))
     w_qkv = pick_qkv(came, owner_bits[:12], slot_in_owner[:12])
     w_qkv_pair = swap(w_qkv, 1, 0)
     out_grad_low = lax.dynamic_slice(cotangent, (wt * rows, 0), (rows, width))
@@ -888,7 +889,7 @@
     gu_sum = (grad_w_gu[:, :512] + gu_back.astype(F32)).astype(LOW)
     down_came = return_halves(grad_w_down.reshape(4, tile_rows, width), lane_starts)
 
-    part_slots = cap * 2 // 3
+    part_slots = cap // 2 + 1
     send_to = owner_bits + 8 * (slot_in_owner // part_slots)
     send_row = slot_in_owner % part_slots
     place = jnp.stack([z_at, x_at])

time: 861 us -> 863 us (level)
  waiting for transfers between devices: 384 us -> 401 us
  starting transfers between devices: 187 us -> 171 us
    ppermute x138, waiting for transfers between devices: 384 us -> 401 us  [swap(): return lax.ppermute(value, AXES, pairs)]
    ppermute x138, starting transfers between devices: 187 us -> 171 us  [swap(): return lax.ppermute(value, AXES, pairs)]
    unnamed x231 -> x233, local copies, waits for them, and re-layouts: 19.7 us -> 20.1 us
  transfers between devices with their start and end apart: 138 -> 138, of which waited for: 45 -> 46; matrix products, arithmetic and copies ran while one was open for 13% -> 13% of each run, Pallas kernels for 13% -> 13%
where the time goes in v5:
time: 863 us; the launch traced here: 854 us
  waiting for transfers between devices  401 us (46%)
  starting transfers between devices  171 us (20%)
  Pallas kernels  125 us (14%)
  matrix products  58.9 us (7%)
  local copies, waits for them, and re-layouts  49.5 us (6%)
  other arithmetic  45.4 us (5%)
    ppermute x138, waiting for transfers between devices, swap(): return lax.ppermute(value, AXES, pairs)  401 us
    ppermute x138, starting transfers between devices, swap(): return lax.ppermute(value, AXES, pairs)  171 us
    pallas_call x2, Pallas kernels, update(): pl.pallas_call(body, grid_spec=pltpu.PrefetchScalarGridSpec(num_scalar_pr...  37 us
    dot_general x5, matrix products, dot_tn(): lax.dot_general(left, right, (((0,), (0,)), ((), ())), preferred_element_...  21 us
    dot_general x5, matrix products, dot_nt(): lax.dot_general(left, right, (((1,), (1,)), ((), ())), preferred_element_...  20.5 us
    unnamed x233, local copies, waits for them, and re-layouts  20.1 us
    pallas_call x4, Pallas kernels, stack_rows(): pl.pallas_call(body, in_specs=[VMEM_SPEC] * len(blocks), out_specs=VMEM_S...  17.7 us
    dot_general x5, matrix products, dot(): return jnp.dot(left, right, preferred_element_type=F32)  17.4 us
  transfers between devices with their start and end apart: 138, of which 46 were waited for; matrix products, arithmetic and copies ran while one was open for 13% of the time, Pallas kernels for 13%

profile of v5, /device:TPU:0, one launch (start us, length us, event | category | flops | bytes accessed | tf_op | source)
XLA Modules:
  0.0 853.8 jit_solution(3767423549745293369)
XLA Ops:
  1.4 12.4 %lane_split.1 = (bf16[12,128,256]{2,1,0:T(8,128)(2,1)}, bf16[12,128,256]{2,1,0:T(8,128)(2,1)}, bf16[12,128,256]{2,1,0:T(8,128)(2,1)}, bf16[12,128,256]{2,1,0:T(8...) custom-call(s32[16]{0:T(128)} %mul.240.starts, ...), custom_call_target="tpu_custom_call" | custom-call | tf_op jit(solution)/shard_map/lane_split/pallas_call | solution.py:307
  28.1 42.2 %collective-permute-done.refs_4_ = bf16[12,128,256]{2,1,0:T(8,128)(2,1)S(1)} collective-permute-done((bf16[12,128,256]{2,1,0:T(8,128)(2,1)}, bf16[12,128,256]{2,1,0:T(8,128)(2,1)S(1)}, u32[]{:S(2)}, u32[]{:S(2)}) %collective-permute-start) | collective-permute-done | bytes 786464 | tf_op jit(solution)/shard_map/ppermute | solution.py:280
  73.1 16.3 %collective-permute-done.1.refs_5_ = bf16[12,128,256]{2,1,0:T(8,128)(2,1)S(1)} collective-permute-done((bf16[12,128,256]{2,1,0:T(8,128)(2,1)}, bf16[12,128,256]{2,1,0:T(8,128)(2,1)S(1)}, u32[]{:S(2)}, u32[]{:S(2)}) %collective-permute-start.1) | collective-permute-done | bytes 786464 | tf_op jit(solution)/shard_map/ppermute | solution.py:280
  97.3 31.2 %collective-permute-done.15.refs_3_ = bf16[12,128,256]{2,1,0:T(8,128)(2,1)} collective-permute-done((bf16[12,128,256]{2,1,0:T(8,128)(2,1)}, bf16[12,128,256]{2,1,0:T(8,128)(2,1)}, u32[]{:S(2)}, u32[]{:S(2)}) %collective-permute-start.15) | collective-permute-done | bytes 786464 | tf_op jit(solution)/shard_map/ppermute | solution.py:280
  129.2 16.0 %collective-permute-start.7 = (bf16[64,2048]{1,0:T(8,128)(2,1)S(1)}, bf16[64,2048]{1,0:T(8,128)(2,1)}, u32[]{:S(2)}, u32[]{:S(2)}) collective-permute-start(bf16[64,2048]{1,0:T(8,128)(2,1)S(1)} %maximum_select_fusion.1), channel_id=1, source_target_pairs={{0,16},{1,17},{2,18},{3,19},{4,20},{5,21},{6,22},{7,23},{8,24},{9,... | collective-permute-start | bytes 786440 | tf_op jit(solution)/shard_map/ppermute | solution.py:280
  155.4 20.8 %collective-permute-done.7 = bf16[64,2048]{1,0:T(8,128)(2,1)} collective-permute-done((bf16[64,2048]{1,0:T(8,128)(2,1)S(1)}, bf16[64,2048]{1,0:T(8,128)(2,1)}, u32[]{:S(2)}, u32[]{:S(2)}) %collective-permute-start.7) | collective-permute-done | bytes 262176 | tf_op jit(solution)/shard_map/ppermute | solution.py:280
  193.8 10.9 %collective-permute-start.20 = (bf16[1,128,256]{2,1,0:T(8,128)(2,1)}, bf16[1,128,256]{2,1,0:T(8,128)(2,1)S(1)}, u32[]{:S(2)}, u32[]{:S(2)}) collective-permute-start(bf16[1,128,256]{2,1,0:T(8,128)(2,1)} %get-tuple-element.105), channel_id=1, source_target_pairs={{0,8},{1,9},{2,10},{3,11},{4,12},{5,13},{6,14},{7,15},{8,0},{9,1},... | collective-permute-start | bytes 196616 | tf_op jit(solution)/shard_map/ppermute | solution.py:280
  229.0 10.0 %collective-permute-done.23.other_ref = bf16[4,1,128,256]{3,2,1,0:T(8,128)(2,1)S(1)} collective-permute-done((bf16[4,1,128,256]{3,2,1,0:T(8,128)(2,1)S(1)}, bf16[4,1,128,256]{3,2,1,0:T(8,128)(2,1)S(1)}, u32[]{:S(2)}, u32[]{:S(2)}) %collective-permute-start.23) | collective-permute-done | bytes 262176 | tf_op jit(solution)/shard_map/ppermute | solution.py:280
  245.5 8.1 attend.1
  267.9 7.0 collective-permute-done.50
  277.1 6.7 collective-permute-done.27
  302.0 8.0 collective-permute-done.31
  316.6 7.4 collective-permute-done.37
  325.7 7.8 collective-permute-done.40
  340.2 15.2 %collective-permute-done.44 = bf16[64,2048]{1,0:T(8,128)(2,1)S(1)} collective-permute-done((bf16[64,2048]{1,0:T(8,128)(2,1)S(1)}, bf16[64,2048]{1,0:T(8,128)(2,1)S(1)}, u32[]{:S(2)}, u32[]{:S(2)}) %collective-permute-start.44) | collective-permute-done | bytes 262176 | tf_op jit(solution)/shard_map/ppermute | solution.py:280
  375.5 7.3 collective-permute-done.46
  382.8 22.0 %collective-permute-done.47 = bf16[16,128,256]{2,1,0:T(8,128)(2,1)} collective-permute-done((bf16[16,128,256]{2,1,0:T(8,128)(2,1)}, bf16[16,128,256]{2,1,0:T(8,128)(2,1)}, u32[]{:S(2)}, u32[]{:S(2)}) %collective-permute-start.47) | collective-permute-done | bytes 1048608 | tf_op jit(solution)/shard_map/ppermute | solution.py:280
  404.8 8.2 fusion.31
  420.9 6.7 convolution_convert_fusion.2
  504.4 10.7 %collective-permute-done.97 = bf16[64,2048]{1,0:T(8,128)(2,1)S(1)} collective-permute-done((bf16[64,2048]{1,0:T(8,128)(2,1)S(1)}, bf16[64,2048]{1,0:T(8,128)(2,1)S(1)}, u32[]{:S(2)}, u32[]{:S(2)}) %collective-permute-start.97) | collective-permute-done | bytes 262176 | tf_op jit(solution)/shard_map/ppermute | solution.py:280
  540.6 11.7 %attend_back.1 = (f32[1024,128]{1,0:T(8,128)}, f32[1024,256]{1,0:T(8,128)}, bf16[1024,256]{1,0:T(8,128)(2,1)}) custom-call(bf16[1024,128]{1,0:T(8,128)(2,1)} %pad_maximum_fusion.13.q, bf16[1024,256]{1,0:T(8,128)(2,1)} %copy-done.5, bf16[1024,256]{1,0:T(8,128)(2,1)} %copy-done.29, bf16[1024,128]{1,0:T(8,128)(2,1)} %convolution_convert_fusion.5.do, ...), custom_call_target="tpu_custom_call" | custom-call | tf_op jit(solution)/shard_map/attend_back/pallas_call | solution.py:653
  561.6 13.8 %collective-permute-done.99.there = bf16[1024,256]{1,0:T(8,128)(2,1)S(1)} collective-permute-done((bf16[1024,256]{1,0:T(8,128)(2,1)}, bf16[1024,256]{1,0:T(8,128)(2,1)S(1)}, u32[]{:S(2)}, u32[]{:S(2)}) %collective-permute-start.99) | collective-permute-done | bytes 524320 | tf_op jit(solution)/shard_map/ppermute | solution.py:280
  596.7 5.9 place_mlp.1
  634.4 13.5 %collective-permute-done.81 = bf16[64,2048]{1,0:T(8,128)(2,1)S(1)} collective-permute-done((bf16[64,2048]{1,0:T(8,128)(2,1)S(1)}, bf16[64,2048]{1,0:T(8,128)(2,1)S(1)}, u32[]{:S(2)}, u32[]{:S(2)}) %collective-permute-start.81) | collective-permute-done | bytes 262176 | tf_op jit(solution)/shard_map/ppermute | solution.py:280
  657.0 5.6 collective-permute-done.116
  673.1 5.7 collective-permute-done.128.refs_3_
  680.2 38.1 %collective-permute-done.130.refs_4_ = bf16[7,128,256]{2,1,0:T(8,128)(2,1)S(1)} collective-permute-done((bf16[7,128,256]{2,1,0:T(8,128)(2,1)S(1)}, bf16[7,128,256]{2,1,0:T(8,128)(2,1)S(1)}, u32[]{:S(2)}, u32[]{:S(2)}) %collective-permute-start.130) | collective-permute-done | bytes 458784 | tf_op jit(solution)/shard_map/ppermute | solution.py:280
  719.1 15.2 %collective-permute-done.132.refs_5_ = bf16[7,128,256]{2,1,0:T(8,128)(2,1)} collective-permute-done((bf16[7,128,256]{2,1,0:T(8,128)(2,1)S(1)}, bf16[7,128,256]{2,1,0:T(8,128)(2,1)}, u32[]{:S(2)}, u32[]{:S(2)}) %collective-permute-start.132) | collective-permute-done | bytes 458784 | tf_op jit(solution)/shard_map/ppermute | solution.py:280
  740.2 24.3 %collective-permute-done.117 = bf16[64,2048]{1,0:T(8,128)(2,1)} collective-permute-done((bf16[64,2048]{1,0:T(8,128)(2,1)}, bf16[64,2048]{1,0:T(8,128)(2,1)}, u32[]{:S(2)}, u32[]{:S(2)}) %collective-permute-start.117) | collective-permute-done | bytes 262176 | tf_op jit(solution)/shard_map/ppermute | solution.py:280
  787.8 22.6 %collective-permute-done.131.refs_4_ = bf16[5,128,256]{2,1,0:T(8,128)(2,1)} collective-permute-done((bf16[5,128,256]{2,1,0:T(8,128)(2,1)}, bf16[5,128,256]{2,1,0:T(8,128)(2,1)}, u32[]{:S(2)}, u32[]{:S(2)}) %collective-permute-start.131) | collective-permute-done | bytes 327712 | tf_op jit(solution)/shard_map/ppermute | solution.py:280
  812.1 21.1 %update.2 = (f32[12,128,2048]{2,1,0:T(8,128)}, f32[12,128,2048]{2,1,0:T(8,128)}, f32[12,128,2048]{2,1,0:T(8,128)}, bf16[12,128,2048]{2,1,0:T(8,128)(2,1)}) custom-call(s32[16]{0:T(128)} %mul.240.starts, s32[12]{0:T(128)} %convert_element_type.570.live, f32[12,128,2048]{2,1,0:T(8,128)} %mas.3, f32[12,128,2048]{2,1,0:T(8,128)} %one.3, f32[12,128,2048]{2,1,0:T(8,128)} %two.3, ...), custom_call_target="tpu_custom_call" | custom-call | tf_op jit(solution)/shard_map/update/pallas_call | solution.py:698
  834.2 15.9 %update.3 = (f32[12,128,2048]{2,1,0:T(8,128)}, f32[12,128,2048]{2,1,0:T(8,128)}, f32[12,128,2048]{2,1,0:T(8,128)}, bf16[12,128,2048]{2,1,0:T(8,128)(2,1)}) custom-call(s32[16]{0:T(128)} %mul.240.starts, s32[12]{0:T(128)} %convert_element_type.570.live, ...), custom_call_target="tpu_custom_call", output_to_operand_aliasing={{0}: (13, {}), {1}: (14, {}), {2}: (15, {}), {3}: (16, {})} | custom-call | tf_op jit(solution)/shard_map/update/pallas_call | solution.py:698
  (658 shorter events, 382.6 us)
Async XLA Ops:
  13.7 56.5 %collective-permute-start = (bf16[12,128,256]{2,1,0:T(8,128)(2,1)}, bf16[12,128,256]{2,1,0:T(8,128)(2,1)S(1)}, u32[]{:S(2)}, u32[]{:S(2)}) collective-permute-start(bf16[12,128,256]{2,1,0:T(8,128)(2,1)} %get-tuple-element.94), channel_id=1, source_target_pairs={{0,16},{1,17},{2,18},{3,19},{4,20},{5,21},{6,22},{7,23},{8,24},{9,... | collective-permute-start | bytes 2359304 | tf_op jit(solution)/shard_map/ppermute | solution.py:280
  17.9 71.5 %collective-permute-start.1 = (bf16[12,128,256]{2,1,0:T(8,128)(2,1)}, bf16[12,128,256]{2,1,0:T(8,128)(2,1)S(1)}, u32[]{:S(2)}, u32[]{:S(2)}) collective-permute-start(bf16[12,128,256]{2,1,0:T(8,128)(2,1)} %get-tuple-element.95), channel_id=1, source_target_pairs={{0,20},{1,21},{2,22},{3,23},{4,16},{5,17},{6,18},{7,19},{8,28},{9,... | collective-permute-start | bytes 2359304 | tf_op jit(solution)/shard_map/ppermute | solution.py:280
  19.1 72.8 %collective-permute-start.13 = (bf16[12,128,256]{2,1,0:T(8,128)(2,1)}, bf16[12,128,256]{2,1,0:T(8,128)(2,1)}, u32[]{:S(2)}, u32[]{:S(2)}) collective-permute-start(bf16[12,128,256]{2,1,0:T(8,128)(2,1)} %get-tuple-element.97), channel_id=1, source_target_pairs={{0,4},{1,5},{2,6},{3,7},{4,0},{5,1},{6,2},{7,3},{8,12},{9,13},{10,... | collective-permute-start | bytes 2359304 | tf_op jit(solution)/shard_map/ppermute | solution.py:280
  19.4 76.6 %collective-permute-start.14 = (bf16[12,128,256]{2,1,0:T(8,128)(2,1)}, bf16[12,128,256]{2,1,0:T(8,128)(2,1)}, u32[]{:S(2)}, u32[]{:S(2)}) collective-permute-start(bf16[12,128,256]{2,1,0:T(8,128)(2,1)} %get-tuple-element.98), channel_id=1, source_target_pairs={{0,8},{1,9},{2,10},{3,11},{4,12},{5,13},{6,14},{7,15},{8,0},{9,1},... | collective-permute-start | bytes 2359304 | tf_op jit(solution)/shard_map/ppermute | solution.py:280
  21.2 107.2 %collective-permute-start.15 = (bf16[12,128,256]{2,1,0:T(8,128)(2,1)}, bf16[12,128,256]{2,1,0:T(8,128)(2,1)}, u32[]{:S(2)}, u32[]{:S(2)}) collective-permute-start(bf16[12,128,256]{2,1,0:T(8,128)(2,1)} %get-tuple-element.99), channel_id=1, source_target_pairs={{0,12},{1,13},{2,14},{3,15},{4,8},{5,9},{6,10},{7,11},{8,4},{9,5},... | collective-permute-start | bytes 2359304 | tf_op jit(solution)/shard_map/ppermute | solution.py:280
  70.3 58.9 %collective-permute-start.16 = (bf16[12,128,256]{2,1,0:T(8,128)(2,1)}, bf16[12,128,256]{2,1,0:T(8,128)(2,1)}, u32[]{:S(2)}, u32[]{:S(2)}) collective-permute-start(bf16[12,128,256]{2,1,0:T(8,128)(2,1)} %get-tuple-element.100), channel_id=1, source_target_pairs={{0,24},{1,25},{2,26},{3,27},{4,28},{5,29},{6,30},{7,31},{8,16},{9,... | collective-permute-start | bytes 2359304 | tf_op jit(solution)/shard_map/ppermute | solution.py:280
  89.4 55.8 %collective-permute-start.17 = (bf16[12,128,256]{2,1,0:T(8,128)(2,1)}, bf16[12,128,256]{2,1,0:T(8,128)(2,1)}, u32[]{:S(2)}, u32[]{:S(2)}) collective-permute-start(bf16[12,128,256]{2,1,0:T(8,128)(2,1)} %get-tuple-element.101), channel_id=1, source_target_pairs={{0,28},{1,29},{2,30},{3,31},{4,24},{5,25},{6,26},{7,27},{8,20},{9,... | collective-permute-start | bytes 2359304 | tf_op jit(solution)/shard_map/ppermute | solution.py:280
  92.0 59.7 %collective-permute-start.2 = (bf16[64,2048]{1,0:T(8,128)(2,1)S(1)}, bf16[64,2048]{1,0:T(8,128)(2,1)}, u32[]{:S(2)}, u32[]{:S(2)}) collective-permute-start(bf16[64,2048]{1,0:T(8,128)(2,1)S(1)} %maximum_select_fusion.1), channel_id=1, source_target_pairs={{0,2},{1,3},{2,0},{3,1},{4,6},{5,7},{6,4},{7,5},{8,10},{9,11},{10,... | collective-permute-start | bytes 786440 | tf_op jit(solution)/shard_map/ppermute | solution.py:280
  96.0 57.4 %collective-permute-start.10 = (bf16[64,2048]{1,0:T(8,128)(2,1)S(1)}, bf16[64,2048]{1,0:T(8,128)(2,1)}, u32[]{:S(2)}, u32[]{:S(2)}) collective-permute-start(bf16[64,2048]{1,0:T(8,128)(2,1)S(1)} %maximum_select_fusion.1), channel_id=1, source_target_pairs={{0,24},{1,25},{2,26},{3,27},{4,28},{5,29},{6,30},{7,31},{8,16},{9,... | collective-permute-start | bytes 786440 | tf_op jit(solution)/shard_map/ppermute | solution.py:280
  129.2 47.0 %collective-permute-start.7 = (bf16[64,2048]{1,0:T(8,128)(2,1)S(1)}, bf16[64,2048]{1,0:T(8,128)(2,1)}, u32[]{:S(2)}, u32[]{:S(2)}) collective-permute-start(bf16[64,2048]{1,0:T(8,128)(2,1)S(1)} %maximum_select_fusion.1), channel_id=1, source_target_pairs={{0,16},{1,17},{2,18},{3,19},{4,20},{5,21},{6,22},{7,23},{8,24},{9,... | collective-permute-start | bytes 786440 | tf_op jit(solution)/shard_map/ppermute | solution.py:280
  150.1 61.7 %collective-permute-start.18 = (bf16[1024,384]{1,0:T(8,128)(2,1)}, bf16[1024,384]{1,0:T(8,128)(2,1)}, u32[]{:S(2)}, u32[]{:S(2)}) collective-permute-start(bf16[1024,384]{1,0:T(8,128)(2,1)} %pick_qkv.1), channel_id=1, source_target_pairs={{0,4},{1,5},{2,6},{3,7},{4,0},{5,1},{6,2},{7,3},{8,12},{9,13},{10,... | collective-permute-start | bytes 2359304 | tf_op jit(solution)/shard_map/ppermute | solution.py:280
  153.3 40.4 %collective-permute-start.3 = (bf16[128,2048]{1,0:T(8,128)(2,1)}, bf16[128,2048]{1,0:T(8,128)(2,1)}, u32[]{:S(2)}, u32[]{:S(2)}) collective-permute-start(bf16[128,2048]{1,0:T(8,128)(2,1)} %constant_dynamic-update-slice_fusion.refs_0_), channel_id=1, source_target_pairs={{0,1},{1,0},{2,3},{3,2},{4,5},{5,4},{6,7},{7,6},{8,9},{9,8},{10,11... | collective-permute-start | bytes 1572872 | tf_op jit(solution)/shard_map/ppermute | solution.py:280
  297.2 37.0 %collective-permute-start.49 = (bf16[128,2048]{1,0:T(8,128)(2,1)S(1)}, bf16[128,2048]{1,0:T(8,128)(2,1)}, u32[]{:S(2)}, u32[]{:S(2)}) collective-permute-start(bf16[128,2048]{1,0:T(8,128)(2,1)S(1)} %constant_dynamic-update-slice_fusion.15.refs_0_), channel_id=1, source_target_pairs={{0,1},{1,0},{2,3},{3,2},{4,5},{5,4},{6,7},{7,6},{8,9},{9,8},{10,11... | collective-permute-start | bytes 1572872 | tf_op jit(solution)/shard_map/ppermute | solution.py:280
  355.9 48.9 %collective-permute-start.47 = (bf16[16,128,256]{2,1,0:T(8,128)(2,1)}, bf16[16,128,256]{2,1,0:T(8,128)(2,1)}, u32[]{:S(2)}, u32[]{:S(2)}) collective-permute-start(bf16[16,128,256]{2,1,0:T(8,128)(2,1)} %get-tuple-element.112), channel_id=1, source_target_pairs={{0,4},{1,5},{2,6},{3,7},{4,0},{5,1},{6,2},{7,3},{8,12},{9,13},{10,... | collective-permute-start | bytes 3145736 | tf_op jit(solution)/shard_map/ppermute | solution.py:280
  473.6 45.1 %collective-permute-start.106 = (bf16[4,4,128,256]{3,2,1,0:T(8,128)(2,1)}, bf16[4,4,128,256]{3,2,1,0:T(8,128)(2,1)S(1)}, u32[]{:S(2)}, u32[]{:S(2)}) collective-permute-start(bf16[4,4,128,256]{3,2,1,0:T(8,128)(2,1)} %get-tuple-element.129), channel_id=1, source_target_pairs={{0,4},{1,5},{2,6},{3,7},{4,0},{5,1},{6,2},{7,3},{8,12},{9,13},{10,... | collective-permute-start | bytes 3145736 | tf_op jit(solution)/shard_map/ppermute | solution.py:280
  515.8 69.3 %collective-permute-start.105 = (bf16[2048,512]{1,0:T(8,128)(2,1)}, bf16[2048,512]{1,0:T(8,128)(2,1)}, u32[]{:S(2)}, u32[]{:S(2)}) collective-permute-start(bf16[2048,512]{1,0:T(8,128)(2,1)} %slice.804), channel_id=1, source_target_pairs={{0,4},{1,5},{2,6},{3,7},{4,0},{5,1},{6,2},{7,3},{8,12},{9,13},{10,... | collective-permute-start | bytes 6291464 | tf_op jit(solution)/shard_map/ppermute | solution.py:280
  526.3 92.8 %collective-permute-start.80 = (bf16[64,2048]{1,0:T(8,128)(2,1)}, bf16[64,2048]{1,0:T(8,128)(2,1)}, u32[]{:S(2)}, u32[]{:S(2)}) collective-permute-start(bf16[64,2048]{1,0:T(8,128)(2,1)} %slice.810), channel_id=1, source_target_pairs={{0,2},{1,3},{2,0},{3,1},{4,6},{5,7},{6,4},{7,5},{8,10},{9,11},{10,... | collective-permute-start | bytes 786440 | tf_op jit(solution)/shard_map/ppermute | solution.py:280
  526.9 65.7 %collective-permute-start.109 = (bf16[4,128,256]{2,1,0:T(8,128)(2,1)}, bf16[4,128,256]{2,1,0:T(8,128)(2,1)}, u32[]{:S(2)}, u32[]{:S(2)}) collective-permute-start(bf16[4,128,256]{2,1,0:T(8,128)(2,1)} %get-tuple-element.229), channel_id=1, source_target_pairs={{0,24},{1,25},{2,26},{3,27},{4,28},{5,29},{6,30},{7,31},{8,16},{9,... | collective-permute-start | bytes 786440 | tf_op jit(solution)/shard_map/ppermute | solution.py:280
  529.6 64.5 %collective-permute-start.108 = (bf16[4,128,256]{2,1,0:T(8,128)(2,1)}, bf16[4,128,256]{2,1,0:T(8,128)(2,1)}, u32[]{:S(2)}, u32[]{:S(2)}) collective-permute-start(bf16[4,128,256]{2,1,0:T(8,128)(2,1)} %get-tuple-element.230), channel_id=1, source_target_pairs={{0,16},{1,17},{2,18},{3,19},{4,20},{5,21},{6,22},{7,23},{8,24},{9,... | collective-permute-start | bytes 786440 | tf_op jit(solution)/shard_map/ppermute | solution.py:280
  664.6 53.7 %collective-permute-start.130 = (bf16[7,128,256]{2,1,0:T(8,128)(2,1)S(1)}, bf16[7,128,256]{2,1,0:T(8,128)(2,1)S(1)}, u32[]{:S(2)}, u32[]{:S(2)}) collective-permute-start(bf16[7,128,256]{2,1,0:T(8,128)(2,1)S(1)} %copy-done.74), channel_id=1, source_target_pairs={{0,16},{1,17},{2,18},{3,19},{4,20},{5,21},{6,22},{7,23},{8,24},{9,... | collective-permute-start | bytes 1376264 | tf_op jit(solution)/shard_map/ppermute | solution.py:280
  664.7 69.5 %collective-permute-start.132 = (bf16[7,128,256]{2,1,0:T(8,128)(2,1)S(1)}, bf16[7,128,256]{2,1,0:T(8,128)(2,1)}, u32[]{:S(2)}, u32[]{:S(2)}) collective-permute-start(bf16[7,128,256]{2,1,0:T(8,128)(2,1)S(1)} %copy-done.75), channel_id=1, source_target_pairs={{0,20},{1,21},{2,22},{3,23},{4,16},{5,17},{6,18},{7,19},{8,28},{9,... | collective-permute-start | bytes 1376264 | tf_op jit(solution)/shard_map/ppermute | solution.py:280
  668.0 66.3 %collective-permute-start.134 = (bf16[7,128,256]{2,1,0:T(8,128)(2,1)S(1)}, bf16[7,128,256]{2,1,0:T(8,128)(2,1)}, u32[]{:S(2)}, u32[]{:S(2)}) collective-permute-start(bf16[7,128,256]{2,1,0:T(8,128)(2,1)S(1)} %copy-done.76), channel_id=1, source_target_pairs={{0,24},{1,25},{2,26},{3,27},{4,28},{5,29},{6,30},{7,31},{8,16},{9,... | collective-permute-start | bytes 1376264 | tf_op jit(solution)/shard_map/ppermute | solution.py:280
  669.9 68.7 %collective-permute-start.136 = (bf16[7,128,256]{2,1,0:T(8,128)(2,1)}, bf16[7,128,256]{2,1,0:T(8,128)(2,1)S(1)}, u32[]{:S(2)}, u32[]{:S(2)}) collective-permute-start(bf16[7,128,256]{2,1,0:T(8,128)(2,1)} %get-tuple-element.168), channel_id=1, source_target_pairs={{0,28},{1,29},{2,30},{3,31},{4,24},{5,25},{6,26},{7,27},{8,20},{9,... | collective-permute-start | bytes 1376264 | tf_op jit(solution)/shard_map/ppermute | solution.py:280
  678.9 59.7 %collective-permute-start.111 = (bf16[64,2048]{1,0:T(8,128)(2,1)}, bf16[64,2048]{1,0:T(8,128)(2,1)}, u32[]{:S(2)}, u32[]{:S(2)}) collective-permute-start(bf16[64,2048]{1,0:T(8,128)(2,1)} %slice.808), channel_id=1, source_target_pairs={{0,2},{1,3},{2,0},{3,1},{4,6},{5,7},{6,4},{7,5},{8,10},{9,11},{10,... | collective-permute-start | bytes 786440 | tf_op jit(solution)/shard_map/ppermute | solution.py:280
  738.6 34.9 %collective-permute-start.87 = (bf16[64,2048]{1,0:T(8,128)(2,1)}, bf16[64,2048]{1,0:T(8,128)(2,1)}, u32[]{:S(2)}, u32[]{:S(2)}) collective-permute-start(bf16[64,2048]{1,0:T(8,128)(2,1)} %copy-done.85), channel_id=1, source_target_pairs={{0,1},{1,0},{2,3},{3,2},{4,5},{5,4},{6,7},{7,6},{8,9},{9,8},{10,11... | collective-permute-start | bytes 786440 | tf_op jit(solution)/shard_map/ppermute | solution.py:280
  739.1 37.8 %collective-permute-start.125 = (bf16[5,128,256]{2,1,0:T(8,128)(2,1)S(1)}, bf16[5,128,256]{2,1,0:T(8,128)(2,1)}, u32[]{:S(2)}, u32[]{:S(2)}) collective-permute-start(bf16[5,128,256]{2,1,0:T(8,128)(2,1)S(1)} %copy-done.77), channel_id=1, source_target_pairs={{0,4},{1,5},{2,6},{3,7},{4,0},{5,1},{6,2},{7,3},{8,12},{9,13},{10,... | collective-permute-start | bytes 983048 | tf_op jit(solution)/shard_map/ppermute | solution.py:280
  771.3 39.1 %collective-permute-start.131 = (bf16[5,128,256]{2,1,0:T(8,128)(2,1)}, bf16[5,128,256]{2,1,0:T(8,128)(2,1)}, u32[]{:S(2)}, u32[]{:S(2)}) collective-permute-start(bf16[5,128,256]{2,1,0:T(8,128)(2,1)} %get-tuple-element.160), channel_id=1, source_target_pairs={{0,16},{1,17},{2,18},{3,19},{4,20},{5,21},{6,22},{7,23},{8,24},{9,... | collective-permute-start | bytes 983048 | tf_op jit(solution)/shard_map/ppermute | solution.py:280
  773.5 59.8 %collective-permute-start.133 = (bf16[5,128,256]{2,1,0:T(8,128)(2,1)}, bf16[5,128,256]{2,1,0:T(8,128)(2,1)S(1)}, u32[]{:S(2)}, u32[]{:S(2)}) collective-permute-start(bf16[5,128,256]{2,1,0:T(8,128)(2,1)} %get-tuple-element.163), channel_id=1, source_target_pairs={{0,20},{1,21},{2,22},{3,23},{4,16},{5,17},{6,18},{7,19},{8,28},{9,... | collective-permute-start | bytes 983048 | tf_op jit(solution)/shard_map/ppermute | solution.py:280
  776.9 56.4 %collective-permute-start.135 = (bf16[5,128,256]{2,1,0:T(8,128)(2,1)}, bf16[5,128,256]{2,1,0:T(8,128)(2,1)S(1)}, u32[]{:S(2)}, u32[]{:S(2)}) collective-permute-start(bf16[5,128,256]{2,1,0:T(8,128)(2,1)} %get-tuple-element.166), channel_id=1, source_target_pairs={{0,24},{1,25},{2,26},{3,27},{4,28},{5,29},{6,30},{7,31},{8,16},{9,... | collective-permute-start | bytes 983048 | tf_op jit(solution)/shard_map/ppermute | solution.py:280
  779.1 54.2 %collective-permute-start.137 = (bf16[5,128,256]{2,1,0:T(8,128)(2,1)}, bf16[5,128,256]{2,1,0:T(8,128)(2,1)S(1)}, u32[]{:S(2)}, u32[]{:S(2)}) collective-permute-start(bf16[5,128,256]{2,1,0:T(8,128)(2,1)} %get-tuple-element.169), channel_id=1, source_target_pairs={{0,28},{1,29},{2,30},{3,31},{4,24},{5,25},{6,26},{7,27},{8,20},{9,... | collective-permute-start | bytes 983048 | tf_op jit(solution)/shard_map/ppermute | solution.py:280
  784.7 65.4 %collective-permute-start.121 = (bf16[64,2048]{1,0:T(8,128)(2,1)}, bf16[64,2048]{1,0:T(8,128)(2,1)S(1)}, u32[]{:S(2)}, u32[]{:S(2)}) collective-permute-start(bf16[64,2048]{1,0:T(8,128)(2,1)} %get-tuple-element.179), channel_id=1, source_target_pairs={{0,2},{1,3},{2,0},{3,1},{4,6},{5,7},{6,4},{7,5},{8,10},{9,11},{10,... | collective-permute-start | bytes 786440 | tf_op jit(solution)/shard_map/ppermute | solution.py:280
  810.4 40.2 %collective-permute-start.122 = (bf16[64,2048]{1,0:T(8,128)(2,1)}, bf16[64,2048]{1,0:T(8,128)(2,1)S(1)}, u32[]{:S(2)}, u32[]{:S(2)}) collective-permute-start(bf16[64,2048]{1,0:T(8,128)(2,1)} %get-tuple-element.179), channel_id=1, source_target_pairs={{0,1},{1,0},{2,3},{3,2},{4,5},{5,4},{6,7},{7,6},{8,9},{9,8},{10,11... | collective-permute-start | bytes 786440 | tf_op jit(solution)/shard_map/ppermute | solution.py:280
  (215 other events, 3941.9 us)
